TPU v7x, 512 devices: a whole 4x4x16 slice. The times are simulated.
512 devices in a mesh: sec: 4 (over x_lo, core), fsdp: 128 (over y, z, x_hi).
Axes of the slice: x: 4 (x_hi: 2, x_lo: 2; x = x_hi * 2 + x_lo), y: 4, z: 16, core: 2. Of those that a mesh axis runs over, the one named last changes fastest.
Arguments:
- tokens: bfloat16 [65536, 6144], P('fsdp', 'sec'), may hold values from -6 to 6
- grad_out: bfloat16 [65536, 6144], P('fsdp', 'sec'), may hold values from -24 to 24
- gain: float32 [6144], P('sec'), may hold values from 0.1 to 7
- qkv_weight: bfloat16 [6144, 384], P(('sec', 'fsdp')), may hold values from -0.078125 to 0.078125
- out_weight: bfloat16 [128, 6144], P(None, ('sec', 'fsdp')), may hold values from -0.5 to 0.5
Outputs:
- grad_tokens: bfloat16 [65536, 6144], P('fsdp', 'sec')
- grad_qkv: float32 [6144, 384], P(('sec', 'fsdp'))
- grad_outw: float32 [128, 6144], P(None, ('sec', 'fsdp'))
- grad_gain: float32 [6144], P(('sec', 'fsdp'))
All inputs are finite; a program needn't handle non-finite values.
Results may differ from a plain program's by a relative error of at most 0.012.
The roundings to bfloat16 on the way count: a program that leaves them out, or rounds other values in their place, can miss the bound.
Values may be sent and summed in bfloat16 or wider, within the bound.
No kernel may reach another device: no remote copies, remote signals or barrier semaphores. Data moves between devices by JAX's collectives and lax.ppermute only.
A program may use at most 64 MiB of HBM per device.

v0:
```python
import jax
import jax.numpy as jnp
from jax import lax
from jax.sharding import PartitionSpec as P

PATCHES = 256


EPS = 1e-06


def on_device(tokens, grad_out, gain, qkv_weight, out_weight):
    tok_rows, local_width = tokens.shape
    model_width = local_width * lax.axis_size("sec")
    head_size = out_weight.shape[0]
    images = tok_rows // PATCHES
    tok_float = tokens.astype(jnp.float32)
    row_sums, row_squares = lax.psum(
        (jnp.sum(tok_float, axis=1), jnp.sum(tok_float * tok_float, axis=1)), "sec"
    )
    row_mean = row_sums / model_width
    row_var = row_squares / model_width - row_mean * row_mean
    inv_std = lax.rsqrt(row_var + EPS)
    normed = (tok_float - row_mean[:, None]) * inv_std[:, None]
    hidden = (normed * gain[None, :]).astype(jnp.bfloat16)
    columns = hidden
    partial_value = jnp.dot(
        columns,
        lax.all_gather(qkv_weight, "fsdp", axis=0, tiled=True),
        preferred_element_type=jnp.float32,
    )
    proj = lax.psum(partial_value, "sec").astype(jnp.bfloat16)
    parts = proj.reshape(images, PATCHES, 3, head_size)
    query, key_in, value = (parts[:, :, 0], parts[:, :, 1], parts[:, :, 2])
    scale = 1.0 / head_size**0.5
    scores = jnp.einsum("ipd,iqd->ipq", query, key_in, preferred_element_type=jnp.float32) * scale
    probs = jax.nn.softmax(scores, axis=-1)
    probs_b = probs.astype(jnp.bfloat16)
    attended = jnp.einsum(
        "ipq,iqd->ipd", probs_b, value, preferred_element_type=jnp.float32
    ).astype(jnp.bfloat16)
    attended = attended.reshape(tok_rows, head_size)
    local_outw = lax.dot_general(
        attended, grad_out, (((0,), (0,)), ((), ())), preferred_element_type=jnp.float32
    )
    grad_outw = lax.psum_scatter(local_outw, "fsdp", scatter_dimension=1, tiled=True)
    columns = grad_out
    att_partial = lax.dot_general(
        columns,
        lax.all_gather(out_weight, "fsdp", axis=1, tiled=True),
        (((1,), (1,)), ((), ())),
        preferred_element_type=jnp.float32,
    )
    grad_att = lax.psum(att_partial, "sec").astype(jnp.bfloat16)
    grad_att3 = grad_att.reshape(images, PATCHES, head_size)
    grad_prob = jnp.einsum("ipd,iqd->ipq", grad_att3, value, preferred_element_type=jnp.float32)
    grad_score = (
        probs * (grad_prob - jnp.sum(grad_prob * probs, axis=-1, keepdims=True)) * scale
    ).astype(jnp.bfloat16)
    grad_query = jnp.einsum("ipq,iqd->ipd", grad_score, key_in, preferred_element_type=jnp.float32)
    grad_key = jnp.einsum("ipq,ipd->iqd", grad_score, query, preferred_element_type=jnp.float32)
    grad_value = jnp.einsum("ipq,ipd->iqd", probs_b, grad_att3, preferred_element_type=jnp.float32)
    grad_proj = (
        jnp.stack([grad_query, grad_key, grad_value], axis=2)
        .reshape(tok_rows, 3 * head_size)
        .astype(jnp.bfloat16)
    )
    local_qkv = lax.dot_general(
        hidden, grad_proj, (((0,), (0,)), ((), ())), preferred_element_type=jnp.float32
    )
    grad_hidden = lax.dot_general(
        grad_proj,
        lax.all_gather(qkv_weight, "fsdp", axis=0, tiled=True),
        (((1,), (1,)), ((), ())),
        preferred_element_type=jnp.float32,
    )
    local_gain = jnp.sum(grad_hidden * normed, axis=0)
    grad_normed = grad_hidden * gain[None, :]
    first_sum, second_sum = lax.psum(
        (jnp.sum(grad_normed, axis=1), jnp.sum(grad_normed * normed, axis=1)), "sec"
    )
    first = first_sum / model_width
    second = second_sum / model_width
    grad_tokens = grad_out.astype(jnp.float32) + inv_std[:, None] * (
        grad_normed - first[:, None] - normed * second[:, None]
    )
    grad_qkv, grad_gain = (
        lax.psum_scatter(local_qkv, "fsdp", scatter_dimension=0, tiled=True),
        lax.psum_scatter(local_gain, "fsdp", scatter_dimension=0, tiled=True),
    )
    return (grad_tokens.astype(jnp.bfloat16), grad_qkv, grad_outw, grad_gain)


def solution(mesh):
    placed = (
        P("fsdp", "sec"),
        P("fsdp", "sec"),
        P("sec"),
        P(("sec", "fsdp"), None),
        P(None, ("sec", "fsdp")),
    )
    return jax.shard_map(
        on_device,
        mesh=mesh,
        in_specs=placed,
        out_specs=(
            P("fsdp", "sec"),
            P(("sec", "fsdp"), None),
            P(None, ("sec", "fsdp")),
            P(("sec", "fsdp")),
        ),
        check_vma=False,
    )
```

profile of v0, /device:TPU:30, one launch (start us, length us, event | category | flops | bytes accessed | tf_op | source)
XLA Modules:
  0.0 1461.0 jit_solution(10307876886539656827)
XLA Ops:
  7.9 319.0 %all-gather.1 = bf16[128,12,128]{2,1,0:T(8,128)(2,1)S(1)} all-gather(bf16[1,12,128]{2,1,0:T(8,128)(2,1)} %bitcast.80), channel_id=1, replica_groups=mesh['sec'=4,'fsdp'=128] {'fsdp'}, dimensions={0}, use_global_device_ids=true | all-gather | bytes 396288 | tf_op jit(solution)/shard_map/all_gather | solution.py:50
  329.5 5.8 all-reduce.7
  339.6 26.2 %all-reduce.10 = (bf16[512,128]{1,0:T(8,128)(2,1)S(1)}, bf16[512,384]{1,0:T(8,128)(2,1)S(1)}) all-reduce(f32[512,128]{1,0:T(8,128)S(1)} %fusion.49, f32[512,384]{1,0:T(8,128)} %fusion.43), channel_id=1, replica_groups=mesh['sec'=4,'fsdp'=128] {'sec'}, use_global_device_ids=true, to_apply=%region_7.0 | all-reduce | flops 262144 | bytes 1572864 | tf_op jit(solution)/shard_map/psum | solution.py:54
  378.4 364.2 %fusion.45 = (f32[16,384]{1,0:T(8,128)}, f32[128,16]{0,1:T(8,128)S(1)}) fusion(f32[1536,384]{1,0:T(8,128)} %fusion.41, f32[128,1536]{0,1:T(8,128)} %fusion.50), kind=kCustom, calls=%all-reduce-scatter.2 | all-reduce-scatter fusion | flops 1048577 | bytes 3180544
  742.6 5.8 collective-permute-start.32
  749.7 6.5 collective-permute-start.33
  756.3 9.8 collective-permute-start.34
  766.1 10.5 collective-permute-start.35
  776.6 14.4 collective-permute-start.36
  791.1 14.9 %collective-permute-start.37 = (f32[128,16]{0,1:T(8,128)S(1)}, f32[128,16]{0,1:T(8,128)S(1)}, u32[]{:S(2)}, u32[]{:S(2)}) collective-permute-start(f32[128,16]{0,1:T(8,128)S(1)} %get-tuple-element.18), channel_id=1, source_target_pairs={{0,6},{1,7},{2,8},{3,9},{4,10},{5,11},{6,12},{7,13},{8,14},{9,15},... | collective-permute-start | bytes 24584
  806.0 18.0 %collective-permute-start.38 = (f32[128,16]{0,1:T(8,128)S(1)}, f32[128,16]{0,1:T(8,128)S(1)}, u32[]{:S(2)}, u32[]{:S(2)}) collective-permute-start(f32[128,16]{0,1:T(8,128)S(1)} %get-tuple-element.18), channel_id=1, source_target_pairs={{0,7},{1,8},{2,9},{3,10},{4,11},{5,12},{6,13},{7,14},{8,15},{9,16}... | collective-permute-start | bytes 24584
  824.1 6.1 collective-permute-start.39
  896.8 7.6 collective-permute-done.57
  911.8 9.3 collective-permute-done.60
  972.0 6.2 all-reduce.5
  987.8 5.7 collective-permute-done.23
  1011.0 322.6 %all-reduce.2 = f32[1536]{0:T(1024)S(1)} all-reduce(f32[1536]{0:T(1024)} %get-tuple-element.4), channel_id=4, replica_groups=mesh['sec'=4,'fsdp'=128] {'fsdp'}, use_global_device_ids=true, to_apply=%region_16.0.clone | all-reduce | flops 1536 | bytes 12288
  1334.3 16.0 %concatenate.1 = f32[128,524]{0,1:T(8,128)S(1)} concatenate(f32[128,12]{0,1:T(8,128)S(1)} %copy-done.10, f32[128,16]{0,1:T(8,128)} %copy-done.51, f32[128,16]{0,1:T(8,128)} %copy-done.50, f32[128,16]{0,1:T(8,128)} %copy-done.49, f32[128,16]{0,1:T(8,128)} %copy-done.48, f32[128,16]{0,1:T(8,128)} %copy-done.47, f32[128,16]{0,1:T(8,128)} %copy-done.46, f32[128,16]{0,1:T(8,128)} %copy-done.45, ...), dimensions={1} | concatenate | bytes 536576
  1350.3 15.1 %collective-permute-start.5 = (f32[16,384]{1,0:T(8,128)S(1)}, f32[16,384]{1,0:T(8,128)S(1)}, u32[]{:S(2)}, u32[]{:S(2)}) collective-permute-start(f32[16,384]{1,0:T(8,128)S(1)} %copy-done.5), channel_id=1, source_target_pairs={{0,6},{1,7},{2,8},{3,9},{4,10},{5,11},{6,12},{7,13},{8,14},{9,15},... | collective-permute-start | bytes 73736
  1365.4 18.8 %collective-permute-start.6 = (f32[16,384]{1,0:T(8,128)S(1)}, f32[16,384]{1,0:T(8,128)S(1)}, u32[]{:S(2)}, u32[]{:S(2)}) collective-permute-start(f32[16,384]{1,0:T(8,128)S(1)} %copy-done.5), channel_id=1, source_target_pairs={{0,7},{1,8},{2,9},{3,10},{4,11},{5,12},{6,13},{7,14},{8,15},{9,16}... | collective-permute-start | bytes 73736
  1384.3 19.1 %collective-permute-start.7 = (f32[16,384]{1,0:T(8,128)S(1)}, f32[16,384]{1,0:T(8,128)S(1)}, u32[]{:S(2)}, u32[]{:S(2)}) collective-permute-start(f32[16,384]{1,0:T(8,128)S(1)} %copy-done.5), channel_id=1, source_target_pairs={{0,8},{1,9},{2,10},{3,11},{4,12},{5,13},{6,14},{7,15},{8,16},{9,17... | collective-permute-start | bytes 73736
  1403.4 22.5 %collective-permute-start.8 = (f32[16,384]{1,0:T(8,128)S(1)}, f32[16,384]{1,0:T(8,128)S(1)}, u32[]{:S(2)}, u32[]{:S(2)}) collective-permute-start(f32[16,384]{1,0:T(8,128)S(1)} %copy-done.5), channel_id=1, source_target_pairs={{0,9},{1,10},{2,11},{3,12},{4,13},{5,14},{6,15},{7,16},{8,17},{9,1... | collective-permute-start | bytes 73736
  1428.4 10.1 collective-permute-done.9
  1438.5 15.0 %concatenate = f32[524,384]{1,0:T(8,128)S(1)} concatenate(f32[12,384]{1,0:T(8,128)S(1)} %copy-done.8, f32[16,384]{1,0:T(8,128)S(1)} %collective-permute-done.30, f32[16,384]{1,0:T(8,128)S(1)} %collective-permute-done.29, f32[16,384]{1,0:T(8,128)S(1)} %collective-permute-done.28, f32[16,384]{1,0:T(8,128)S(1)} %collective-permute-done.27, f32[16,384]{1,0:T(8,128)S(1)} %collective-permute-done.26, ...), dimensions={0} | concatenate | bytes 1609728
  (253 shorter events, 174.9 us)
Async XLA Ops:
  7.2 328.2 %all-gather.4.cloned.1.call-start = ((), (), s32[]{:S(2)}) async-start(), calls=%async_computation | async-start | bytes 1585152 | tf_op jit(solution)/shard_map/all_gather | solution.py:29
  742.6 48.5 %collective-permute-start.32 = (f32[128,16]{0,1:T(8,128)S(1)}, f32[128,16]{0,1:T(8,128)S(1)}, u32[]{:S(2)}, u32[]{:S(2)}) collective-permute-start(f32[128,16]{0,1:T(8,128)S(1)} %get-tuple-element.18), channel_id=1, source_target_pairs={{0,1},{1,2},{2,3},{3,4},{4,5},{5,6},{6,7},{7,8},{8,9},{9,10},{10,1... | collective-permute-start | bytes 24584
  748.4 28.2 %collective-permute-start.63 = (f32[128,12]{0,1:T(8,128)S(1)}, f32[128,12]{0,1:T(8,128)S(1)}, u32[]{:S(2)}, u32[]{:S(2)}) collective-permute-start(f32[128,12]{0,1:T(8,128)S(1)} %slice.16), channel_id=1, source_target_pairs={{0,32},{1,33},{2,34},{3,35},{4,36},{5,37},{6,38},{7,39},{8,40},{9,... | collective-permute-start | bytes 18440
  749.7 56.3 %collective-permute-start.33 = (f32[128,16]{0,1:T(8,128)S(1)}, f32[128,16]{0,1:T(8,128)S(1)}, u32[]{:S(2)}, u32[]{:S(2)}) collective-permute-start(f32[128,16]{0,1:T(8,128)S(1)} %get-tuple-element.18), channel_id=1, source_target_pairs={{0,2},{1,3},{2,4},{3,5},{4,6},{5,7},{6,8},{7,9},{8,10},{9,11},{10,... | collective-permute-start | bytes 24584
  756.3 67.8 %collective-permute-start.34 = (f32[128,16]{0,1:T(8,128)S(1)}, f32[128,16]{0,1:T(8,128)S(1)}, u32[]{:S(2)}, u32[]{:S(2)}) collective-permute-start(f32[128,16]{0,1:T(8,128)S(1)} %get-tuple-element.18), channel_id=1, source_target_pairs={{0,3},{1,4},{2,5},{3,6},{4,7},{5,8},{6,9},{7,10},{8,11},{9,12},{10... | collective-permute-start | bytes 24584
  766.1 64.1 %collective-permute-start.35 = (f32[128,16]{0,1:T(8,128)S(1)}, f32[128,16]{0,1:T(8,128)S(1)}, u32[]{:S(2)}, u32[]{:S(2)}) collective-permute-start(f32[128,16]{0,1:T(8,128)S(1)} %get-tuple-element.18), channel_id=1, source_target_pairs={{0,4},{1,5},{2,6},{3,7},{4,8},{5,9},{6,10},{7,11},{8,12},{9,13},{1... | collective-permute-start | bytes 24584
  776.6 55.5 %collective-permute-start.36 = (f32[128,16]{0,1:T(8,128)S(1)}, f32[128,16]{0,1:T(8,128)S(1)}, u32[]{:S(2)}, u32[]{:S(2)}) collective-permute-start(f32[128,16]{0,1:T(8,128)S(1)} %get-tuple-element.18), channel_id=1, source_target_pairs={{0,5},{1,6},{2,7},{3,8},{4,9},{5,10},{6,11},{7,12},{8,13},{9,14},{... | collective-permute-start | bytes 24584
  791.1 43.0 %collective-permute-start.37 = (f32[128,16]{0,1:T(8,128)S(1)}, f32[128,16]{0,1:T(8,128)S(1)}, u32[]{:S(2)}, u32[]{:S(2)}) collective-permute-start(f32[128,16]{0,1:T(8,128)S(1)} %get-tuple-element.18), channel_id=1, source_target_pairs={{0,6},{1,7},{2,8},{3,9},{4,10},{5,11},{6,12},{7,13},{8,14},{9,15},... | collective-permute-start | bytes 24584
  806.0 30.0 %collective-permute-start.38 = (f32[128,16]{0,1:T(8,128)S(1)}, f32[128,16]{0,1:T(8,128)S(1)}, u32[]{:S(2)}, u32[]{:S(2)}) collective-permute-start(f32[128,16]{0,1:T(8,128)S(1)} %get-tuple-element.18), channel_id=1, source_target_pairs={{0,7},{1,8},{2,9},{3,10},{4,11},{5,12},{6,13},{7,14},{8,15},{9,16}... | collective-permute-start | bytes 24584
  882.1 50.3 %collective-permute-start = (f32[16,384]{1,0:T(8,128)}, f32[16,384]{1,0:T(8,128)}, u32[]{:S(2)}, u32[]{:S(2)}) collective-permute-start(f32[16,384]{1,0:T(8,128)} %get-tuple-element.17), channel_id=1, source_target_pairs={{0,1},{1,2},{2,3},{3,4},{4,5},{5,6},{6,7},{7,8},{8,9},{9,10},{10,1... | collective-permute-start | bytes 73736
  885.2 43.0 %collective-permute-start.31 = (f32[12,384]{1,0:T(8,128)S(1)}, f32[12,384]{1,0:T(8,128)S(1)}, u32[]{:S(2)}, u32[]{:S(2)}) collective-permute-start(f32[12,384]{1,0:T(8,128)S(1)} %slice.15), channel_id=1, source_target_pairs={{0,32},{1,33},{2,34},{3,35},{4,36},{5,37},{6,38},{7,39},{8,40},{9,... | collective-permute-start | bytes 55304
  952.3 25.8 %collective-permute-start.19 = (f32[16,384]{1,0:T(8,128)}, f32[16,384]{1,0:T(8,128)}, u32[]{:S(2)}, u32[]{:S(2)}) collective-permute-start(f32[16,384]{1,0:T(8,128)} %get-tuple-element.17), channel_id=1, source_target_pairs={{0,20},{1,21},{2,22},{3,23},{4,24},{5,25},{6,26},{7,27},{8,28},{9,... | collective-permute-start | bytes 73736
  954.5 25.6 %collective-permute-start.2 = (f32[16,384]{1,0:T(8,128)}, f32[16,384]{1,0:T(8,128)}, u32[]{:S(2)}, u32[]{:S(2)}) collective-permute-start(f32[16,384]{1,0:T(8,128)} %get-tuple-element.17), channel_id=1, source_target_pairs={{0,3},{1,4},{2,5},{3,6},{4,7},{5,8},{6,9},{7,10},{8,11},{9,12},{10... | collective-permute-start | bytes 73736
  958.6 23.4 %collective-permute-start.20 = (f32[16,384]{1,0:T(8,128)}, f32[16,384]{1,0:T(8,128)}, u32[]{:S(2)}, u32[]{:S(2)}) collective-permute-start(f32[16,384]{1,0:T(8,128)} %get-tuple-element.17), channel_id=1, source_target_pairs={{0,21},{1,22},{2,23},{3,24},{4,25},{5,26},{6,27},{7,28},{8,29},{9,... | collective-permute-start | bytes 73736
  960.6 23.4 %collective-permute-start.21 = (f32[16,384]{1,0:T(8,128)}, f32[16,384]{1,0:T(8,128)}, u32[]{:S(2)}, u32[]{:S(2)}) collective-permute-start(f32[16,384]{1,0:T(8,128)} %get-tuple-element.17), channel_id=1, source_target_pairs={{0,22},{1,23},{2,24},{3,25},{4,26},{5,27},{6,28},{7,29},{8,30},{9,... | collective-permute-start | bytes 73736
  993.5 356.8 %collective-permute-start.28 = (f32[16,384]{1,0:T(8,128)}, f32[16,384]{1,0:T(8,128)S(1)}, u32[]{:S(2)}, u32[]{:S(2)}) collective-permute-start(f32[16,384]{1,0:T(8,128)} %get-tuple-element.17), channel_id=1, source_target_pairs={{0,29},{1,30},{2,31},{3,32},{4,33},{5,34},{6,35},{7,36},{8,37},{9,... | collective-permute-start | bytes 73736
  998.3 367.1 %collective-permute-start.29 = (f32[16,384]{1,0:T(8,128)}, f32[16,384]{1,0:T(8,128)S(1)}, u32[]{:S(2)}, u32[]{:S(2)}) collective-permute-start(f32[16,384]{1,0:T(8,128)} %get-tuple-element.17), channel_id=1, source_target_pairs={{0,30},{1,31},{2,32},{3,33},{4,34},{5,35},{6,36},{7,37},{8,38},{9,... | collective-permute-start | bytes 73736
  1000.2 384.1 %collective-permute-start.3 = (f32[16,384]{1,0:T(8,128)}, f32[16,384]{1,0:T(8,128)S(1)}, u32[]{:S(2)}, u32[]{:S(2)}) collective-permute-start(f32[16,384]{1,0:T(8,128)} %get-tuple-element.17), channel_id=1, source_target_pairs={{0,4},{1,5},{2,6},{3,7},{4,8},{5,9},{6,10},{7,11},{8,12},{9,13},{1... | collective-permute-start | bytes 73736
  1002.1 401.3 %collective-permute-start.30 = (f32[16,384]{1,0:T(8,128)}, f32[16,384]{1,0:T(8,128)S(1)}, u32[]{:S(2)}, u32[]{:S(2)}) collective-permute-start(f32[16,384]{1,0:T(8,128)} %get-tuple-element.17), channel_id=1, source_target_pairs={{0,31},{1,32},{2,33},{3,34},{4,35},{5,36},{6,37},{7,38},{8,39},{9,... | collective-permute-start | bytes 73736
  1003.4 422.4 %collective-permute-start.4 = (f32[16,384]{1,0:T(8,128)}, f32[16,384]{1,0:T(8,128)S(1)}, u32[]{:S(2)}, u32[]{:S(2)}) collective-permute-start(f32[16,384]{1,0:T(8,128)} %get-tuple-element.17), channel_id=1, source_target_pairs={{0,5},{1,6},{2,7},{3,8},{4,9},{5,10},{6,11},{7,12},{8,13},{9,14},{... | collective-permute-start | bytes 73736
  1350.3 78.1 %collective-permute-start.5 = (f32[16,384]{1,0:T(8,128)S(1)}, f32[16,384]{1,0:T(8,128)S(1)}, u32[]{:S(2)}, u32[]{:S(2)}) collective-permute-start(f32[16,384]{1,0:T(8,128)S(1)} %copy-done.5), channel_id=1, source_target_pairs={{0,6},{1,7},{2,8},{3,9},{4,10},{5,11},{6,12},{7,13},{8,14},{9,15},... | collective-permute-start | bytes 73736
  1365.4 63.0 %collective-permute-start.6 = (f32[16,384]{1,0:T(8,128)S(1)}, f32[16,384]{1,0:T(8,128)S(1)}, u32[]{:S(2)}, u32[]{:S(2)}) collective-permute-start(f32[16,384]{1,0:T(8,128)S(1)} %copy-done.5), channel_id=1, source_target_pairs={{0,7},{1,8},{2,9},{3,10},{4,11},{5,12},{6,13},{7,14},{8,15},{9,16}... | collective-permute-start | bytes 73736
  1384.3 44.2 %collective-permute-start.7 = (f32[16,384]{1,0:T(8,128)S(1)}, f32[16,384]{1,0:T(8,128)S(1)}, u32[]{:S(2)}, u32[]{:S(2)}) collective-permute-start(f32[16,384]{1,0:T(8,128)S(1)} %copy-done.5), channel_id=1, source_target_pairs={{0,8},{1,9},{2,10},{3,11},{4,12},{5,13},{6,14},{7,15},{8,16},{9,17... | collective-permute-start | bytes 73736
  1403.4 25.0 %collective-permute-start.8 = (f32[16,384]{1,0:T(8,128)S(1)}, f32[16,384]{1,0:T(8,128)S(1)}, u32[]{:S(2)}, u32[]{:S(2)}) collective-permute-start(f32[16,384]{1,0:T(8,128)S(1)} %copy-done.5), channel_id=1, source_target_pairs={{0,9},{1,10},{2,11},{3,12},{4,13},{5,14},{6,15},{7,16},{8,17},{9,1... | collective-permute-start | bytes 73736
  (96 other events, 7442.3 us)
Sparse Core Ops, SparseCore 0:
  12.3 201.5 all-gather.3
where the time goes:
time: 1470 us; the launch traced here: 1460 us
  blocking collectives  1040 us (71%)
  starting transfers between devices  268 us (18%)
  waiting for transfers between devices  67.4 us (5%)
  local copies, waits for them, and re-layouts  40.5 us (3%)
  matrix products  19.5 us (1%)
  between operations  16.9 us (1%)
    unnamed x2, blocking collectives  687 us
    all_gather x1, blocking collectives, on_device(): lax.all_gather(out_weight, 'fsdp', axis=1, tiled=True)  319 us
    unnamed x64, starting transfers between devices  268 us
    unnamed x65, waiting for transfers between devices  67.4 us
    unnamed x121, local copies, waits for them, and re-layouts  39.3 us
  transfers between devices with their start and end apart: 65, of which 24 were waited for; matrix products, arithmetic and copies ran while one was open for 2% of the time, Pallas kernels for 0%

commit v1 on v0

v1 whole, which is shorter than its diff:
```python
import jax
import jax.numpy as jnp
from jax import lax
from jax.sharding import Mesh
from jax.sharding import PartitionSpec as P

PATCHES = 256


EPS = 1e-06

SEC = ("xlo", "core")
FSDP = ("y", "z", "xhi")
NEAR = ("y", "xhi")


def gather_weights(block):
    rows, width = block.shape
    ny, nz, nx = (lax.axis_size(a) for a in FSDP)
    padded = jnp.pad(block, ((0, -rows % 16), (0, 0)))
    along_z = lax.all_to_all(
        jnp.broadcast_to(padded[None], (nz,) + padded.shape), "z", 0, 0
    )[:, :rows].reshape(nz * rows, width)
    near = lax.all_to_all(
        jnp.broadcast_to(along_z[None], (ny * nx,) + along_z.shape), NEAR, 0, 0
    )
    near = near.reshape(ny, nx, nz, rows, width).transpose(0, 2, 1, 3, 4)
    return near.reshape(ny * nz * nx * rows, width)


def scatter_sums(partial):
    ny, nz, nx = (lax.axis_size(a) for a in FSDP)
    total, width = partial.shape
    rows = total // (ny * nz * nx)
    near = partial.reshape(ny, nz, nx, rows, width).transpose(0, 2, 1, 3, 4)
    near = near.reshape(ny * nx, nz * rows, width).astype(jnp.bfloat16)
    near = lax.all_to_all(near, NEAR, 0, 0)
    summed = jnp.sum(near.astype(jnp.float32), axis=0).reshape(nz, rows, width)
    summed = jnp.pad(summed, ((0, 0), (0, -rows % 16), (0, 0))).astype(jnp.bfloat16)
    along_z = lax.all_to_all(summed, "z", 0, 0)[:, :rows]
    return jnp.sum(along_z.astype(jnp.float32), axis=0)


def sum_over_sec(partial):
    rows, width = partial.shape
    half = lax.all_to_all(partial.reshape(2, rows // 2, width), "core", 0, 0)
    half = half[0] + half[1]
    quarter = lax.all_to_all(half.reshape(2, rows // 4, width), "xlo", 0, 0)
    quarter = (quarter[0] + quarter[1]).astype(jnp.bfloat16)
    half = lax.all_gather(quarter, "xlo", axis=0, tiled=True)
    return lax.all_gather(half, "core", axis=0, tiled=True)


def on_device(tokens, grad_out, gain, qkv_weight, out_weight):
    tok_rows, local_width = tokens.shape
    model_width = local_width * lax.axis_size(SEC)
    head_size = out_weight.shape[0]
    images = tok_rows // PATCHES
    own_rows = qkv_weight.shape[0]

    weights = gather_weights(jnp.concatenate([qkv_weight, out_weight.T], axis=1))
    qkv_all = weights[:, : 3 * head_size]
    outw_all = weights[:, 3 * head_size :]

    tok_float = tokens.astype(jnp.float32)
    gain_high = gain.astype(jnp.bfloat16)
    gain_low = (gain - gain_high.astype(jnp.float32)).astype(jnp.bfloat16)
    weight_sums = jnp.dot(
        jnp.stack([gain_high, gain_low]), qkv_all, preferred_element_type=jnp.float32
    ).sum(axis=0)
    row_sums, row_squares, weight_sums = lax.psum(
        (jnp.sum(tok_float, axis=1), jnp.sum(tok_float * tok_float, axis=1), weight_sums), SEC
    )
    row_mean = row_sums / model_width
    row_var = row_squares / model_width - row_mean * row_mean
    inv_std = lax.rsqrt(row_var + EPS)
    normed = (tok_float - row_mean[:, None]) * inv_std[:, None]
    hidden = (normed * gain[None, :]).astype(jnp.bfloat16)
    proj_partial = jnp.dot(hidden, qkv_all, preferred_element_type=jnp.float32)
    att_partial = jnp.dot(grad_out, outw_all, preferred_element_type=jnp.float32)
    both = sum_over_sec(jnp.concatenate([proj_partial, att_partial], axis=1))
    proj = both[:, : 3 * head_size]
    grad_att3 = both[:, 3 * head_size :].reshape(images, PATCHES, head_size)
    parts = proj.reshape(images, PATCHES, 3, head_size)
    query, key_in, value = (parts[:, :, 0], parts[:, :, 1], parts[:, :, 2])
    scale = 1.0 / head_size**0.5
    scores = jnp.einsum("ipd,iqd->ipq", query, key_in, preferred_element_type=jnp.float32) * scale
    probs = jax.nn.softmax(scores, axis=-1)
    probs_b = probs.astype(jnp.bfloat16)
    attended = jnp.einsum(
        "ipq,iqd->ipd", probs_b, value, preferred_element_type=jnp.float32
    ).astype(jnp.bfloat16)
    attended = attended.reshape(tok_rows, head_size)
    grad_prob = jnp.einsum("ipd,iqd->ipq", grad_att3, value, preferred_element_type=jnp.float32)
    grad_score = (
        probs * (grad_prob - jnp.sum(grad_prob * probs, axis=-1, keepdims=True)) * scale
    ).astype(jnp.bfloat16)
    grad_query = jnp.einsum("ipq,iqd->ipd", grad_score, key_in, preferred_element_type=jnp.float32)
    grad_key = jnp.einsum("ipq,ipd->iqd", grad_score, query, preferred_element_type=jnp.float32)
    grad_value = jnp.einsum("ipq,ipd->iqd", probs_b, grad_att3, preferred_element_type=jnp.float32)
    grad_proj = (
        jnp.stack([grad_query, grad_key, grad_value], axis=2)
        .reshape(tok_rows, 3 * head_size)
        .astype(jnp.bfloat16)
    )
    over_rows = (((0,), (0,)), ((), ()))
    local_qkv = lax.dot_general(hidden, grad_proj, over_rows, preferred_element_type=jnp.float32)
    local_outw = lax.dot_general(grad_out, attended, over_rows, preferred_element_type=jnp.float32)
    summed = scatter_sums(jnp.concatenate([local_qkv, local_outw], axis=1))
    grad_qkv = summed[:, : 3 * head_size]
    grad_outw = summed[:, 3 * head_size :].T
    own = lax.axis_index(FSDP) * own_rows
    grad_gain = jnp.sum(qkv_weight.astype(jnp.float32) * grad_qkv, axis=1) / lax.dynamic_slice(
        gain, (own,), (own_rows,)
    )

    grad_hidden = lax.dot_general(
        grad_proj, qkv_all, (((1,), (1,)), ((), ())), preferred_element_type=jnp.float32
    )
    proj_grad = grad_proj.astype(jnp.float32)
    first = jnp.sum(proj_grad * weight_sums[None, :], axis=1) / model_width
    second = jnp.sum(proj_grad * proj.astype(jnp.float32), axis=1) / model_width
    grad_normed = grad_hidden * gain[None, :]
    grad_tokens = grad_out.astype(jnp.float32) + inv_std[:, None] * (
        grad_normed - first[:, None] - normed * second[:, None]
    )
    return (grad_tokens.astype(jnp.bfloat16), grad_qkv, grad_outw, grad_gain)


def solution(mesh):
    fine = Mesh(mesh.devices.reshape(2, 2, 4, 16, 2), SEC + FSDP)
    placed = (
        P(FSDP, SEC),
        P(FSDP, SEC),
        P(SEC),
        P(SEC + FSDP, None),
        P(None, SEC + FSDP),
    )
    return jax.shard_map(
        on_device,
        mesh=fine,
        in_specs=placed,
        out_specs=(
            P(FSDP, SEC),
            P(SEC + FSDP, None),
            P(None, SEC + FSDP),
            P(SEC + FSDP),
        ),
        check_vma=False,
    )
```

time: 1470 us -> 182 us (0.12)
  the two profiles are of different devices: /device:TPU:30 before, /device:TPU:64 now
where the time goes in v1:
time: 182 us; the launch traced here: 181 us
  blocking collectives  62.1 us (34%)
  waiting for transfers between devices  53.9 us (30%)
  local copies, waits for them, and re-layouts  25.2 us (14%)
  starting transfers between devices  20 us (11%)
  matrix products  11.8 us (6%)
  other arithmetic  6.95 us (4%)
    all_to_all x1, blocking collectives, gather_weights(): lax.all_to_all(jnp.broadcast_to(padded[None], (nz,) + padded.shape), 'z',...  32.7 us
    all_to_all x1, waiting for transfers between devices, scatter_sums(): near = lax.all_to_all(near, NEAR, 0, 0)  23.4 us
    all_to_all x1, waiting for transfers between devices, gather_weights(): lax.all_to_all(jnp.broadcast_to(along_z[None], (ny * nx,) + along_z.shape...  18.8 us
    all_to_all x1, waiting for transfers between devices, scatter_sums(): along_z = lax.all_to_all(summed, 'z', 0, 0)[:, :rows]  11.7 us
    all_to_all x1, blocking collectives, sum_over_sec(): quarter = lax.all_to_all(half.reshape(2, rows // 4, width), 'xlo', 0, 0)  11 us
    all_to_all x1, starting transfers between devices, scatter_sums(): along_z = lax.all_to_all(summed, 'z', 0, 0)[:, :rows]  9.41 us
    convert_element_type x3, local copies, waits for them, and re-layouts, scatter_sums(): near = near.reshape(ny * nx, nz * rows, width).astype(jnp.bfloat16)  7.57 us
    all_to_all x1, starting transfers between devices, gather_weights(): lax.all_to_all(jnp.broadcast_to(along_z[None], (ny * nx,) + along_z.shape...  7.06 us
  transfers between devices with their start and end apart: 3, of which 3 were waited for; matrix products, arithmetic and copies ran while one was open for 4% of the time, Pallas kernels for 0%

profile of v1, /device:TPU:64, one launch (start us, length us, event | category | flops | bytes accessed | tf_op | source)
XLA Modules:
  0.0 181.0 jit_solution(711815306517727849)
XLA Ops:
  1.4 32.7 %all_to_all.30 = bf16[16,16,512]{2,1,0:T(8,128)(2,1)S(1)} all-to-all(bf16[16,16,512]{2,1,0:T(8,128)(2,1)S(1)} %broadcast_in_dim.6), channel_id=1, replica_groups=mesh['xlo'=2,'core'=2,'y'=4,'z'=16,'xhi'=2] {'z'}, dimensions={0} | all-to-all | bytes 524288 | tf_op jit(solution)/shard_map/all_to_all | solution.py:21
  35.4 7.1 %all-to-all-start.1 = ((bf16[8,192,512]{2,1,0:T(8,128)(2,1)}), bf16[8,192,512]{2,1,0:T(8,128)(2,1)S(1)}, u32[]{:S(2)}, u32[]{:S(2)}) async-start(bf16[8,192,512]{2,1,0:T(8,128)(2,1)} %broadcast_in_dim.8), calls=%async_computation.1 | async-start | bytes 3145728 | tf_op jit(solution)/shard_map/all_to_all | solution.py:24
  43.1 18.8 %all-to-all-done.1 = bf16[8,192,512]{2,1,0:T(8,128)(2,1)S(1)} async-done(((bf16[8,192,512]{2,1,0:T(8,128)(2,1)}), bf16[8,192,512]{2,1,0:T(8,128)(2,1)S(1)}, u32[]{:S(2)}, u32[]{:S(2)}) %all-to-all-start.1) | async-done | bytes 1572896 | tf_op jit(solution)/shard_map/all_to_all | solution.py:24
  62.8 2.0 %reshape.68 = bf16[4,2,16,12,512]{4,1,0,3,2:T(2,128)(2,1)} reshape(bf16[8,192,512]{2,0,1:T(8,128)(2,1)S(1)} %copy.49) | data formatting | bytes 3145728 | tf_op jit(solution)/shard_map/reshape | solution.py:27
  64.8 2.1 %copy.50 = bf16[4,16,2,12,512]{4,3,2,1,0:T(8,128)(2,1)S(1)} copy(bf16[4,16,2,12,512]{4,2,0,3,1:T(2,128)(2,1)} %bitcast.80) | data formatting | bytes 3145728 | tf_op jit(solution)/shard_map/transpose | solution.py:27
  66.9 1.3 reshape.69
  68.2 2.3 %convolution_bitcast_fusion.3 = f32[512,128]{0,1:T(8,128)S(1)} fusion(bf16[512,1536]{1,0:T(8,128)(2,1)} %param.6, bf16[1536,512]{1,0:T(8,128)(2,1)} %reshape.69), kind=kOutput, calls=%fused_computation.30 | convolution fusion | flops 201326592 | bytes 2228224 | tf_op jit(solution)/shard_map/dot_general | solution.py:80
  70.9 6.1 %all-reduce.2 = (f32[512]{0:T(512)S(1)}, f32[512]{0:T(512)S(1)}, f32[3,128]{1,0:T(4,128)S(1)}) all-reduce(f32[512]{0:T(512)S(1)} %get-tuple-element.5, f32[512]{0:T(512)S(1)} %get-tuple-element.4, f32[3,128]{1,0:T(4,128)S(1)} %bitcast.94), channel_id=1, replica_groups=mesh['xlo'=2,'core'=2,'y'=4,'z'=16,'xhi'=2] {'xlo','core'}, use_global_device_ids=true, to_apply=%region_3.4 | all-reduce | flops 1408 | bytes 11264 | tf_op jit(solution)/shard_map/psum | solution.py:71
  78.5 4.6 %all_to_all.31 = f32[2,256,512]{2,1,0:T(8,128)S(1)} all-to-all(f32[2,256,512]{2,1,0:T(8,128)S(1)} %bitcast.81), channel_id=1, replica_groups=mesh['xlo'=2,'core'=2,'y'=4,'z'=16,'xhi'=2] {'core'}, dimensions={0} | all-to-all | bytes 2097152 | tf_op jit(solution)/shard_map/all_to_all | solution.py:46
  83.1 11.0 %all_to_all.32 = f32[2,128,512]{2,1,0:T(8,128)S(1)} all-to-all(f32[2,128,512]{2,1,0:T(8,128)S(1)} %bitcast.85), channel_id=1, replica_groups=mesh['xlo'=2,'core'=2,'y'=4,'z'=16,'xhi'=2] {'xlo'}, dimensions={0} | all-to-all | bytes 1048576 | tf_op jit(solution)/shard_map/all_to_all | solution.py:48
  94.1 5.6 %all-gather = bf16[1,256,512]{2,1,0:T(8,128)(2,1)S(1)} all-gather(bf16[1,128,512]{2,1,0:T(8,128)(2,1)S(1)} %fusion.28), channel_id=2, replica_groups=mesh['xlo'=2,'core'=2,'y'=4,'z'=16,'xhi'=2] {'xlo'}, dimensions={1}, use_global_device_ids=true | all-gather | bytes 393216 | tf_op jit(solution)/shard_map/all_gather | solution.py:50
  99.8 2.2 %all-gather.1 = bf16[1,512,512]{2,1,0:T(8,128)(2,1)S(1)} all-gather(bf16[1,256,512]{2,1,0:T(8,128)(2,1)S(1)} %all-gather), channel_id=3, replica_groups=mesh['xlo'=2,'core'=2,'y'=4,'z'=16,'xhi'=2] {'core'}, dimensions={1}, use_global_device_ids=true | all-gather | bytes 786432 | tf_op jit(solution)/shard_map/all_gather | solution.py:51
  109.1 1.6 copy.65
  110.7 2.4 %convert_element_type.93 = bf16[4,16,2,12,512]{4,3,2,1,0:T(8,128)(2,1)S(1)} reshape(bf16[1536,512]{1,0:T(8,128)(2,1)} %copy.65) | data formatting | bytes 3145728 | tf_op jit(solution)/shard_map/convert_element_type | solution.py:36
  113.0 1.6 copy.76
  114.6 3.6 %reshape.77 = bf16[8,192,512]{2,1,0:T(8,128)(2,1)} reshape(bf16[4,2,16,12,512]{4,3,2,1,0:T(8,128)(2,1)} %copy.76) | data formatting | bytes 3145728 | tf_op jit(solution)/shard_map/convert_element_type | solution.py:36
  118.2 3.6 %all-to-all-start.4 = ((bf16[8,192,512]{2,1,0:T(8,128)(2,1)}), bf16[8,192,512]{2,1,0:T(8,128)(2,1)S(1)}, u32[]{:S(2)}, u32[]{:S(2)}) async-start(bf16[8,192,512]{2,1,0:T(8,128)(2,1)} %reshape.77), calls=%async_computation.4 | async-start | bytes 3145728 | tf_op jit(solution)/shard_map/all_to_all | solution.py:37
  121.8 23.4 %all-to-all-done.4 = bf16[8,192,512]{2,1,0:T(8,128)(2,1)S(1)} async-done(((bf16[8,192,512]{2,1,0:T(8,128)(2,1)}), bf16[8,192,512]{2,1,0:T(8,128)(2,1)S(1)}, u32[]{:S(2)}, u32[]{:S(2)}) %all-to-all-start.4) | async-done | bytes 1572896 | tf_op jit(solution)/shard_map/all_to_all | solution.py:37
  146.1 1.8 reshape.74
  147.9 1.7 pad.10
  149.6 9.4 %all-to-all-start.5 = ((bf16[16,16,512]{2,1,0:T(8,128)(2,1)}), bf16[16,16,512]{2,1,0:T(8,128)(2,1)}, u32[]{:S(2)}, u32[]{:S(2)}) async-start(bf16[16,16,512]{2,1,0:T(8,128)(2,1)} %pad.10), calls=%async_computation.5 | async-start | bytes 524288 | tf_op jit(solution)/shard_map/all_to_all | solution.py:40
  159.9 1.3 multiply_reduce_fusion.1
  161.3 4.4 %fusion.11 = bf16[512,1536]{1,0:T(8,128)(2,1)} fusion(bf16[512,1536]{1,0:T(8,128)(2,1)} %param.5, bf16[512,384]{0,1:T(8,128)(2,1)S(1)} %bitcast.88, bf16[512,1536]{1,0:T(8,128)(2,1)S(1)} %copy-done.3, f32[512]{0:T(512)S(1)} %broadcast_multiply_fusion, f32[512]{0:T(512)S(1)} %bitcast.96, f32[1536]{0:T(1024)} %param.7, f32[512]{0:T(512)} %copy-done.10, ...), kind=kOutput, calls=%fused_computation.15 | convolution fusion | flops 612630528 | bytes 6305792 | tf_op jit(solution)/shard_map/dot_general | solution.py:117
  165.7 11.7 %all-to-all-done.5 = bf16[16,16,512]{2,1,0:T(8,128)(2,1)} async-done(((bf16[16,16,512]{2,1,0:T(8,128)(2,1)}), bf16[16,16,512]{2,1,0:T(8,128)(2,1)}, u32[]{:S(2)}, u32[]{:S(2)}) %all-to-all-start.5) | async-done | bytes 262176 | tf_op jit(solution)/shard_map/all_to_all | solution.py:40
  (65 shorter events, 17.8 us)
Async XLA Ops:
  35.4 7.1 %copy-start.9 = (f32[1536]{0:T(1024)S(1)}, f32[1536]{0:T(1024)}, u32[]{:S(2)}) copy-start(f32[1536]{0:T(1024)} %param.7) | copy-start | bytes 18436
  35.4 7.1 %copy-start.5 = (bf16[512,1536]{1,0:T(8,128)(2,1)S(1)}, bf16[512,1536]{1,0:T(8,128)(2,1)}, u32[]{:S(2)}) copy-start(bf16[512,1536]{1,0:T(8,128)(2,1)} %param.5) | copy-start | bytes 4718596
  35.4 26.5 %all-to-all-start.1 = ((bf16[8,192,512]{2,1,0:T(8,128)(2,1)}), bf16[8,192,512]{2,1,0:T(8,128)(2,1)S(1)}, u32[]{:S(2)}, u32[]{:S(2)}) async-start(bf16[8,192,512]{2,1,0:T(8,128)(2,1)} %broadcast_in_dim.8), calls=%async_computation.1 | async-start | bytes 3145728 | tf_op jit(solution)/shard_map/all_to_all | solution.py:24
  68.2 2.3 %copy-start = (bf16[1536,512]{1,0:T(8,128)(2,1)S(1)}, bf16[1536,512]{1,0:T(8,128)(2,1)}, u32[]{:S(2)}) copy-start(bf16[1536,512]{1,0:T(8,128)(2,1)} %reshape.69) | copy-start | bytes 4718596
  68.2 8.8 %copy-start.6 = (bf16[512,1536]{1,0:T(8,128)(2,1)S(1)}, bf16[512,1536]{1,0:T(8,128)(2,1)}, u32[]{:S(2)}) copy-start(bf16[512,1536]{1,0:T(8,128)(2,1)} %param.5) | copy-start | bytes 4718596
  77.0 1.1 copy-start.10
  101.9 0.8 copy-start.4
  105.9 1.4 copy-start.2
  106.4 1.5 copy-start.7
  106.5 1.5 copy-start.11
  118.2 27.0 %all-to-all-start.4 = ((bf16[8,192,512]{2,1,0:T(8,128)(2,1)}), bf16[8,192,512]{2,1,0:T(8,128)(2,1)S(1)}, u32[]{:S(2)}, u32[]{:S(2)}) async-start(bf16[8,192,512]{2,1,0:T(8,128)(2,1)} %reshape.77), calls=%async_computation.4 | async-start | bytes 3145728 | tf_op jit(solution)/shard_map/all_to_all | solution.py:37
  145.2 16.0 %copy-start.3 = (bf16[512,1536]{1,0:T(8,128)(2,1)S(1)}, bf16[512,1536]{1,0:T(8,128)(2,1)}, u32[]{:S(2)}) copy-start(bf16[512,1536]{1,0:T(8,128)(2,1)} %param.6) | copy-start | bytes 4718596
  146.1 15.1 %copy-start.1 = (bf16[1536,512]{1,0:T(8,128)(2,1)S(1)}, bf16[1536,512]{1,0:T(8,128)(2,1)}, u32[]{:S(2)}) copy-start(bf16[1536,512]{1,0:T(8,128)(2,1)} %reshape.69) | copy-start | bytes 4718596
  149.6 27.7 %all-to-all-start.5 = ((bf16[16,16,512]{2,1,0:T(8,128)(2,1)}), bf16[16,16,512]{2,1,0:T(8,128)(2,1)}, u32[]{:S(2)}, u32[]{:S(2)}) async-start(bf16[16,16,512]{2,1,0:T(8,128)(2,1)} %pad.10), calls=%async_computation.5 | async-start | bytes 524288 | tf_op jit(solution)/shard_map/all_to_all | solution.py:40
  161.2 17.1 %copy-start.8 = (bf16[12,384]{1,0:T(8,128)(2,1)S(1)}, bf16[12,384]{1,0:T(8,128)(2,1)}, u32[]{:S(2)}) copy-start(bf16[12,384]{1,0:T(8,128)(2,1)} %param.8) | copy-start | bytes 27652

commit v2 on v1

v2 whole, which is shorter than its diff:
```python
import functools

import jax
import jax.numpy as jnp
from jax import lax
from jax.experimental import pallas as pl
from jax.experimental.pallas import tpu as pltpu
from jax.sharding import Mesh
from jax.sharding import PartitionSpec as P

PATCHES = 256


EPS = 1e-06

SEC = ("xlo", "core")
FSDP = ("y", "z", "xhi")
NEAR = ("y", "xhi")
LANES = 128
VMEM_LIMIT = 28 * 1024 * 1024

nt_dims = (((1,), (1,)), ((), ()))
tn_dims = (((0,), (0,)), ((), ()))


def dot(a, b, dims=(((1,), (0,)), ((), ()))):
    return lax.dot_general(a, b, dims, preferred_element_type=jnp.float32)


def by_rows(index, rows):
    return lax.shift_right_logical(index * (65536 // rows + 1), jnp.full_like(index, 16))


def picks(shape, source_of_row):
    row = lax.broadcasted_iota(jnp.int32, shape, 0)
    column = lax.broadcasted_iota(jnp.int32, shape, 1)
    return (column == source_of_row(row)).astype(jnp.float32).astype(jnp.bfloat16)


def unpack_block(rows, blocks, column_block):
    return lambda i: i + by_rows(i, rows) * (rows * (blocks - 1)) + column_block * rows


def near_order(rows, nz):
    def source(i):
        z = by_rows(i, 2 * rows)
        rest = i - z * 2 * rows
        high = (rest >= rows).astype(jnp.int32)
        return high * (nz * rows) + z * rows + rest - high * rows

    return source


def spread_kernel(rows, x_ref, o_ref):
    copies, span, width = o_ref.shape
    blocks = width // LANES
    x = x_ref[...]
    for b in range(blocks):
        pick = picks((span, x.shape[0]), unpack_block(rows, blocks, b))
        part = dot(pick, x).astype(jnp.bfloat16)
        for k in range(copies):
            o_ref[k, :, b * LANES : (b + 1) * LANES] = part


def project_kernel(
    rows, nz, near_ref, hidden_ref, gout_ref, gain_ref, w_ref, partial_ref, sums_ref
):
    ny = near_ref.shape[0]
    span = near_ref.shape[1] * near_ref.shape[2]
    heads = hidden_ref.shape[1] // ny
    width = near_ref.shape[3]
    cut = width - LANES
    pick = picks((span, span), near_order(rows, nz))
    sums = jnp.zeros(sums_ref.shape, jnp.float32)
    for y in range(ny):
        block = near_ref[y].reshape(span, width)
        natural = dot(pick, block).astype(jnp.bfloat16)
        w_ref[y * span : (y + 1) * span, :] = natural
        sums = sums + dot(gain_ref[:, y * span : (y + 1) * span], natural[:, :cut])
    sums_ref[...] = sums
    partial_ref[:, :cut] = dot(hidden_ref[...], w_ref[:, :cut])
    partial_ref[:, cut:] = dot(gout_ref[...], w_ref[:, cut:])


def attend_kernel(rows, nz, both_ref, hidden_ref, gout_ref, near_ref, gproj_ref, att_ref):
    ny = near_ref.shape[0]
    width = near_ref.shape[3]
    span = near_ref.shape[1] * near_ref.shape[2]
    head = LANES
    scale = 1.0 / head**0.5
    for image in range(both_ref.shape[0] // PATCHES):
        at = slice(image * PATCHES, (image + 1) * PATCHES)
        query = both_ref[at, :head]
        key_in = both_ref[at, head : 2 * head]
        value = both_ref[at, 2 * head : 3 * head]
        grad_att = both_ref[at, 3 * head :]
        scores = dot(query, key_in, nt_dims) * scale
        raised = jnp.exp(scores - jnp.max(scores, axis=1, keepdims=True))
        probs = raised / jnp.sum(raised, axis=1, keepdims=True)
        probs_b = probs.astype(jnp.bfloat16)
        att_ref[at, :] = dot(probs_b, value).astype(jnp.bfloat16)
        grad_prob = dot(grad_att, value, nt_dims)
        inner = jnp.sum(grad_prob * probs, axis=1, keepdims=True)
        grad_score = (probs * (grad_prob - inner) * scale).astype(jnp.bfloat16)
        gproj_ref[at, :head] = dot(grad_score, key_in).astype(jnp.bfloat16)
        gproj_ref[at, head : 2 * head] = dot(grad_score, query, tn_dims).astype(jnp.bfloat16)
        gproj_ref[at, 2 * head :] = dot(probs_b, grad_att, tn_dims).astype(jnp.bfloat16)
    row = lax.broadcasted_iota(jnp.int32, (span, span), 0)
    column = lax.broadcasted_iota(jnp.int32, (span, span), 1)
    pick = (row == near_order(rows, nz)(column)).astype(jnp.float32).astype(jnp.bfloat16)
    cut = width - head
    for y in range(ny):
        at = slice(y * span, (y + 1) * span)
        qkv_t = dot(gproj_ref[...], hidden_ref[:, at], tn_dims).astype(jnp.bfloat16)
        out_t = dot(att_ref[...], gout_ref[:, at], tn_dims).astype(jnp.bfloat16)
        sent = dot(pick, qkv_t, nt_dims).astype(jnp.bfloat16)
        near_ref[y, :, :, :cut] = sent.reshape(2, span // 2, cut)
        sent = dot(pick, out_t, nt_dims).astype(jnp.bfloat16)
        near_ref[y, :, :, cut:] = sent.reshape(2, span // 2, head)


def fold_kernel(rows, near_ref, o_ref):
    copies, span, width = near_ref.shape
    blocks = width // LANES
    total = near_ref[0].astype(jnp.float32)
    for k in range(1, copies):
        total = total + near_ref[k].astype(jnp.float32)
    total = total.astype(jnp.bfloat16)
    row = lax.broadcasted_iota(jnp.int32, (o_ref.shape[0], span), 0)
    column = lax.broadcasted_iota(jnp.int32, (o_ref.shape[0], span), 1)
    packed = jnp.zeros(o_ref.shape, jnp.float32)
    for b in range(blocks):
        pick = row == unpack_block(rows, blocks, b)(column)
        pick = pick.astype(jnp.float32).astype(jnp.bfloat16)
        packed = packed + dot(pick, total[:, b * LANES : (b + 1) * LANES])
    o_ref[...] = packed.astype(jnp.bfloat16)


def call(kernel, out_shape, flops, moved, **more):
    return pl.pallas_call(
        kernel,
        out_shape=out_shape,
        compiler_params=pltpu.CompilerParams(vmem_limit_bytes=VMEM_LIMIT),
        cost_estimate=pl.CostEstimate(flops=flops, bytes_accessed=moved, transcendentals=0),
        **more,
    )


def array(shape, dtype=jnp.bfloat16):
    return jax.ShapeDtypeStruct(shape, dtype)


def on_device(tokens, grad_out, gain, qkv_weight, out_weight):
    tok_rows, local_width = tokens.shape
    model_width = local_width * lax.axis_size(SEC)
    head = out_weight.shape[0]
    rows = qkv_weight.shape[0]
    ny, nz, nx = (lax.axis_size(a) for a in FSDP)
    cut = 3 * head
    width = cut + head
    blocks = width // LANES

    packed = jnp.concatenate(
        [qkv_weight.reshape(rows, 3, head).transpose(1, 0, 2), out_weight.T[None]], axis=0
    ).reshape(blocks * rows, LANES)
    along_z = lax.all_to_all(
        jnp.broadcast_to(packed[None], (nz,) + packed.shape), "z", 0, 0
    ).reshape(nz * blocks * rows, LANES)

    tok_float = tokens.astype(jnp.float32)
    row_sums, row_squares = lax.psum(
        (jnp.sum(tok_float, axis=1), jnp.sum(tok_float * tok_float, axis=1)), SEC
    )

    spread = call(
        functools.partial(spread_kernel, rows),
        array((ny * nx, nz * rows, width)),
        300_000_000,
        2_000_000,
    )(along_z)
    near = lax.all_to_all(spread, NEAR, 0, 0)

    row_mean = row_sums / model_width
    row_var = row_squares / model_width - row_mean * row_mean
    inv_std = lax.rsqrt(row_var + EPS)
    normed = (tok_float - row_mean[:, None]) * inv_std[:, None]
    hidden = (normed * gain[None, :]).astype(jnp.bfloat16)

    gain_high = gain.astype(jnp.bfloat16)
    gain_low = (gain - gain_high.astype(jnp.float32)).astype(jnp.bfloat16)
    gains = jnp.concatenate(
        [gain_high[None], gain_low[None], jnp.zeros((14, local_width), jnp.bfloat16)], axis=0
    )
    weights, partial, weight_sums = call(
        functools.partial(project_kernel, rows, nz),
        (
            array((local_width, width)),
            array((tok_rows, width), jnp.float32),
            array((16, cut), jnp.float32),
        ),
        1_500_000_000,
        8_000_000,
    )(near.reshape(ny, nx, nz * rows, width), hidden, grad_out, gains)

    half = lax.all_to_all(partial.reshape(2, tok_rows // 2, width), "core", 0, 0)
    half = half[0] + half[1]
    half = (half + lax.ppermute(half, "xlo", [(0, 1), (1, 0)])).astype(jnp.bfloat16)
    both = lax.all_gather(half, "core", axis=0, tiled=True)

    sent, grad_proj = call(
        functools.partial(attend_kernel, rows, nz),
        (array((ny, nx, nz * rows, width)), array((tok_rows, cut))),
        1_800_000_000,
        6_000_000,
        scratch_shapes=[pltpu.VMEM((tok_rows, head), jnp.bfloat16)],
    )(both, hidden, grad_out)

    received = lax.all_to_all(sent.reshape(ny * nx, nz * rows, width), NEAR, 0, 0)
    folded = call(
        functools.partial(fold_kernel, rows),
        array((nz * blocks * rows, LANES)),
        300_000_000,
        2_000_000,
    )(received)
    folded = lax.all_to_all(folded.reshape(nz, blocks * rows, LANES), "z", 0, 0)
    summed = jnp.sum(folded.astype(jnp.float32), axis=0).reshape(blocks, rows, LANES)
    grad_qkv = summed[:3].transpose(1, 0, 2).reshape(rows, cut)
    grad_outw = summed[3].T
    own = lax.axis_index(FSDP) * rows
    grad_gain = jnp.sum(qkv_weight.astype(jnp.float32) * grad_qkv, axis=1) / lax.dynamic_slice(
        gain, (own,), (rows,)
    )

    weight_sums = lax.psum(weight_sums[0] + weight_sums[1], SEC)
    grad_hidden = lax.dot_general(
        grad_proj, weights[:, :cut], nt_dims, preferred_element_type=jnp.float32
    )
    proj_grad = grad_proj.astype(jnp.float32)
    first = jnp.sum(proj_grad * weight_sums[None, :], axis=1) / model_width
    second = jnp.sum(proj_grad * both[:, :cut].astype(jnp.float32), axis=1) / model_width
    grad_normed = grad_hidden * gain[None, :]
    grad_tokens = grad_out.astype(jnp.float32) + inv_std[:, None] * (
        grad_normed - first[:, None] - normed * second[:, None]
    )
    return (grad_tokens.astype(jnp.bfloat16), grad_qkv, grad_outw, grad_gain)


def solution(mesh):
    fine = Mesh(mesh.devices.reshape(2, 2, 4, 16, 2), SEC + FSDP)
    placed = (
        P(FSDP, SEC),
        P(FSDP, SEC),
        P(SEC),
        P(SEC + FSDP, None),
        P(None, SEC + FSDP),
    )
    return jax.shard_map(
        on_device,
        mesh=fine,
        in_specs=placed,
        out_specs=(
            P(FSDP, SEC),
            P(SEC + FSDP, None),
            P(None, SEC + FSDP),
            P(SEC + FSDP),
        ),
        check_vma=False,
    )
```

time: 182 us -> 152 us (0.84)
  the two profiles are of different devices: /device:TPU:64 before, /device:TPU:32 now
where the time goes in v2:
time: 152 us
  blocking collectives  46.5 us (31%)
  waiting for transfers between devices  41.3 us (27%)
  starting transfers between devices  37.4 us (25%)
  Pallas kernels  9.81 us (6%)
  other arithmetic  6.1 us (4%)
  matrix products  4.83 us (3%)
  local copies, waits for them, and re-layouts  4.75 us (3%)
    psum x1, blocking collectives, on_device(): weight_sums = lax.psum(weight_sums[0] + weight_sums[1], SEC)  20.1 us
    psum x1, blocking collectives, on_device(): lax.psum((jnp.sum(tok_float, axis=1), jnp.sum(tok_float * tok_float, axis...  19.6 us
    all_to_all x1, starting transfers between devices, on_device(): lax.all_to_all(jnp.broadcast_to(packed[None], (nz,) + packed.shape), 'z',...  15.2 us
    all_to_all x1, waiting for transfers between devices, on_device(): lax.all_to_all(jnp.broadcast_to(packed[None], (nz,) + packed.shape), 'z',...  14.9 us
    ppermute x1, waiting for transfers between devices, on_device(): lax.ppermute(half, 'xlo', [(0, 1), (1, 0)])  13.3 us
    all_to_all x1, waiting for transfers between devices, on_device(): folded = lax.all_to_all(folded.reshape(nz, blocks * rows, LANES), 'z', 0, 0)  10.6 us
    all_to_all x1, starting transfers between devices, on_device(): near = lax.all_to_all(spread, NEAR, 0, 0)  7.06 us
    all_to_all x1, starting transfers between devices, on_device(): lax.all_to_all(sent.reshape(ny * nx, nz * rows, width), NEAR, 0, 0)  6.44 us
  transfers between devices with their start and end apart: 5, of which 5 were waited for; matrix products, arithmetic and copies ran while one was open for 6% of the time, Pallas kernels for 0%

profile of v2, /device:TPU:32, one launch (start us, length us, event | category | flops | bytes accessed | tf_op | source)
XLA Modules:
  0.0 151.5 jit_solution(851010859190137686)
XLA Ops:
  0.6 0.7 reshape.46
  2.8 15.2 %all-to-all-start = ((bf16[16,48,128]{2,1,0:T(8,128)(2,1)}), bf16[16,48,128]{2,1,0:T(8,128)(2,1)S(1)}, u32[]{:S(2)}, u32[]{:S(2)}) async-start(bf16[16,48,128]{2,1,0:T(8,128)(2,1)} %broadcast_in_dim.14), calls=%async_computation | async-start | bytes 393216 | tf_op jit(solution)/shard_map/all_to_all | solution.py:166
  18.0 0.8 subtract_convert_fusion
  18.9 14.9 %all-to-all-done = bf16[16,48,128]{2,1,0:T(8,128)(2,1)S(1)} async-done(((bf16[16,48,128]{2,1,0:T(8,128)(2,1)}), bf16[16,48,128]{2,1,0:T(8,128)(2,1)S(1)}, u32[]{:S(2)}, u32[]{:S(2)}) %all-to-all-start) | async-done | bytes 196640 | tf_op jit(solution)/shard_map/all_to_all | solution.py:166
  33.8 1.7 %shard_map.84 = bf16[8,192,512]{2,1,0:T(8,128)(2,1)} custom-call(bf16[768,128]{1,0:T(8,128)(2,1)S(1)} %bitcast.25), custom_call_target="tpu_custom_call" | custom-call | flops 300000000 | bytes 2000000 | tf_op jit(solution)/shard_map/pallas_call | solution.py:175
  35.5 7.1 %all-to-all-start.1 = ((bf16[8,192,512]{2,1,0:T(8,128)(2,1)}), bf16[8,192,512]{2,1,0:T(8,128)(2,1)S(1)}, u32[]{:S(2)}, u32[]{:S(2)}) async-start(bf16[8,192,512]{2,1,0:T(8,128)(2,1)} %shard_map.84), calls=%async_computation.1 | async-start | bytes 3145728 | tf_op jit(solution)/shard_map/all_to_all | solution.py:181
  43.1 19.6 %all-reduce = (f32[512]{0:T(512)S(1)}, f32[512]{0:T(512)S(1)}) all-reduce(f32[512]{0:T(512)S(1)} %get-tuple-element.15, f32[512]{0:T(512)S(1)} %get-tuple-element.14), channel_id=1, replica_groups=mesh['xlo'=2,'core'=2,'y'=4,'z'=16,'xhi'=2] {'xlo','core'}, use_global_device_ids=true, to_apply=%region_3.0 | all-reduce | flops 1024 | bytes 8192 | tf_op jit(solution)/shard_map/psum | solution.py:171
  62.8 1.9 %fusion.8.hidden_ref = bf16[512,1536]{1,0:T(8,128)(2,1)S(1)} fusion(bf16[512,1536]{1,0:T(8,128)(2,1)} %param.5, f32[1536]{0:T(1024)S(1)} %copy-done.7, f32[512]{0:T(512)S(1)} %get-tuple-element.23, f32[512]{0:T(512)S(1)} %get-tuple-element.22), kind=kLoop, calls=%fused_computation.12 | loop fusion | flops 3932160 | bytes 3155968 | tf_op jit(solution)/shard_map/convert_element_type | solution.py:187
  65.0 1.4 copy-done.2
  66.4 2.7 %shard_map.85 = (bf16[1536,512]{1,0:T(8,128)(2,1)S(1)}, f32[512,512]{1,0:T(8,128)S(1)}, f32[16,384]{1,0:T(8,128)S(1)}) custom-call(bf16[4,2,192,512]{3,2,1,0:T(8,128)(2,1)S(1)} %bitcast.23, bf16[512,1536]{1,0:T(8,128)(2,1)S(1)} %fusion.8.hidden_ref, bf16[512,1536]{1,0:T(8,128)(2,1)S(1)} %copy-done.2, bf16[16,1536]{1,0:T(8,128)(2,1)S(1)} %maximum_maximum_fusion.gain_ref), custom_call_target="tpu_custom_call" | custom-call | flops 1500000000 | bytes 8000000 | tf_op jit(solution)/shard_map/pallas_call | solution.py:194
  69.1 4.6 %all_to_all.25 = f32[2,256,512]{2,1,0:T(8,128)S(1)} all-to-all(f32[2,256,512]{2,1,0:T(8,128)S(1)} %bitcast.24), channel_id=1, replica_groups=mesh['xlo'=2,'core'=2,'y'=4,'z'=16,'xhi'=2] {'core'}, dimensions={0} | all-to-all | bytes 2097152 | tf_op jit(solution)/shard_map/all_to_all | solution.py:205
  73.8 2.5 %collective-permute-start = (f32[256,512]{1,0:T(8,128)S(1)}, f32[256,512]{1,0:T(8,128)S(1)}, u32[]{:S(2)}, u32[]{:S(2)}) collective-permute-start(f32[256,512]{1,0:T(8,128)S(1)} %fusion.13), channel_id=1, source_target_pairs={{0,256},{256,0},{1,257},{257,1},{2,258},{258,2},{3,259},{259,3},{4... | collective-permute-start | bytes 1572872 | tf_op jit(solution)/shard_map/ppermute | solution.py:207
  76.3 13.3 %collective-permute-done = f32[256,512]{1,0:T(8,128)S(1)} collective-permute-done((f32[256,512]{1,0:T(8,128)S(1)}, f32[256,512]{1,0:T(8,128)S(1)}, u32[]{:S(2)}, u32[]{:S(2)}) %collective-permute-start) | collective-permute-done | bytes 524320 | tf_op jit(solution)/shard_map/ppermute | solution.py:207
  89.8 2.2 %all_gather.3.both_ref = bf16[512,512]{1,0:T(8,128)(2,1)S(1)} all-gather(bf16[256,512]{1,0:T(8,128)(2,1)S(1)} %add_convert_fusion), channel_id=1, replica_groups=mesh['xlo'=2,'core'=2,'y'=4,'z'=16,'xhi'=2] {'core'}, dimensions={0}, use_global_device_ids=true | all-gather | bytes 786432 | tf_op jit(solution)/shard_map/all_gather | solution.py:208
  92.0 4.0 %shard_map.86 = (bf16[4,2,192,512]{3,2,1,0:T(8,128)(2,1)S(1)}, bf16[512,384]{1,0:T(8,128)(2,1)S(1)}) custom-call(bf16[512,512]{1,0:T(8,128)(2,1)S(1)} %all_gather.3.both_ref, bf16[512,1536]{1,0:T(8,128)(2,1)S(1)} %fusion.8.hidden_ref, bf16[512,1536]{1,0:T(8,128)(2,1)S(1)} %copy-done.2), custom_call_target="tpu_custom_call" | custom-call | flops 1800000000 | bytes 6000000 | tf_op jit(solution)/shard_map/pallas_call | solution.py:210
  96.0 1.1 copy-done
  97.1 6.4 %all-to-all-start.3 = ((bf16[8,192,512]{2,1,0:T(8,128)(2,1)}), bf16[8,192,512]{2,1,0:T(8,128)(2,1)S(1)}, u32[]{:S(2)}, u32[]{:S(2)}) async-start(bf16[8,192,512]{2,1,0:T(8,128)(2,1)} %bitcast.22), calls=%async_computation.3 | async-start | bytes 3145728 | tf_op jit(solution)/shard_map/all_to_all | solution.py:218
  103.5 0.8 add_reduce_fusion
  104.3 20.1 %psum.23 = f32[384]{0:T(512)S(1)} all-reduce(f32[384]{0:T(512)S(1)} %add_reduce_fusion), channel_id=1, replica_groups=mesh['xlo'=2,'core'=2,'y'=4,'z'=16,'xhi'=2] {'xlo','core'}, use_global_device_ids=true, to_apply=%region_4.0 | all-reduce | flops 384 | bytes 3072 | tf_op jit(solution)/shard_map/psum | solution.py:234
  124.4 2.3 %all-to-all-done.3.near_ref = bf16[8,192,512]{2,1,0:T(8,128)(2,1)S(1)} async-done(((bf16[8,192,512]{2,1,0:T(8,128)(2,1)}), bf16[8,192,512]{2,1,0:T(8,128)(2,1)S(1)}, u32[]{:S(2)}, u32[]{:S(2)}) %all-to-all-start.3) | async-done | bytes 1572896 | tf_op jit(solution)/shard_map/all_to_all | solution.py:218
  126.7 1.4 shard_map.87
  128.1 6.2 %all-to-all-start.4 = ((bf16[16,48,128]{2,1,0:T(8,128)(2,1)}), bf16[16,48,128]{2,1,0:T(8,128)(2,1)S(1)}, u32[]{:S(2)}, u32[]{:S(2)}) async-start(bf16[16,48,128]{2,1,0:T(8,128)(2,1)} %bitcast.8), calls=%async_computation.4 | async-start | bytes 393216 | tf_op jit(solution)/shard_map/all_to_all | solution.py:225
  134.7 4.8 %fusion.9 = bf16[512,1536]{1,0:T(8,128)(2,1)} fusion(bf16[512,1536]{1,0:T(8,128)(2,1)} %param.5, bf16[512,384]{1,0:T(8,128)(2,1)S(1)} %get-tuple-element.10, bf16[512,1536]{1,0:T(8,128)(2,1)} %gout_ref.3, f32[512]{0:T(512)S(1)} %get-tuple-element.24, f32[512]{0:T(512)S(1)} %get-tuple-element.25, f32[1536]{0:T(1024)S(1)} %copy-done.7, ...), kind=kOutput, calls=%fused_computation.13 | convolution fusion | flops 612630528 | bytes 6305792 | tf_op jit(solution)/shard_map/dot_general | solution.py:235
  139.5 10.6 %all-to-all-done.4 = bf16[16,48,128]{2,1,0:T(8,128)(2,1)S(1)} async-done(((bf16[16,48,128]{2,1,0:T(8,128)(2,1)}), bf16[16,48,128]{2,1,0:T(8,128)(2,1)S(1)}, u32[]{:S(2)}, u32[]{:S(2)}) %all-to-all-start.4) | async-done | bytes 196640 | tf_op jit(solution)/shard_map/all_to_all | solution.py:225
  (39 shorter events, 4.3 us)
Async XLA Ops:
  2.8 31.0 %all-to-all-start = ((bf16[16,48,128]{2,1,0:T(8,128)(2,1)}), bf16[16,48,128]{2,1,0:T(8,128)(2,1)S(1)}, u32[]{:S(2)}, u32[]{:S(2)}) async-start(bf16[16,48,128]{2,1,0:T(8,128)(2,1)} %broadcast_in_dim.14), calls=%async_computation | async-start | bytes 393216 | tf_op jit(solution)/shard_map/all_to_all | solution.py:166
  35.5 7.1 %copy-start.4 = (bf16[512,1536]{1,0:T(8,128)(2,1)S(1)}, bf16[512,1536]{1,0:T(8,128)(2,1)}, u32[]{:S(2)}) copy-start(bf16[512,1536]{1,0:T(8,128)(2,1)} %param.5) | copy-start | bytes 4718596
  35.5 29.4 %all-to-all-start.1 = ((bf16[8,192,512]{2,1,0:T(8,128)(2,1)}), bf16[8,192,512]{2,1,0:T(8,128)(2,1)S(1)}, u32[]{:S(2)}, u32[]{:S(2)}) async-start(bf16[8,192,512]{2,1,0:T(8,128)(2,1)} %shard_map.84), calls=%async_computation.1 | async-start | bytes 3145728 | tf_op jit(solution)/shard_map/all_to_all | solution.py:181
  42.6 20.2 %copy-start.7 = (f32[1536]{0:T(1024)S(1)}, f32[1536]{0:T(1024)}, u32[]{:S(2)}) copy-start(f32[1536]{0:T(1024)} %param.7) | copy-start | bytes 18436
  65.0 1.4 copy-start.2
  69.1 4.7 %copy-start.1 = (f32[16,384]{1,0:T(8,128)}, f32[16,384]{1,0:T(8,128)S(1)}, u32[]{:S(2)}) copy-start(f32[16,384]{1,0:T(8,128)S(1)} %get-tuple-element.12) | copy-start | bytes 73732
  69.1 4.7 %copy-start.3 = (bf16[1536,512]{1,0:T(8,128)(2,1)}, bf16[1536,512]{1,0:T(8,128)(2,1)S(1)}, u32[]{:S(2)}) copy-start(bf16[1536,512]{1,0:T(8,128)(2,1)S(1)} %get-tuple-element.11) | copy-start | bytes 4718596
  73.8 15.9 %collective-permute-start = (f32[256,512]{1,0:T(8,128)S(1)}, f32[256,512]{1,0:T(8,128)S(1)}, u32[]{:S(2)}, u32[]{:S(2)}) collective-permute-start(f32[256,512]{1,0:T(8,128)S(1)} %fusion.13), channel_id=1, source_target_pairs={{0,256},{256,0},{1,257},{257,1},{2,258},{258,2},{3,259},{259,3},{4... | collective-permute-start | bytes 1572872 | tf_op jit(solution)/shard_map/ppermute | solution.py:207
  96.0 1.1 copy-start
  97.1 29.6 %all-to-all-start.3 = ((bf16[8,192,512]{2,1,0:T(8,128)(2,1)}), bf16[8,192,512]{2,1,0:T(8,128)(2,1)S(1)}, u32[]{:S(2)}, u32[]{:S(2)}) async-start(bf16[8,192,512]{2,1,0:T(8,128)(2,1)} %bitcast.22), calls=%async_computation.3 | async-start | bytes 3145728 | tf_op jit(solution)/shard_map/all_to_all | solution.py:218
  128.1 22.0 %all-to-all-start.4 = ((bf16[16,48,128]{2,1,0:T(8,128)(2,1)}), bf16[16,48,128]{2,1,0:T(8,128)(2,1)S(1)}, u32[]{:S(2)}, u32[]{:S(2)}) async-start(bf16[16,48,128]{2,1,0:T(8,128)(2,1)} %bitcast.8), calls=%async_computation.4 | async-start | bytes 393216 | tf_op jit(solution)/shard_map/all_to_all | solution.py:225
  134.7 16.1 %copy-start.6 = (bf16[12,384]{1,0:T(8,128)(2,1)S(1)}, bf16[12,384]{1,0:T(8,128)(2,1)}, u32[]{:S(2)}) copy-start(bf16[12,384]{1,0:T(8,128)(2,1)} %param.8) | copy-start | bytes 27652
  150.8 0.7 copy-start.5

commit v3 on v2

--- a/solution.py
+++ b/solution.py
@@ -51,7 +51,25 @@
     return source
 
 
-def spread_kernel(rows, x_ref, o_ref):
+def pack_kernel(qkv_ref, out_t_ref, o_ref):
+    copies, span, _ = o_ref.shape
+    rows = qkv_ref.shape[0]
+    blocks = span // rows
+    packed = jnp.zeros((span, LANES), jnp.float32)
+    for b in range(blocks):
+        pick = picks((span, rows), lambda i: i - b * rows)
+        last = b == blocks - 1
+        block = out_t_ref[...] if last else qkv_ref[:, b * LANES : (b + 1) * LANES]
+        packed = packed + dot(pick, block)
+    packed = packed.astype(jnp.bfloat16)
+    for k in range(copies):
+        o_ref[k] = packed
+
+
+def spread_kernel(rows, model_width, x_ref, stats_ref, o_ref, norm_ref):
+    mean = stats_ref[0:1] / model_width
+    norm_ref[0:1] = mean
+    norm_ref[1:2] = lax.rsqrt(stats_ref[1:2] / model_width - mean * mean + EPS)
     copies, span, width = o_ref.shape
     blocks = width // LANES
     x = x_ref[...]
@@ -63,27 +81,39 @@
 
 
 def project_kernel(
-    rows, nz, near_ref, hidden_ref, gout_ref, gain_ref, w_ref, partial_ref, sums_ref
+    rows, nz, near_ref, hidden_ref, gout_hbm, gain_ref, w_ref, partial_ref, gout_ref, sem
 ):
+    fetch = pltpu.make_async_copy(gout_hbm, gout_ref, sem)
+    fetch.start()
     ny = near_ref.shape[0]
     span = near_ref.shape[1] * near_ref.shape[2]
-    heads = hidden_ref.shape[1] // ny
     width = near_ref.shape[3]
     cut = width - LANES
+    half = hidden_ref.shape[0] // 2
     pick = picks((span, span), near_order(rows, nz))
-    sums = jnp.zeros(sums_ref.shape, jnp.float32)
+    sums = jnp.zeros((gain_ref.shape[0], cut), jnp.float32)
     for y in range(ny):
         block = near_ref[y].reshape(span, width)
         natural = dot(pick, block).astype(jnp.bfloat16)
         w_ref[y * span : (y + 1) * span, :] = natural
         sums = sums + dot(gain_ref[:, y * span : (y + 1) * span], natural[:, :cut])
-    sums_ref[...] = sums
-    partial_ref[:, :cut] = dot(hidden_ref[...], w_ref[:, :cut])
-    partial_ref[:, cut:] = dot(gout_ref[...], w_ref[:, cut:])
-
-
-def attend_kernel(rows, nz, both_ref, hidden_ref, gout_ref, near_ref, gproj_ref, att_ref):
+    for h in range(2):
+        at = slice(h * half, (h + 1) * half)
+        partial_ref[h, half:, :cut] = sums[:8]
+        partial_ref[h, half:, cut:] = jnp.zeros((8, LANES), jnp.float32)
+        partial_ref[h, :half, :cut] = dot(hidden_ref[at, :], w_ref[:, :cut])
+    fetch.wait()
+    for h in range(2):
+        at = slice(h * half, (h + 1) * half)
+        partial_ref[h, :half, cut:] = dot(gout_ref[at, :], w_ref[:, cut:])
+
+
+def attend_kernel(
+    rows, nz, both_ref, hidden_ref, gout_hbm, near_hbm, gproj_ref, att_ref, gout_ref, near_ref, sem
+):
     ny = near_ref.shape[0]
+    fetch = pltpu.make_async_copy(gout_hbm, gout_ref, sem.at[ny])
+    fetch.start()
     width = near_ref.shape[3]
     span = near_ref.shape[1] * near_ref.shape[2]
     head = LANES
@@ -109,6 +139,8 @@
     column = lax.broadcasted_iota(jnp.int32, (span, span), 1)
     pick = (row == near_order(rows, nz)(column)).astype(jnp.float32).astype(jnp.bfloat16)
     cut = width - head
+    fetch.wait()
+    stores = []
     for y in range(ny):
         at = slice(y * span, (y + 1) * span)
         qkv_t = dot(gproj_ref[...], hidden_ref[:, at], tn_dims).astype(jnp.bfloat16)
@@ -117,6 +149,10 @@
         near_ref[y, :, :, :cut] = sent.reshape(2, span // 2, cut)
         sent = dot(pick, out_t, nt_dims).astype(jnp.bfloat16)
         near_ref[y, :, :, cut:] = sent.reshape(2, span // 2, head)
+        stores.append(pltpu.make_async_copy(near_ref.at[y], near_hbm.at[y], sem.at[y]))
+        stores[y].start()
+    for store in stores:
+        store.wait()
 
 
 def fold_kernel(rows, near_ref, o_ref):
@@ -136,6 +172,27 @@
     o_ref[...] = packed.astype(jnp.bfloat16)
 
 
+def finish_kernel(x_ref, qkv_ref, gain_ref, grad_ref, out_t_ref, gg_ref):
+    rows = qkv_ref.shape[0]
+    copies, span, _ = x_ref.shape
+    x = x_ref[...].reshape(copies * span, LANES)
+    blocks = span // rows
+    row = lax.broadcasted_iota(jnp.int32, (rows, copies * span), 0)
+    column = lax.broadcasted_iota(jnp.int32, (rows, copies * span), 1)
+    within = column - by_rows(column, span) * span
+    products = jnp.zeros((rows, LANES), jnp.float32)
+    for b in range(blocks):
+        pick = (within == row + b * rows).astype(jnp.float32).astype(jnp.bfloat16)
+        part = dot(pick, x)
+        if b == blocks - 1:
+            out_t_ref[...] = part
+        else:
+            at = slice(b * LANES, (b + 1) * LANES)
+            grad_ref[:, at] = part
+            products = products + part * qkv_ref[:, at].astype(jnp.float32)
+    gg_ref[...] = jnp.sum(products, axis=1, keepdims=True) / gain_ref[...]
+
+
 def call(kernel, out_shape, flops, moved, **more):
     return pl.pallas_call(
         kernel,
@@ -160,29 +217,25 @@
     width = cut + head
     blocks = width // LANES
 
-    packed = jnp.concatenate(
-        [qkv_weight.reshape(rows, 3, head).transpose(1, 0, 2), out_weight.T[None]], axis=0
-    ).reshape(blocks * rows, LANES)
-    along_z = lax.all_to_all(
-        jnp.broadcast_to(packed[None], (nz,) + packed.shape), "z", 0, 0
-    ).reshape(nz * blocks * rows, LANES)
+    packed = call(pack_kernel, array((nz, blocks * rows, LANES)), 1_000_000, 200_000)(
+        qkv_weight, out_weight.T
+    )
+    along_z = lax.all_to_all(packed, "z", 0, 0).reshape(nz * blocks * rows, LANES)
 
     tok_float = tokens.astype(jnp.float32)
-    row_sums, row_squares = lax.psum(
-        (jnp.sum(tok_float, axis=1), jnp.sum(tok_float * tok_float, axis=1)), SEC
-    )
-
-    spread = call(
-        functools.partial(spread_kernel, rows),
-        array((ny * nx, nz * rows, width)),
+    stats = lax.psum(
+        jnp.stack([jnp.sum(tok_float, axis=1), jnp.sum(tok_float * tok_float, axis=1)]), SEC
+    )
+
+    spread, norms = call(
+        functools.partial(spread_kernel, rows, model_width),
+        (array((ny * nx, nz * rows, width)), array((2, tok_rows), jnp.float32)),
         300_000_000,
         2_000_000,
-    )(along_z)
+    )(along_z, stats)
     near = lax.all_to_all(spread, NEAR, 0, 0)
 
-    row_mean = row_sums / model_width
-    row_var = row_squares / model_width - row_mean * row_mean
-    inv_std = lax.rsqrt(row_var + EPS)
+    row_mean, inv_std = norms[0], norms[1]
     normed = (tok_float - row_mean[:, None]) * inv_std[:, None]
     hidden = (normed * gain[None, :]).astype(jnp.bfloat16)
 
@@ -191,29 +244,42 @@
     gains = jnp.concatenate(
         [gain_high[None], gain_low[None], jnp.zeros((14, local_width), jnp.bfloat16)], axis=0
     )
-    weights, partial, weight_sums = call(
+    grad_out_hbm = pltpu.with_memory_space_constraint(grad_out, pltpu.HBM)
+    in_hbm = pl.BlockSpec(memory_space=pltpu.HBM)
+    in_vmem = pl.BlockSpec(memory_space=pltpu.VMEM)
+    half_rows = tok_rows // 2
+    weights, partial = call(
         functools.partial(project_kernel, rows, nz),
-        (
-            array((local_width, width)),
-            array((tok_rows, width), jnp.float32),
-            array((16, cut), jnp.float32),
-        ),
+        (array((local_width, width)), array((2, half_rows + 8, width), jnp.float32)),
         1_500_000_000,
         8_000_000,
-    )(near.reshape(ny, nx, nz * rows, width), hidden, grad_out, gains)
-
-    half = lax.all_to_all(partial.reshape(2, tok_rows // 2, width), "core", 0, 0)
+        in_specs=[in_vmem, in_vmem, in_hbm, in_vmem],
+        scratch_shapes=[
+            pltpu.VMEM((tok_rows, local_width), jnp.bfloat16),
+            pltpu.SemaphoreType.DMA,
+        ],
+    )(near.reshape(ny, nx, nz * rows, width), hidden, grad_out_hbm, gains)
+
+    half = lax.all_to_all(partial, "core", 0, 0)
     half = half[0] + half[1]
-    half = (half + lax.ppermute(half, "xlo", [(0, 1), (1, 0)])).astype(jnp.bfloat16)
-    both = lax.all_gather(half, "core", axis=0, tiled=True)
+    half = half + lax.ppermute(half, "xlo", [(0, 1), (1, 0)])
+    weight_sums = half[half_rows, :cut] + half[half_rows + 1, :cut]
+    both = lax.all_gather(half[:half_rows].astype(jnp.bfloat16), "core", axis=0, tiled=True)
 
     sent, grad_proj = call(
         functools.partial(attend_kernel, rows, nz),
-        (array((ny, nx, nz * rows, width)), array((tok_rows, cut))),
+        (pltpu.HBM((ny, nx, nz * rows, width), jnp.bfloat16), array((tok_rows, cut))),
         1_800_000_000,
         6_000_000,
-        scratch_shapes=[pltpu.VMEM((tok_rows, head), jnp.bfloat16)],
-    )(both, hidden, grad_out)
+        in_specs=[in_vmem, in_vmem, in_hbm],
+        out_specs=(in_hbm, in_vmem),
+        scratch_shapes=[
+            pltpu.VMEM((tok_rows, head), jnp.bfloat16),
+            pltpu.VMEM((tok_rows, local_width), jnp.bfloat16),
+            pltpu.VMEM((ny, nx, nz * rows, width), jnp.bfloat16),
+            pltpu.SemaphoreType.DMA((ny + 1,)),
+        ],
+    )(both, hidden, grad_out_hbm)
 
     received = lax.all_to_all(sent.reshape(ny * nx, nz * rows, width), NEAR, 0, 0)
     folded = call(
@@ -223,15 +289,19 @@
         2_000_000,
     )(received)
     folded = lax.all_to_all(folded.reshape(nz, blocks * rows, LANES), "z", 0, 0)
-    summed = jnp.sum(folded.astype(jnp.float32), axis=0).reshape(blocks, rows, LANES)
-    grad_qkv = summed[:3].transpose(1, 0, 2).reshape(rows, cut)
-    grad_outw = summed[3].T
     own = lax.axis_index(FSDP) * rows
-    grad_gain = jnp.sum(qkv_weight.astype(jnp.float32) * grad_qkv, axis=1) / lax.dynamic_slice(
-        gain, (own,), (rows,)
-    )
-
-    weight_sums = lax.psum(weight_sums[0] + weight_sums[1], SEC)
+    own_gain = lax.dynamic_slice(gain, (own,), (rows,)).reshape(rows, 1)
+    grad_qkv, grad_outw_t, grad_gain = call(
+        finish_kernel,
+        (
+            array((rows, cut), jnp.float32),
+            array((rows, head), jnp.float32),
+            array((rows, 1), jnp.float32),
+        ),
+        10_000_000,
+        300_000,
+    )(folded, qkv_weight, own_gain)
+
     grad_hidden = lax.dot_general(
         grad_proj, weights[:, :cut], nt_dims, preferred_element_type=jnp.float32
     )
@@ -242,7 +312,12 @@
     grad_tokens = grad_out.astype(jnp.float32) + inv_std[:, None] * (
         grad_normed - first[:, None] - normed * second[:, None]
     )
-    return (grad_tokens.astype(jnp.bfloat16), grad_qkv, grad_outw, grad_gain)
+    return (
+        grad_tokens.astype(jnp.bfloat16),
+        grad_qkv,
+        grad_outw_t.T,
+        grad_gain.reshape(rows),
+    )
 
 
 def solution(mesh):

time: 152 us -> 150 us (0.987)
  waiting for transfers between devices: 41.3 us -> 75.4 us
  blocking collectives: 46.5 us -> 13.1 us
  Pallas kernels: 9.81 us -> 13.9 us
  local copies, waits for them, and re-layouts: 4.75 us -> 1.72 us
  starting transfers between devices: 37.4 us -> 34.5 us
    psum x2 -> x1, blocking collectives: 39.7 us -> 6.33 us  [on_device(): lax.psum(jnp.stack([jnp.sum(tok_float, axis=1), jnp.sum(tok_float * tok_f...]
    all_to_all x1, waiting for transfers between devices: 2.27 us -> 23.2 us  [on_device(): lax.all_to_all(sent.reshape(ny * nx, nz * rows, width), NEAR, 0, 0)]
    all_to_all x1, waiting for transfers between devices: 0.18 us -> 20.2 us  [on_device(): near = lax.all_to_all(spread, NEAR, 0, 0)]
    all_to_all x1, waiting for transfers between devices: 14.9 us -> 7.51 us  [on_device(): lax.all_to_all(packed, 'z', 0, 0).reshape(nz * blocks * rows, LANES)]
    all_to_all x1, starting transfers between devices: 6.44 us -> 3.59 us  [on_device(): lax.all_to_all(sent.reshape(ny * nx, nz * rows, width), NEAR, 0, 0)]
    pallas_call x2 -> x4, Pallas kernels: 5.68 us -> 8.29 us  [the longest x1 4.92 us: on_device(): call(functools.partial(attend_kernel, rows, nz), (pltpu.HBM((ny, nx, nz *...]
where the time goes in v3:
time: 150 us
  waiting for transfers between devices  75.4 us (50%)
  starting transfers between devices  34.5 us (23%)
  Pallas kernels  13.9 us (9%)
  blocking collectives  13.1 us (9%)
  other arithmetic  5.19 us (3%)
  matrix products  4.83 us (3%)
  local copies, waits for them, and re-layouts  1.72 us (1%)
    all_to_all x1, waiting for transfers between devices, on_device(): lax.all_to_all(sent.reshape(ny * nx, nz * rows, width), NEAR, 0, 0)  23.2 us
    all_to_all x1, waiting for transfers between devices, on_device(): near = lax.all_to_all(spread, NEAR, 0, 0)  20.2 us
    all_to_all x1, starting transfers between devices, on_device(): lax.all_to_all(packed, 'z', 0, 0).reshape(nz * blocks * rows, LANES)  15.2 us
    ppermute x1, waiting for transfers between devices, on_device(): half = half + lax.ppermute(half, 'xlo', [(0, 1), (1, 0)])  13.7 us
    all_to_all x1, waiting for transfers between devices, on_device(): folded = lax.all_to_all(folded.reshape(nz, blocks * rows, LANES), 'z', 0, 0)  10.9 us
    all_to_all x1, waiting for transfers between devices, on_device(): lax.all_to_all(packed, 'z', 0, 0).reshape(nz * blocks * rows, LANES)  7.51 us
    all_to_all x1, starting transfers between devices, on_device(): near = lax.all_to_all(spread, NEAR, 0, 0)  7.05 us
    psum x1, blocking collectives, on_device(): lax.psum(jnp.stack([jnp.sum(tok_float, axis=1), jnp.sum(tok_float * tok_f...  6.33 us
  transfers between devices with their start and end apart: 5, of which 5 were waited for; matrix products, arithmetic and copies ran while one was open for 6% of the time, Pallas kernels for 0%

profile of v3, /device:TPU:32, one launch (start us, length us, event | category | flops | bytes accessed | tf_op | source)
XLA Modules:
  0.0 149.5 jit_solution(12643680343218830572)
XLA Ops:
  0.6 0.7 copy-done.2
  1.3 0.7 copy-done.4
  2.0 0.8 shard_map.84
  2.9 15.2 %all-to-all-start = ((bf16[16,48,128]{2,1,0:T(8,128)(2,1)}), bf16[16,48,128]{2,1,0:T(8,128)(2,1)S(1)}, u32[]{:S(2)}, u32[]{:S(2)}) async-start(bf16[16,48,128]{2,1,0:T(8,128)(2,1)} %shard_map.84), calls=%async_computation | async-start | bytes 393216 | tf_op jit(solution)/shard_map/all_to_all | solution.py:223
  18.1 2.0 %convert_reduce_fusion = (f32[512]{0:T(512)S(1)}, f32[512]{0:T(512)S(1)}) fusion(bf16[512,1536]{1,0:T(8,128)(2,1)} %param.5), kind=kLoop, calls=%fused_computation.2 | loop fusion | flops 3144704 | bytes 1576960 | tf_op jit(solution)/shard_map/reduce_sum | solution.py:227
  20.1 6.3 %psum.7.stats_ref = f32[2,512]{1,0:T(2,128)S(1)} all-reduce(f32[2,512]{1,0:T(2,128)S(1)} %pad_maximum_fusion), channel_id=1, replica_groups=mesh['xlo'=2,'core'=2,'y'=4,'z'=16,'xhi'=2] {'xlo','core'}, use_global_device_ids=true, to_apply=%region_2.0 | all-reduce | flops 1024 | bytes 8192 | tf_op jit(solution)/shard_map/psum | solution.py:226
  26.4 7.5 %all-to-all-done = bf16[16,48,128]{2,1,0:T(8,128)(2,1)S(1)} async-done(((bf16[16,48,128]{2,1,0:T(8,128)(2,1)}), bf16[16,48,128]{2,1,0:T(8,128)(2,1)S(1)}, u32[]{:S(2)}, u32[]{:S(2)}) %all-to-all-start) | async-done | bytes 196640 | tf_op jit(solution)/shard_map/all_to_all | solution.py:223
  33.9 1.7 %shard_map.85 = (bf16[8,192,512]{2,1,0:T(8,128)(2,1)}, f32[2,512]{1,0:T(2,128)S(1)}) custom-call(bf16[768,128]{1,0:T(8,128)(2,1)S(1)} %bitcast.18, f32[2,512]{1,0:T(2,128)S(1)} %psum.7.stats_ref), custom_call_target="tpu_custom_call" | custom-call | flops 300000000 | bytes 2000000 | tf_op jit(solution)/shard_map/pallas_call | solution.py:230
  35.6 7.0 %all-to-all-start.1 = ((bf16[8,192,512]{2,1,0:T(8,128)(2,1)}), bf16[8,192,512]{2,1,0:T(8,128)(2,1)S(1)}, u32[]{:S(2)}, u32[]{:S(2)}) async-start(bf16[8,192,512]{2,1,0:T(8,128)(2,1)} %get-tuple-element.14), calls=%async_computation.1 | async-start | bytes 3145728 | tf_op jit(solution)/shard_map/all_to_all | solution.py:236
  42.9 1.9 %fusion.8.hidden_ref = bf16[512,1536]{1,0:T(8,128)(2,1)S(1)} fusion(bf16[512,1536]{1,0:T(8,128)(2,1)} %param.5, f32[1536]{0:T(1024)S(1)} %copy-done.6, f32[512]{0:T(512)S(1)} %bitcast.23, f32[512]{0:T(512)S(1)} %bitcast.21), kind=kLoop, calls=%fused_computation.12 | loop fusion | flops 3932160 | bytes 3155968 | tf_op jit(solution)/shard_map/convert_element_type | solution.py:240
  44.8 20.2 %all-to-all-done.1 = bf16[8,192,512]{2,1,0:T(8,128)(2,1)S(1)} async-done(((bf16[8,192,512]{2,1,0:T(8,128)(2,1)}), bf16[8,192,512]{2,1,0:T(8,128)(2,1)S(1)}, u32[]{:S(2)}, u32[]{:S(2)}) %all-to-all-start.1) | async-done | bytes 1572896 | tf_op jit(solution)/shard_map/all_to_all | solution.py:236
  65.0 4.2 %shard_map.86 = (bf16[1536,512]{1,0:T(8,128)(2,1)S(1)}, f32[2,264,512]{2,1,0:T(8,128)S(1)}) custom-call(bf16[4,2,192,512]{3,2,1,0:T(8,128)(2,1)S(1)} %bitcast.17, bf16[512,1536]{1,0:T(8,128)(2,1)S(1)} %fusion.8.hidden_ref, bf16[512,1536]{1,0:T(8,128)(2,1)} %gout_hbm.3, bf16[16,1536]{1,0:T(8,128)(2,1)S(1)} %maximum_maximum_fusion.gain_ref), custom_call_target="tpu_custom_call" | custom-call | flops 1500000000 | bytes 8000000 | tf_op jit(solution)/shard_map/pallas_call | solution.py:251
  69.3 4.6 %all_to_all.25 = f32[2,264,512]{2,1,0:T(8,128)S(1)} all-to-all(f32[2,264,512]{2,1,0:T(8,128)S(1)} %get-tuple-element.15), channel_id=1, replica_groups=mesh['xlo'=2,'core'=2,'y'=4,'z'=16,'xhi'=2] {'core'}, dimensions={0} | all-to-all | bytes 2162688 | tf_op jit(solution)/shard_map/all_to_all | solution.py:263
  73.9 2.6 %collective-permute-start = (f32[264,512]{1,0:T(8,128)S(1)}, f32[264,512]{1,0:T(8,128)S(1)}, u32[]{:S(2)}, u32[]{:S(2)}) collective-permute-start(f32[264,512]{1,0:T(8,128)S(1)} %fusion.13), channel_id=1, source_target_pairs={{0,256},{256,0},{1,257},{257,1},{2,258},{258,2},{3,259},{259,3},{4... | collective-permute-start | bytes 1622024 | tf_op jit(solution)/shard_map/ppermute | solution.py:265
  76.6 13.7 %collective-permute-done = f32[264,512]{1,0:T(8,128)S(1)} collective-permute-done((f32[264,512]{1,0:T(8,128)S(1)}, f32[264,512]{1,0:T(8,128)S(1)}, u32[]{:S(2)}, u32[]{:S(2)}) %collective-permute-start) | collective-permute-done | bytes 540704 | tf_op jit(solution)/shard_map/ppermute | solution.py:265
  90.5 2.2 %all_gather.3.both_ref = bf16[512,512]{1,0:T(8,128)(2,1)S(1)} all-gather(bf16[256,512]{1,0:T(8,128)(2,1)S(1)} %slice.55), channel_id=1, replica_groups=mesh['xlo'=2,'core'=2,'y'=4,'z'=16,'xhi'=2] {'core'}, dimensions={0}, use_global_device_ids=true | all-gather | bytes 786432 | tf_op jit(solution)/shard_map/all_gather | solution.py:267
  92.7 4.9 %shard_map.87 = (bf16[4,2,192,512]{3,2,1,0:T(8,128)(2,1)}, bf16[512,384]{1,0:T(8,128)(2,1)S(1)}) custom-call(bf16[512,512]{1,0:T(8,128)(2,1)S(1)} %all_gather.3.both_ref, bf16[512,1536]{1,0:T(8,128)(2,1)S(1)} %copy-done.1, bf16[512,1536]{1,0:T(8,128)(2,1)} %gout_hbm.3), custom_call_target="tpu_custom_call" | custom-call | flops 1800000000 | bytes 6000000 | tf_op jit(solution)/shard_map/pallas_call | solution.py:269
  97.6 3.6 %all-to-all-start.3 = ((bf16[8,192,512]{2,1,0:T(8,128)(2,1)}), bf16[8,192,512]{2,1,0:T(8,128)(2,1)S(1)}, u32[]{:S(2)}, u32[]{:S(2)}) async-start(bf16[8,192,512]{2,1,0:T(8,128)(2,1)} %bitcast.20), calls=%async_computation.3 | async-start | bytes 3145728 | tf_op jit(solution)/shard_map/all_to_all | solution.py:284
  101.4 23.2 %all-to-all-done.3.near_ref = bf16[8,192,512]{2,1,0:T(8,128)(2,1)S(1)} async-done(((bf16[8,192,512]{2,1,0:T(8,128)(2,1)}), bf16[8,192,512]{2,1,0:T(8,128)(2,1)S(1)}, u32[]{:S(2)}, u32[]{:S(2)}) %all-to-all-start.3) | async-done | bytes 1572896 | tf_op jit(solution)/shard_map/all_to_all | solution.py:284
  124.6 1.4 shard_map.88
  126.0 6.1 %all-to-all-start.4 = ((bf16[16,48,128]{2,1,0:T(8,128)(2,1)}), bf16[16,48,128]{2,1,0:T(8,128)(2,1)S(1)}, u32[]{:S(2)}, u32[]{:S(2)}) async-start(bf16[16,48,128]{2,1,0:T(8,128)(2,1)} %bitcast.9), calls=%async_computation.4 | async-start | bytes 393216 | tf_op jit(solution)/shard_map/all_to_all | solution.py:291
  132.4 4.8 %fusion.9 = bf16[512,1536]{1,0:T(8,128)(2,1)} fusion(bf16[512,1536]{1,0:T(8,128)(2,1)} %param.5, bf16[512,384]{1,0:T(8,128)(2,1)S(1)} %get-tuple-element.16, bf16[512,1536]{1,0:T(8,128)(2,1)} %gout_hbm.3, f32[512]{0:T(512)S(1)} %get-tuple-element.30, f32[512]{0:T(512)S(1)} %get-tuple-element.31, f32[1536]{0:T(1024)S(1)} %copy-done.6, f32[512]{0:T(512)S(1)} %bitcast.24, ...), kind=kOutput, calls=%fused_computation.13 | convolution fusion | flops 612630528 | bytes 6305792 | tf_op jit(solution)/shard_map/dot_general | solution.py:305
  137.2 10.9 %all-to-all-done.4.x_ref = bf16[16,48,128]{2,1,0:T(8,128)(2,1)S(1)} async-done(((bf16[16,48,128]{2,1,0:T(8,128)(2,1)}), bf16[16,48,128]{2,1,0:T(8,128)(2,1)S(1)}, u32[]{:S(2)}, u32[]{:S(2)}) %all-to-all-start.4) | async-done | bytes 196640 | tf_op jit(solution)/shard_map/all_to_all | solution.py:291
  148.1 0.8 shard_map.89
  (29 shorter events, 1.6 us)
Async XLA Ops:
  0.6 0.7 copy-start.2
  1.3 0.7 copy-start.4
  2.9 31.0 %all-to-all-start = ((bf16[16,48,128]{2,1,0:T(8,128)(2,1)}), bf16[16,48,128]{2,1,0:T(8,128)(2,1)S(1)}, u32[]{:S(2)}, u32[]{:S(2)}) async-start(bf16[16,48,128]{2,1,0:T(8,128)(2,1)} %shard_map.84), calls=%async_computation | async-start | bytes 393216 | tf_op jit(solution)/shard_map/all_to_all | solution.py:223
  35.6 7.1 %copy-start.6 = (f32[1536]{0:T(1024)S(1)}, f32[1536]{0:T(1024)}, u32[]{:S(2)}) copy-start(f32[1536]{0:T(1024)} %param.7) | copy-start | bytes 18436
  35.6 29.4 %all-to-all-start.1 = ((bf16[8,192,512]{2,1,0:T(8,128)(2,1)}), bf16[8,192,512]{2,1,0:T(8,128)(2,1)S(1)}, u32[]{:S(2)}, u32[]{:S(2)}) async-start(bf16[8,192,512]{2,1,0:T(8,128)(2,1)} %get-tuple-element.14), calls=%async_computation.1 | async-start | bytes 3145728 | tf_op jit(solution)/shard_map/all_to_all | solution.py:236
  44.8 24.4 %copy-start = (bf16[512,1536]{1,0:T(8,128)(2,1)}, bf16[512,1536]{1,0:T(8,128)(2,1)S(1)}, u32[]{:S(2)}) copy-start(bf16[512,1536]{1,0:T(8,128)(2,1)S(1)} %fusion.8.hidden_ref) | copy-start | bytes 4718596
  69.2 4.6 %copy-start.5 = (bf16[1536,512]{1,0:T(8,128)(2,1)}, bf16[1536,512]{1,0:T(8,128)(2,1)S(1)}, u32[]{:S(2)}) copy-start(bf16[1536,512]{1,0:T(8,128)(2,1)S(1)} %get-tuple-element.17) | copy-start | bytes 4718596
  73.9 18.7 %copy-start.1 = (bf16[512,1536]{1,0:T(8,128)(2,1)S(1)}, bf16[512,1536]{1,0:T(8,128)(2,1)}, u32[]{:S(2)}) copy-start(bf16[512,1536]{1,0:T(8,128)(2,1)} %copy-done) | copy-start | bytes 4718596
  73.9 16.3 %collective-permute-start = (f32[264,512]{1,0:T(8,128)S(1)}, f32[264,512]{1,0:T(8,128)S(1)}, u32[]{:S(2)}, u32[]{:S(2)}) collective-permute-start(f32[264,512]{1,0:T(8,128)S(1)} %fusion.13), channel_id=1, source_target_pairs={{0,256},{256,0},{1,257},{257,1},{2,258},{258,2},{3,259},{259,3},{4... | collective-permute-start | bytes 1622024 | tf_op jit(solution)/shard_map/ppermute | solution.py:265
  97.6 27.0 %all-to-all-start.3 = ((bf16[8,192,512]{2,1,0:T(8,128)(2,1)}), bf16[8,192,512]{2,1,0:T(8,128)(2,1)S(1)}, u32[]{:S(2)}, u32[]{:S(2)}) async-start(bf16[8,192,512]{2,1,0:T(8,128)(2,1)} %bitcast.20), calls=%async_computation.3 | async-start | bytes 3145728 | tf_op jit(solution)/shard_map/all_to_all | solution.py:284
  126.0 22.1 %all-to-all-start.4 = ((bf16[16,48,128]{2,1,0:T(8,128)(2,1)}), bf16[16,48,128]{2,1,0:T(8,128)(2,1)S(1)}, u32[]{:S(2)}, u32[]{:S(2)}) async-start(bf16[16,48,128]{2,1,0:T(8,128)(2,1)} %bitcast.9), calls=%async_computation.4 | async-start | bytes 393216 | tf_op jit(solution)/shard_map/all_to_all | solution.py:291
  132.4 15.7 %copy-start.3 = (bf16[12,384]{1,0:T(8,128)(2,1)S(1)}, bf16[12,384]{1,0:T(8,128)(2,1)}, u32[]{:S(2)}) copy-start(bf16[12,384]{1,0:T(8,128)(2,1)} %qkv_ref.3) | copy-start | bytes 27652

commit v4 on v3

--- a/solution.py
+++ b/solution.py
@@ -15,7 +15,7 @@
 
 SEC = ("xlo", "core")
 FSDP = ("y", "z", "xhi")
-NEAR = ("y", "xhi")
+NEAR = ("xhi", "y")
 LANES = 128
 VMEM_LIMIT = 28 * 1024 * 1024
 
@@ -51,7 +51,15 @@
     return source
 
 
-def pack_kernel(qkv_ref, out_t_ref, o_ref):
+def pack_kernel(qkv_hbm, out_t_hbm, o_ref, qkv_ref, out_t_ref, sem):
+    fetches = [
+        pltpu.make_async_copy(qkv_hbm, qkv_ref, sem.at[0]),
+        pltpu.make_async_copy(out_t_hbm, out_t_ref, sem.at[1]),
+    ]
+    for fetch in fetches:
+        fetch.start()
+    for fetch in fetches:
+        fetch.wait()
     copies, span, _ = o_ref.shape
     rows = qkv_ref.shape[0]
     blocks = span // rows
@@ -66,10 +74,7 @@
         o_ref[k] = packed
 
 
-def spread_kernel(rows, model_width, x_ref, stats_ref, o_ref, norm_ref):
-    mean = stats_ref[0:1] / model_width
-    norm_ref[0:1] = mean
-    norm_ref[1:2] = lax.rsqrt(stats_ref[1:2] / model_width - mean * mean + EPS)
+def spread_kernel(rows, x_ref, o_ref):
     copies, span, width = o_ref.shape
     blocks = width // LANES
     x = x_ref[...]
@@ -85,37 +90,35 @@
 ):
     fetch = pltpu.make_async_copy(gout_hbm, gout_ref, sem)
     fetch.start()
-    ny = near_ref.shape[0]
-    span = near_ref.shape[1] * near_ref.shape[2]
-    width = near_ref.shape[3]
+    nx, ny, part, width = near_ref.shape
+    span = nx * part
     cut = width - LANES
     half = hidden_ref.shape[0] // 2
     pick = picks((span, span), near_order(rows, nz))
     sums = jnp.zeros((gain_ref.shape[0], cut), jnp.float32)
     for y in range(ny):
-        block = near_ref[y].reshape(span, width)
+        block = jnp.concatenate([near_ref[x, y] for x in range(nx)], axis=0)
         natural = dot(pick, block).astype(jnp.bfloat16)
         w_ref[y * span : (y + 1) * span, :] = natural
         sums = sums + dot(gain_ref[:, y * span : (y + 1) * span], natural[:, :cut])
+    proj = dot(hidden_ref[...], w_ref[:, :cut])
     for h in range(2):
-        at = slice(h * half, (h + 1) * half)
         partial_ref[h, half:, :cut] = sums[:8]
         partial_ref[h, half:, cut:] = jnp.zeros((8, LANES), jnp.float32)
-        partial_ref[h, :half, :cut] = dot(hidden_ref[at, :], w_ref[:, :cut])
+        partial_ref[h, :half, :cut] = proj[h * half : (h + 1) * half]
     fetch.wait()
+    att = dot(gout_ref[...], w_ref[:, cut:])
     for h in range(2):
-        at = slice(h * half, (h + 1) * half)
-        partial_ref[h, :half, cut:] = dot(gout_ref[at, :], w_ref[:, cut:])
+        partial_ref[h, :half, cut:] = att[h * half : (h + 1) * half]
 
 
 def attend_kernel(
-    rows, nz, both_ref, hidden_ref, gout_hbm, near_hbm, gproj_ref, att_ref, gout_ref, near_ref, sem
+    rows, nz, both_ref, hidden_ref, gout_hbm, near_ref, gproj_ref, att_ref, gout_ref, sem
 ):
-    ny = near_ref.shape[0]
-    fetch = pltpu.make_async_copy(gout_hbm, gout_ref, sem.at[ny])
+    fetch = pltpu.make_async_copy(gout_hbm, gout_ref, sem)
     fetch.start()
-    width = near_ref.shape[3]
-    span = near_ref.shape[1] * near_ref.shape[2]
+    nx, ny, part, width = near_ref.shape
+    span = nx * part
     head = LANES
     scale = 1.0 / head**0.5
     for image in range(both_ref.shape[0] // PATCHES):
@@ -140,19 +143,16 @@
     pick = (row == near_order(rows, nz)(column)).astype(jnp.float32).astype(jnp.bfloat16)
     cut = width - head
     fetch.wait()
-    stores = []
     for y in range(ny):
         at = slice(y * span, (y + 1) * span)
         qkv_t = dot(gproj_ref[...], hidden_ref[:, at], tn_dims).astype(jnp.bfloat16)
         out_t = dot(att_ref[...], gout_ref[:, at], tn_dims).astype(jnp.bfloat16)
         sent = dot(pick, qkv_t, nt_dims).astype(jnp.bfloat16)
-        near_ref[y, :, :, :cut] = sent.reshape(2, span // 2, cut)
+        for x in range(nx):
+            near_ref[x, y, :, :cut] = sent[x * part : (x + 1) * part]
         sent = dot(pick, out_t, nt_dims).astype(jnp.bfloat16)
-        near_ref[y, :, :, cut:] = sent.reshape(2, span // 2, head)
-        stores.append(pltpu.make_async_copy(near_ref.at[y], near_hbm.at[y], sem.at[y]))
-        stores[y].start()
-    for store in stores:
-        store.wait()
+        for x in range(nx):
+            near_ref[x, y, :, cut:] = sent[x * part : (x + 1) * part]
 
 
 def fold_kernel(rows, near_ref, o_ref):
@@ -190,7 +190,15 @@
             at = slice(b * LANES, (b + 1) * LANES)
             grad_ref[:, at] = part
             products = products + part * qkv_ref[:, at].astype(jnp.float32)
-    gg_ref[...] = jnp.sum(products, axis=1, keepdims=True) / gain_ref[...]
+    ones = jnp.ones((8, LANES), jnp.float32)
+    totals = lax.dot_general(
+        ones,
+        products,
+        nt_dims,
+        precision=lax.Precision.HIGHEST,
+        preferred_element_type=jnp.float32,
+    )
+    gg_ref[...] = totals[:1] / gain_ref[...]
 
 
 def call(kernel, out_shape, flops, moved, **more):
@@ -217,9 +225,24 @@
     width = cut + head
     blocks = width // LANES
 
-    packed = call(pack_kernel, array((nz, blocks * rows, LANES)), 1_000_000, 200_000)(
-        qkv_weight, out_weight.T
-    )
+    in_hbm = pl.BlockSpec(memory_space=pltpu.HBM)
+    in_vmem = pl.BlockSpec(memory_space=pltpu.VMEM)
+
+    def keep(x):
+        return pltpu.with_memory_space_constraint(x, pltpu.HBM)
+
+    packed = call(
+        pack_kernel,
+        array((nz, blocks * rows, LANES)),
+        1_000_000,
+        200_000,
+        in_specs=[in_hbm, in_hbm],
+        scratch_shapes=[
+            pltpu.VMEM((rows, cut), jnp.bfloat16),
+            pltpu.VMEM((rows, head), jnp.bfloat16),
+            pltpu.SemaphoreType.DMA((2,)),
+        ],
+    )(keep(qkv_weight), keep(out_weight.T))
     along_z = lax.all_to_all(packed, "z", 0, 0).reshape(nz * blocks * rows, LANES)
 
     tok_float = tokens.astype(jnp.float32)
@@ -227,26 +250,30 @@
         jnp.stack([jnp.sum(tok_float, axis=1), jnp.sum(tok_float * tok_float, axis=1)]), SEC
     )
 
-    spread, norms = call(
-        functools.partial(spread_kernel, rows, model_width),
-        (array((ny * nx, nz * rows, width)), array((2, tok_rows), jnp.float32)),
-        300_000_000,
-        2_000_000,
-    )(along_z, stats)
-    near = lax.all_to_all(spread, NEAR, 0, 0)
-
-    row_mean, inv_std = norms[0], norms[1]
+    row_mean = stats[0] / model_width
+    inv_std = lax.rsqrt(stats[1] / model_width - row_mean * row_mean + EPS)
     normed = (tok_float - row_mean[:, None]) * inv_std[:, None]
     hidden = (normed * gain[None, :]).astype(jnp.bfloat16)
-
     gain_high = gain.astype(jnp.bfloat16)
     gain_low = (gain - gain_high.astype(jnp.float32)).astype(jnp.bfloat16)
     gains = jnp.concatenate(
         [gain_high[None], gain_low[None], jnp.zeros((14, local_width), jnp.bfloat16)], axis=0
     )
-    grad_out_hbm = pltpu.with_memory_space_constraint(grad_out, pltpu.HBM)
-    in_hbm = pl.BlockSpec(memory_space=pltpu.HBM)
-    in_vmem = pl.BlockSpec(memory_space=pltpu.VMEM)
+    own = lax.axis_index(FSDP) * rows
+    own_gain = lax.dynamic_slice(gain, (own,), (rows,)).reshape(1, rows)
+
+    along_z, hidden, gains, own_gain = lax.optimization_barrier(
+        (along_z, hidden, gains, own_gain)
+    )
+    spread = call(
+        functools.partial(spread_kernel, rows),
+        array((nx * ny, nz * rows, width)),
+        300_000_000,
+        2_000_000,
+    )(along_z)
+    near = lax.all_to_all(spread, NEAR, 0, 0)
+
+    grad_out_hbm = keep(grad_out)
     half_rows = tok_rows // 2
     weights, partial = call(
         functools.partial(project_kernel, rows, nz),
@@ -258,7 +285,7 @@
             pltpu.VMEM((tok_rows, local_width), jnp.bfloat16),
             pltpu.SemaphoreType.DMA,
         ],
-    )(near.reshape(ny, nx, nz * rows, width), hidden, grad_out_hbm, gains)
+    )(near.reshape(nx, ny, nz * rows, width), hidden, grad_out_hbm, gains)
 
     half = lax.all_to_all(partial, "core", 0, 0)
     half = half[0] + half[1]
@@ -266,22 +293,22 @@
     weight_sums = half[half_rows, :cut] + half[half_rows + 1, :cut]
     both = lax.all_gather(half[:half_rows].astype(jnp.bfloat16), "core", axis=0, tiled=True)
 
+    both, weight_sums = lax.optimization_barrier((both, weight_sums))
     sent, grad_proj = call(
         functools.partial(attend_kernel, rows, nz),
-        (pltpu.HBM((ny, nx, nz * rows, width), jnp.bfloat16), array((tok_rows, cut))),
+        (array((nx, ny, nz * rows, width)), array((tok_rows, cut))),
         1_800_000_000,
         6_000_000,
         in_specs=[in_vmem, in_vmem, in_hbm],
-        out_specs=(in_hbm, in_vmem),
         scratch_shapes=[
             pltpu.VMEM((tok_rows, head), jnp.bfloat16),
             pltpu.VMEM((tok_rows, local_width), jnp.bfloat16),
-            pltpu.VMEM((ny, nx, nz * rows, width), jnp.bfloat16),
-            pltpu.SemaphoreType.DMA((ny + 1,)),
+            pltpu.SemaphoreType.DMA,
         ],
     )(both, hidden, grad_out_hbm)
 
-    received = lax.all_to_all(sent.reshape(ny * nx, nz * rows, width), NEAR, 0, 0)
+    received = lax.all_to_all(sent.reshape(nx * ny, nz * rows, width), NEAR, 0, 0)
+    received, grad_proj = lax.optimization_barrier((received, grad_proj))
     folded = call(
         functools.partial(fold_kernel, rows),
         array((nz * blocks * rows, LANES)),
@@ -289,14 +316,12 @@
         2_000_000,
     )(received)
     folded = lax.all_to_all(folded.reshape(nz, blocks * rows, LANES), "z", 0, 0)
-    own = lax.axis_index(FSDP) * rows
-    own_gain = lax.dynamic_slice(gain, (own,), (rows,)).reshape(rows, 1)
     grad_qkv, grad_outw_t, grad_gain = call(
         finish_kernel,
         (
             array((rows, cut), jnp.float32),
             array((rows, head), jnp.float32),
-            array((rows, 1), jnp.float32),
+            array((1, rows), jnp.float32),
         ),
         10_000_000,
         300_000,

time: 150 us -> 144 us (0.960)
  blocking collectives: 13.1 us -> 67.9 us
  waiting for transfers between devices: 75.4 us -> 28.7 us
  starting transfers between devices: 34.5 us -> 24.5 us
  Pallas kernels: 13.9 us -> 12.1 us
    all_to_all x0 -> x2, blocking collectives: none -> 54.8 us  [the longest x1 29 us: on_device(): near = lax.all_to_all(spread, NEAR, 0, 0)]
    all_to_all x2 -> x0, waiting for transfers between devices: 43.4 us -> none  [the longest x1 23.2 us: on_device(): lax.all_to_all(sent.reshape(ny * nx, nz * rows, width), NEAR, 0, 0)]
    all_to_all x2 -> x0, starting transfers between devices: 10.6 us -> none  [the longest x1 7.05 us: on_device(): near = lax.all_to_all(spread, NEAR, 0, 0)]
    all_to_all x1, waiting for transfers between devices: 7.51 us -> 5.13 us  [on_device(): lax.all_to_all(packed, 'z', 0, 0).reshape(nz * blocks * rows, LANES)]
  transfers between devices with their start and end apart: 5 -> 3, of which waited for: 5 -> 3; matrix products, arithmetic and copies ran while one was open for 6% -> 6% of each run, Pallas kernels for 0% -> 0%
where the time goes in v4:
time: 144 us; the launch traced here: 143 us
  blocking collectives  67.9 us (47%)
  waiting for transfers between devices  28.7 us (20%)
  starting transfers between devices  24.5 us (17%)
  Pallas kernels  12.1 us (8%)
  matrix products  4.42 us (3%)
  other arithmetic  3.95 us (3%)
    all_to_all x1, blocking collectives, on_device(): near = lax.all_to_all(spread, NEAR, 0, 0)  29 us
    all_to_all x1, blocking collectives, on_device(): lax.all_to_all(sent.reshape(nx * ny, nz * rows, width), NEAR, 0, 0)  25.8 us
    all_to_all x1, starting transfers between devices, on_device(): lax.all_to_all(packed, 'z', 0, 0).reshape(nz * blocks * rows, LANES)  15.2 us
    ppermute x1, waiting for transfers between devices, on_device(): half = half + lax.ppermute(half, 'xlo', [(0, 1), (1, 0)])  13.7 us
    all_to_all x1, waiting for transfers between devices, on_device(): folded = lax.all_to_all(folded.reshape(nz, blocks * rows, LANES), 'z', 0, 0)  9.84 us
    all_to_all x1, starting transfers between devices, on_device(): folded = lax.all_to_all(folded.reshape(nz, blocks * rows, LANES), 'z', 0, 0)  6.78 us
    psum x1, blocking collectives, on_device(): lax.psum(jnp.stack([jnp.sum(tok_float, axis=1), jnp.sum(tok_float * tok_f...  6.33 us
    all_to_all x1, waiting for transfers between devices, on_device(): lax.all_to_all(packed, 'z', 0, 0).reshape(nz * blocks * rows, LANES)  5.13 us
  transfers between devices with their start and end apart: 3, of which 3 were waited for; matrix products, arithmetic and copies ran while one was open for 6% of the time, Pallas kernels for 0%

profile of v4, /device:TPU:32, one launch (start us, length us, event | category | flops | bytes accessed | tf_op | source)
XLA Modules:
  0.0 143.3 jit_solution(6896580907659078367)
XLA Ops:
  0.7 1.7 %shard_map.84 = bf16[16,48,128]{2,1,0:T(8,128)(2,1)} custom-call(bf16[12,384]{1,0:T(8,128)(2,1)} %qkv_ref.1, bf16[12,128]{1,0:T(8,128)(2,1)} %bitcast.27), custom_call_target="tpu_custom_call" | custom-call | flops 1000000 | bytes 200000 | tf_op jit(solution)/shard_map/pallas_call | solution.py:234
  2.3 15.2 %all-to-all-start = ((bf16[16,48,128]{2,1,0:T(8,128)(2,1)}), bf16[16,48,128]{2,1,0:T(8,128)(2,1)S(1)}, u32[]{:S(2)}, u32[]{:S(2)}) async-start(bf16[16,48,128]{2,1,0:T(8,128)(2,1)} %shard_map.84), calls=%async_computation | async-start | bytes 393216 | tf_op jit(solution)/shard_map/all_to_all | solution.py:246
  17.6 0.8 subtract_convert_fusion
  18.3 0.8 dynamic-slice_bitcast_fusion.gain_ref
  19.1 2.0 %convert_reduce_fusion = (f32[512]{0:T(512)S(1)}, f32[512]{0:T(512)S(1)}) fusion(bf16[512,1536]{1,0:T(8,128)(2,1)} %param.5), kind=kLoop, calls=%fused_computation.2 | loop fusion | flops 3144704 | bytes 1576960 | tf_op jit(solution)/shard_map/reduce_sum | solution.py:250
  21.1 6.3 %psum.7 = f32[2,512]{1,0:T(2,128)S(1)} all-reduce(f32[2,512]{1,0:T(2,128)S(1)} %pad_maximum_fusion), channel_id=1, replica_groups=mesh['xlo'=2,'core'=2,'y'=4,'z'=16,'xhi'=2] {'xlo','core'}, use_global_device_ids=true, to_apply=%region_2.0 | all-reduce | flops 1024 | bytes 8192 | tf_op jit(solution)/shard_map/psum | solution.py:249
  27.7 0.5 fusion.8.hidden_ref
  28.2 5.1 %all-to-all-done = bf16[16,48,128]{2,1,0:T(8,128)(2,1)S(1)} async-done(((bf16[16,48,128]{2,1,0:T(8,128)(2,1)}), bf16[16,48,128]{2,1,0:T(8,128)(2,1)S(1)}, u32[]{:S(2)}, u32[]{:S(2)}) %all-to-all-start) | async-done | bytes 196640 | tf_op jit(solution)/shard_map/all_to_all | solution.py:246
  33.4 0.6 shard_map.85
  34.0 29.0 %all_to_all.25 = bf16[8,192,512]{2,1,0:T(8,128)(2,1)S(1)} all-to-all(bf16[8,192,512]{2,1,0:T(8,128)(2,1)S(1)} %shard_map.85), channel_id=1, replica_groups=mesh['xlo'=2,'core'=2,'y'=4,'z'=16,'xhi'=2] {'xhi','y'}, dimensions={0} | all-to-all | bytes 3145728 | tf_op jit(solution)/shard_map/all_to_all | solution.py:274
  63.0 3.4 %shard_map.86 = (bf16[1536,512]{1,0:T(8,128)(2,1)S(1)}, f32[2,264,512]{2,1,0:T(8,128)S(1)}) custom-call(bf16[2,4,192,512]{3,2,1,0:T(8,128)(2,1)S(1)} %bitcast.18, bf16[512,1536]{1,0:T(8,128)(2,1)S(1)} %fusion.8.hidden_ref, bf16[512,1536]{1,0:T(8,128)(2,1)} %gout_hbm.3, bf16[16,1536]{1,0:T(8,128)(2,1)S(1)} %maximum_maximum_fusion.gain_ref), custom_call_target="tpu_custom_call" | custom-call | flops 1500000000 | bytes 8000000 | tf_op jit(solution)/shard_map/pallas_call | solution.py:278
  66.4 4.6 %all_to_all.26 = f32[2,264,512]{2,1,0:T(8,128)S(1)} all-to-all(f32[2,264,512]{2,1,0:T(8,128)S(1)} %get-tuple-element.22), channel_id=1, replica_groups=mesh['xlo'=2,'core'=2,'y'=4,'z'=16,'xhi'=2] {'core'}, dimensions={0} | all-to-all | bytes 2162688 | tf_op jit(solution)/shard_map/all_to_all | solution.py:290
  71.1 2.5 %collective-permute-start = (f32[264,512]{1,0:T(8,128)S(1)}, f32[264,512]{1,0:T(8,128)S(1)}, u32[]{:S(2)}, u32[]{:S(2)}) collective-permute-start(f32[264,512]{1,0:T(8,128)S(1)} %fusion.13), channel_id=1, source_target_pairs={{0,256},{256,0},{1,257},{257,1},{2,258},{258,2},{3,259},{259,3},{4... | collective-permute-start | bytes 1622024 | tf_op jit(solution)/shard_map/ppermute | solution.py:292
  73.6 13.7 %collective-permute-done = f32[264,512]{1,0:T(8,128)S(1)} collective-permute-done((f32[264,512]{1,0:T(8,128)S(1)}, f32[264,512]{1,0:T(8,128)S(1)}, u32[]{:S(2)}, u32[]{:S(2)}) %collective-permute-start) | collective-permute-done | bytes 540704 | tf_op jit(solution)/shard_map/ppermute | solution.py:292
  87.3 0.2 fusion.16
  87.5 2.2 %all_gather.3.both_ref = bf16[512,512]{1,0:T(8,128)(2,1)S(1)} all-gather(bf16[256,512]{1,0:T(8,128)(2,1)S(1)} %slice.58), channel_id=1, replica_groups=mesh['xlo'=2,'core'=2,'y'=4,'z'=16,'xhi'=2] {'core'}, dimensions={0}, use_global_device_ids=true | all-gather | bytes 786432 | tf_op jit(solution)/shard_map/all_gather | solution.py:294
  89.7 4.1 %shard_map.87 = (bf16[2,4,192,512]{3,2,1,0:T(8,128)(2,1)S(1)}, bf16[512,384]{1,0:T(8,128)(2,1)S(1)}) custom-call(bf16[512,512]{1,0:T(8,128)(2,1)S(1)} %all_gather.3.both_ref, bf16[512,1536]{1,0:T(8,128)(2,1)S(1)} %fusion.8.hidden_ref, bf16[512,1536]{1,0:T(8,128)(2,1)} %gout_hbm.3), custom_call_target="tpu_custom_call" | custom-call | flops 1800000000 | bytes 6000000 | tf_op jit(solution)/shard_map/pallas_call | solution.py:297
  93.9 25.8 %all_to_all.27.near_ref = bf16[8,192,512]{2,1,0:T(8,128)(2,1)S(1)} all-to-all(bf16[8,192,512]{2,1,0:T(8,128)(2,1)S(1)} %bitcast.19), channel_id=1, replica_groups=mesh['xlo'=2,'core'=2,'y'=4,'z'=16,'xhi'=2] {'xhi','y'}, dimensions={0} | all-to-all | bytes 3145728 | tf_op jit(solution)/shard_map/all_to_all | solution.py:310
  119.6 1.4 %shard_map.88 = bf16[768,128]{1,0:T(8,128)(2,1)} custom-call(bf16[8,192,512]{2,1,0:T(8,128)(2,1)S(1)} %all_to_all.27.near_ref), custom_call_target="tpu_custom_call" | custom-call | flops 300000000 | bytes 2000000 | tf_op jit(solution)/shard_map/pallas_call | solution.py:312
  121.1 6.8 %all-to-all-start.4 = ((bf16[16,48,128]{2,1,0:T(8,128)(2,1)}), bf16[16,48,128]{2,1,0:T(8,128)(2,1)S(1)}, u32[]{:S(2)}, u32[]{:S(2)}) async-start(bf16[16,48,128]{2,1,0:T(8,128)(2,1)} %bitcast.10), calls=%async_computation.4 | async-start | bytes 393216 | tf_op jit(solution)/shard_map/all_to_all | solution.py:318
  127.9 0.3 fusion.11
  128.2 4.4 %fusion.9 = bf16[512,1536]{1,0:T(8,128)(2,1)} fusion(bf16[512,1536]{1,0:T(8,128)(2,1)} %param.5, bf16[512,384]{1,0:T(8,128)(2,1)S(1)} %get-tuple-element.26, bf16[512,1536]{1,0:T(8,128)(2,1)S(1)} %copy-done.6, f32[512]{0:T(512)S(1)} %get-tuple-element.42, f32[512]{0:T(512)S(1)} %get-tuple-element.43, f32[1536]{0:T(1024)S(1)} %copy-done.3, ...), kind=kOutput, calls=%fused_computation.13 | convolution fusion | flops 612630528 | bytes 6305792 | tf_op jit(solution)/shard_map/dot_general | solution.py:330
  132.6 9.8 %all-to-all-done.4.x_ref = bf16[16,48,128]{2,1,0:T(8,128)(2,1)S(1)} async-done(((bf16[16,48,128]{2,1,0:T(8,128)(2,1)}), bf16[16,48,128]{2,1,0:T(8,128)(2,1)S(1)}, u32[]{:S(2)}, u32[]{:S(2)}) %all-to-all-start.4) | async-done | bytes 196640 | tf_op jit(solution)/shard_map/all_to_all | solution.py:318
  142.4 0.9 shard_map.89
  (26 shorter events, 0.4 us)
Async XLA Ops:
  0.6 27.0 %copy-start.3 = (f32[1536]{0:T(1024)S(1)}, f32[1536]{0:T(1024)}, u32[]{:S(2)}) copy-start(f32[1536]{0:T(1024)} %param.7) | copy-start | bytes 18436
  0.6 27.0 %copy-start.2 = (bf16[512,1536]{1,0:T(8,128)(2,1)S(1)}, bf16[512,1536]{1,0:T(8,128)(2,1)}, u32[]{:S(2)}) copy-start(bf16[512,1536]{1,0:T(8,128)(2,1)} %param.5) | copy-start | bytes 4718596
  2.3 31.0 %all-to-all-start = ((bf16[16,48,128]{2,1,0:T(8,128)(2,1)}), bf16[16,48,128]{2,1,0:T(8,128)(2,1)S(1)}, u32[]{:S(2)}, u32[]{:S(2)}) async-start(bf16[16,48,128]{2,1,0:T(8,128)(2,1)} %shard_map.84), calls=%async_computation | async-start | bytes 393216 | tf_op jit(solution)/shard_map/all_to_all | solution.py:246
  27.7 0.6 copy-start.4
  66.4 4.7 %copy-start.1 = (bf16[1536,512]{1,0:T(8,128)(2,1)}, bf16[1536,512]{1,0:T(8,128)(2,1)S(1)}, u32[]{:S(2)}) copy-start(bf16[1536,512]{1,0:T(8,128)(2,1)S(1)} %get-tuple-element.27) | copy-start | bytes 4718596
  71.1 16.2 %collective-permute-start = (f32[264,512]{1,0:T(8,128)S(1)}, f32[264,512]{1,0:T(8,128)S(1)}, u32[]{:S(2)}, u32[]{:S(2)}) collective-permute-start(f32[264,512]{1,0:T(8,128)S(1)} %fusion.13), channel_id=1, source_target_pairs={{0,256},{256,0},{1,257},{257,1},{2,258},{258,2},{3,259},{259,3},{4... | collective-permute-start | bytes 1622024 | tf_op jit(solution)/shard_map/ppermute | solution.py:292
  119.6 8.5 %copy-start.5 = (f32[512]{0:T(512)S(1)}, f32[512]{0:T(512)}, u32[]{:S(2)}) copy-start(f32[512]{0:T(512)} %copy-done.4) | copy-start | bytes 6148
  119.6 8.5 %copy-start.6 = (bf16[512,1536]{1,0:T(8,128)(2,1)S(1)}, bf16[512,1536]{1,0:T(8,128)(2,1)}, u32[]{:S(2)}) copy-start(bf16[512,1536]{1,0:T(8,128)(2,1)} %gout_hbm.3) | copy-start | bytes 4718596
  121.1 21.4 %all-to-all-start.4 = ((bf16[16,48,128]{2,1,0:T(8,128)(2,1)}), bf16[16,48,128]{2,1,0:T(8,128)(2,1)S(1)}, u32[]{:S(2)}, u32[]{:S(2)}) async-start(bf16[16,48,128]{2,1,0:T(8,128)(2,1)} %bitcast.10), calls=%async_computation.4 | async-start | bytes 393216 | tf_op jit(solution)/shard_map/all_to_all | solution.py:318
  128.2 14.3 %copy-start = (bf16[12,384]{1,0:T(8,128)(2,1)S(1)}, bf16[12,384]{1,0:T(8,128)(2,1)}, u32[]{:S(2)}) copy-start(bf16[12,384]{1,0:T(8,128)(2,1)} %qkv_ref.1) | copy-start | bytes 27652

commit v5 on v4

--- a/solution.py
+++ b/solution.py
@@ -85,38 +85,64 @@
             o_ref[k, :, b * LANES : (b + 1) * LANES] = part
 
 
-def project_kernel(
-    rows, nz, near_ref, hidden_ref, gout_hbm, gain_ref, w_ref, partial_ref, gout_ref, sem
+def prepare_kernel(
+    rows, nz, hidden_ref, gout_hbm, gain_ref, hp_ref, gp_ref, gains_ref, gout_ref, sem
 ):
     fetch = pltpu.make_async_copy(gout_hbm, gout_ref, sem)
     fetch.start()
+    span = 2 * nz * rows
+    pick = picks((span, span), near_order(rows, nz))
+    for y in range(hidden_ref.shape[1] // span):
+        at = slice(y * span, (y + 1) * span)
+        hp_ref[:, at] = dot(hidden_ref[:, at], pick).astype(jnp.bfloat16)
+        gain = gain_ref[:, at]
+        high = gain.astype(jnp.bfloat16).astype(jnp.float32)
+        row = lax.broadcasted_iota(jnp.int32, (16, span), 0)
+        both = jnp.where(row == 0, high, jnp.where(row == 1, gain - high, 0.0))
+        gains_ref[:, at] = dot(both.astype(jnp.bfloat16), pick).astype(jnp.bfloat16)
+    fetch.wait()
+    for y in range(hidden_ref.shape[1] // span):
+        at = slice(y * span, (y + 1) * span)
+        gp_ref[:, at] = dot(gout_ref[:, at], pick).astype(jnp.bfloat16)
+
+
+def project_kernel(near_ref, hidden_ref, gout_ref, gain_ref, partial_ref, w_ref):
     nx, ny, part, width = near_ref.shape
-    span = nx * part
     cut = width - LANES
     half = hidden_ref.shape[0] // 2
-    pick = picks((span, span), near_order(rows, nz))
-    sums = jnp.zeros((gain_ref.shape[0], cut), jnp.float32)
     for y in range(ny):
-        block = jnp.concatenate([near_ref[x, y] for x in range(nx)], axis=0)
-        natural = dot(pick, block).astype(jnp.bfloat16)
-        w_ref[y * span : (y + 1) * span, :] = natural
-        sums = sums + dot(gain_ref[:, y * span : (y + 1) * span], natural[:, :cut])
+        for x in range(nx):
+            at = (y * nx + x) * part
+            w_ref[at : at + part, :] = near_ref[x, y]
+    sums = dot(gain_ref[...], w_ref[:, :cut])
     proj = dot(hidden_ref[...], w_ref[:, :cut])
+    att = dot(gout_ref[...], w_ref[:, cut:])
     for h in range(2):
         partial_ref[h, half:, :cut] = sums[:8]
         partial_ref[h, half:, cut:] = jnp.zeros((8, LANES), jnp.float32)
         partial_ref[h, :half, :cut] = proj[h * half : (h + 1) * half]
-    fetch.wait()
-    att = dot(gout_ref[...], w_ref[:, cut:])
-    for h in range(2):
         partial_ref[h, :half, cut:] = att[h * half : (h + 1) * half]
 
 
-def attend_kernel(
-    rows, nz, both_ref, hidden_ref, gout_hbm, near_ref, gproj_ref, att_ref, gout_ref, sem
-):
-    fetch = pltpu.make_async_copy(gout_hbm, gout_ref, sem)
-    fetch.start()
+def natural_kernel(rows, nz, near_ref, o_ref):
+    nx, ny, part, _ = near_ref.shape
+    span = nx * part
+    cut = o_ref.shape[1]
+    pick = picks((span, span), near_order(rows, nz))
+    for y in range(ny):
+        block = jnp.concatenate([near_ref[x, y, :, :cut] for x in range(nx)], axis=0)
+        o_ref[y * span : (y + 1) * span, :] = dot(pick, block).astype(jnp.bfloat16)
+
+
+def add_kernel(own_ref, other_ref, both_ref, sums_ref):
+    count = both_ref.shape[0]
+    both_ref[...] = (own_ref[:count] + other_ref[:count]).astype(jnp.bfloat16)
+    cut = sums_ref.shape[1]
+    tail = own_ref[count:, :cut] + other_ref[count:, :cut]
+    sums_ref[...] = tail[0:1] + tail[1:2]
+
+
+def attend_kernel(both_ref, hidden_ref, gout_ref, near_ref, gproj_ref, att_ref):
     nx, ny, part, width = near_ref.shape
     span = nx * part
     head = LANES
@@ -138,21 +164,14 @@
         gproj_ref[at, :head] = dot(grad_score, key_in).astype(jnp.bfloat16)
         gproj_ref[at, head : 2 * head] = dot(grad_score, query, tn_dims).astype(jnp.bfloat16)
         gproj_ref[at, 2 * head :] = dot(probs_b, grad_att, tn_dims).astype(jnp.bfloat16)
-    row = lax.broadcasted_iota(jnp.int32, (span, span), 0)
-    column = lax.broadcasted_iota(jnp.int32, (span, span), 1)
-    pick = (row == near_order(rows, nz)(column)).astype(jnp.float32).astype(jnp.bfloat16)
     cut = width - head
-    fetch.wait()
     for y in range(ny):
         at = slice(y * span, (y + 1) * span)
-        qkv_t = dot(gproj_ref[...], hidden_ref[:, at], tn_dims).astype(jnp.bfloat16)
-        out_t = dot(att_ref[...], gout_ref[:, at], tn_dims).astype(jnp.bfloat16)
-        sent = dot(pick, qkv_t, nt_dims).astype(jnp.bfloat16)
+        part_qkv = dot(hidden_ref[:, at], gproj_ref[...], tn_dims).astype(jnp.bfloat16)
+        part_out = dot(gout_ref[:, at], att_ref[...], tn_dims).astype(jnp.bfloat16)
         for x in range(nx):
-            near_ref[x, y, :, :cut] = sent[x * part : (x + 1) * part]
-        sent = dot(pick, out_t, nt_dims).astype(jnp.bfloat16)
-        for x in range(nx):
-            near_ref[x, y, :, cut:] = sent[x * part : (x + 1) * part]
+            near_ref[x, y, :, :cut] = part_qkv[x * part : (x + 1) * part]
+            near_ref[x, y, :, cut:] = part_out[x * part : (x + 1) * part]
 
 
 def fold_kernel(rows, near_ref, o_ref):
@@ -254,16 +273,26 @@
     inv_std = lax.rsqrt(stats[1] / model_width - row_mean * row_mean + EPS)
     normed = (tok_float - row_mean[:, None]) * inv_std[:, None]
     hidden = (normed * gain[None, :]).astype(jnp.bfloat16)
-    gain_high = gain.astype(jnp.bfloat16)
-    gain_low = (gain - gain_high.astype(jnp.float32)).astype(jnp.bfloat16)
-    gains = jnp.concatenate(
-        [gain_high[None], gain_low[None], jnp.zeros((14, local_width), jnp.bfloat16)], axis=0
-    )
+    hidden_p, gout_p, gains_p = call(
+        functools.partial(prepare_kernel, rows, nz),
+        (
+            array((tok_rows, local_width)),
+            array((tok_rows, local_width)),
+            array((16, local_width)),
+        ),
+        1_300_000_000,
+        6_000_000,
+        in_specs=[in_vmem, in_hbm, in_vmem],
+        scratch_shapes=[
+            pltpu.VMEM((tok_rows, local_width), jnp.bfloat16),
+            pltpu.SemaphoreType.DMA,
+        ],
+    )(hidden, keep(grad_out), gain.reshape(1, local_width))
     own = lax.axis_index(FSDP) * rows
     own_gain = lax.dynamic_slice(gain, (own,), (rows,)).reshape(1, rows)
 
-    along_z, hidden, gains, own_gain = lax.optimization_barrier(
-        (along_z, hidden, gains, own_gain)
+    along_z, hidden_p, gout_p, gains_p, own_gain = lax.optimization_barrier(
+        (along_z, hidden_p, gout_p, gains_p, own_gain)
     )
     spread = call(
         functools.partial(spread_kernel, rows),
@@ -273,42 +302,48 @@
     )(along_z)
     near = lax.all_to_all(spread, NEAR, 0, 0)
 
-    grad_out_hbm = keep(grad_out)
+    near = near.reshape(nx, ny, nz * rows, width)
     half_rows = tok_rows // 2
-    weights, partial = call(
-        functools.partial(project_kernel, rows, nz),
-        (array((local_width, width)), array((2, half_rows + 8, width), jnp.float32)),
-        1_500_000_000,
-        8_000_000,
-        in_specs=[in_vmem, in_vmem, in_hbm, in_vmem],
-        scratch_shapes=[
-            pltpu.VMEM((tok_rows, local_width), jnp.bfloat16),
-            pltpu.SemaphoreType.DMA,
-        ],
-    )(near.reshape(nx, ny, nz * rows, width), hidden, grad_out_hbm, gains)
-
+    partial = call(
+        project_kernel,
+        array((2, half_rows + 8, width), jnp.float32),
+        900_000_000,
+        6_000_000,
+        scratch_shapes=[pltpu.VMEM((local_width, width), jnp.bfloat16)],
+    )(near, hidden_p, gout_p, gains_p)
+
+    near, partial = lax.optimization_barrier((near, partial))
     half = lax.all_to_all(partial, "core", 0, 0)
     half = half[0] + half[1]
-    half = half + lax.ppermute(half, "xlo", [(0, 1), (1, 0)])
-    weight_sums = half[half_rows, :cut] + half[half_rows + 1, :cut]
-    both = lax.all_gather(half[:half_rows].astype(jnp.bfloat16), "core", axis=0, tiled=True)
-
-    both, weight_sums = lax.optimization_barrier((both, weight_sums))
+    near, half = lax.optimization_barrier((near, half))
+    other = lax.ppermute(half, "xlo", [(0, 1), (1, 0)])
+    weights = call(
+        functools.partial(natural_kernel, rows, nz),
+        array((local_width, cut)),
+        460_000_000,
+        3_000_000,
+    )(near)
+    half, weight_sums = call(
+        add_kernel,
+        (array((half_rows, width)), array((1, cut), jnp.float32)),
+        300_000,
+        1_400_000,
+    )(half, other)
+    both = lax.all_gather(half, "core", axis=0, tiled=True)
+
+    both, weights = lax.optimization_barrier((both, weights))
     sent, grad_proj = call(
-        functools.partial(attend_kernel, rows, nz),
+        attend_kernel,
         (array((nx, ny, nz * rows, width)), array((tok_rows, cut))),
-        1_800_000_000,
+        1_300_000_000,
         6_000_000,
-        in_specs=[in_vmem, in_vmem, in_hbm],
-        scratch_shapes=[
-            pltpu.VMEM((tok_rows, head), jnp.bfloat16),
-            pltpu.VMEM((tok_rows, local_width), jnp.bfloat16),
-            pltpu.SemaphoreType.DMA,
-        ],
-    )(both, hidden, grad_out_hbm)
+        scratch_shapes=[pltpu.VMEM((tok_rows, head), jnp.bfloat16)],
+    )(both, hidden_p, gout_p)
 
     received = lax.all_to_all(sent.reshape(nx * ny, nz * rows, width), NEAR, 0, 0)
-    received, grad_proj = lax.optimization_barrier((received, grad_proj))
+    received, grad_proj, weight_sums = lax.optimization_barrier(
+        (received, grad_proj, weight_sums)
+    )
     folded = call(
         functools.partial(fold_kernel, rows),
         array((nz * blocks * rows, LANES)),
@@ -328,10 +363,10 @@
     )(folded, qkv_weight, own_gain)
 
     grad_hidden = lax.dot_general(
-        grad_proj, weights[:, :cut], nt_dims, preferred_element_type=jnp.float32
+        grad_proj, weights, nt_dims, preferred_element_type=jnp.float32
     )
     proj_grad = grad_proj.astype(jnp.float32)
-    first = jnp.sum(proj_grad * weight_sums[None, :], axis=1) / model_width
+    first = jnp.sum(proj_grad * weight_sums, axis=1) / model_width
     second = jnp.sum(proj_grad * both[:, :cut].astype(jnp.float32), axis=1) / model_width
     grad_normed = grad_hidden * gain[None, :]
     grad_tokens = grad_out.astype(jnp.float32) + inv_std[:, None] * (

time: 144 us -> 143 us (level)
  waiting for transfers between devices: 28.7 us -> 25.6 us
  starting transfers between devices: 24.5 us -> 26.5 us
    all_to_all x1, waiting for transfers between devices: 5.13 us -> 3.13 us  [on_device(): lax.all_to_all(packed, 'z', 0, 0).reshape(nz * blocks * rows, LANES)]
    all_to_all x1, starting transfers between devices: 6.78 us -> 8.78 us  [on_device(): folded = lax.all_to_all(folded.reshape(nz, blocks * rows, LANES), 'z', 0, 0)]
    pallas_call x2 -> x5, Pallas kernels: 7.59 us -> 7.9 us  [the longest x1 2.85 us: on_device(): call(attend_kernel, (array((nx, ny, nz * rows, width)), array((tok_rows,...]
  transfers between devices with their start and end apart: 3 -> 3, of which waited for: 3 -> 3; matrix products, arithmetic and copies ran while one was open for 6% -> 5% of each run, Pallas kernels for 0% -> 2%
where the time goes in v5:
time: 143 us; the launch traced here: 142 us
  blocking collectives  68 us (48%)
  starting transfers between devices  26.5 us (19%)
  waiting for transfers between devices  25.6 us (18%)
  Pallas kernels  12.4 us (9%)
  matrix products  4.53 us (3%)
  other arithmetic  2.94 us (2%)
    all_to_all x1, blocking collectives, on_device(): near = lax.all_to_all(spread, NEAR, 0, 0)  29.1 us
    all_to_all x1, blocking collectives, on_device(): lax.all_to_all(sent.reshape(nx * ny, nz * rows, width), NEAR, 0, 0)  25.8 us
    all_to_all x1, starting transfers between devices, on_device(): lax.all_to_all(packed, 'z', 0, 0).reshape(nz * blocks * rows, LANES)  15.2 us
    ppermute x1, waiting for transfers between devices, on_device(): other = lax.ppermute(half, 'xlo', [(0, 1), (1, 0)])  12.8 us
    all_to_all x1, waiting for transfers between devices, on_device(): folded = lax.all_to_all(folded.reshape(nz, blocks * rows, LANES), 'z', 0, 0)  9.72 us
    all_to_all x1, starting transfers between devices, on_device(): folded = lax.all_to_all(folded.reshape(nz, blocks * rows, LANES), 'z', 0, 0)  8.78 us
    psum x1, blocking collectives, on_device(): lax.psum(jnp.stack([jnp.sum(tok_float, axis=1), jnp.sum(tok_float * tok_f...  6.33 us
    all_to_all x1, blocking collectives, on_device(): half = lax.all_to_all(partial, 'core', 0, 0)  4.58 us
  transfers between devices with their start and end apart: 3, of which 3 were waited for; matrix products, arithmetic and copies ran while one was open for 5% of the time, Pallas kernels for 2%

profile of v5, /device:TPU:32, one launch (start us, length us, event | category | flops | bytes accessed | tf_op | source)
XLA Modules:
  0.0 142.1 jit_solution(8894792471597055884)
XLA Ops:
  0.7 1.7 %shard_map.84 = bf16[16,48,128]{2,1,0:T(8,128)(2,1)} custom-call(bf16[12,384]{1,0:T(8,128)(2,1)} %qkv_ref.1, bf16[12,128]{1,0:T(8,128)(2,1)} %bitcast.27), custom_call_target="tpu_custom_call" | custom-call | flops 1000000 | bytes 200000 | tf_op jit(solution)/shard_map/pallas_call | solution.py:253
  2.3 15.2 %all-to-all-start = ((bf16[16,48,128]{2,1,0:T(8,128)(2,1)}), bf16[16,48,128]{2,1,0:T(8,128)(2,1)S(1)}, u32[]{:S(2)}, u32[]{:S(2)}) async-start(bf16[16,48,128]{2,1,0:T(8,128)(2,1)} %shard_map.84), calls=%async_computation | async-start | bytes 393216 | tf_op jit(solution)/shard_map/all_to_all | solution.py:265
  17.6 2.0 %convert_reduce_fusion = (f32[512]{0:T(512)S(1)}, f32[512]{0:T(512)S(1)}) fusion(bf16[512,1536]{1,0:T(8,128)(2,1)} %param.5), kind=kLoop, calls=%fused_computation.2 | loop fusion | flops 3144704 | bytes 1576960 | tf_op jit(solution)/shard_map/reduce_sum | solution.py:269
  19.6 6.3 %psum.7 = f32[2,512]{1,0:T(2,128)S(1)} all-reduce(f32[2,512]{1,0:T(2,128)S(1)} %pad_maximum_fusion), channel_id=1, replica_groups=mesh['xlo'=2,'core'=2,'y'=4,'z'=16,'xhi'=2] {'xlo','core'}, use_global_device_ids=true, to_apply=%region_2.0 | all-reduce | flops 1024 | bytes 8192 | tf_op jit(solution)/shard_map/psum | solution.py:268
  26.0 0.5 fusion.8.hidden_ref
  26.6 2.5 %shard_map.85 = (bf16[512,1536]{1,0:T(8,128)(2,1)S(1)}, bf16[512,1536]{1,0:T(8,128)(2,1)S(1)}, bf16[16,1536]{1,0:T(8,128)(2,1)S(1)}) custom-call(bf16[512,1536]{1,0:T(8,128)(2,1)S(1)} %fusion.8.hidden_ref, bf16[512,1536]{1,0:T(8,128)(2,1)} %gout_hbm.1, f32[1,1536]{1,0:T(1,128)S(1)} %broadcast_in_dim.2.gain_ref), custom_call_target="tpu_custom_call" | custom-call | flops 1300000000 | bytes 6000000 | tf_op jit(solution)/shard_map/pallas_call | solution.py:276
  29.1 1.1 copy-done
  30.2 3.1 %all-to-all-done = bf16[16,48,128]{2,1,0:T(8,128)(2,1)S(1)} async-done(((bf16[16,48,128]{2,1,0:T(8,128)(2,1)}), bf16[16,48,128]{2,1,0:T(8,128)(2,1)S(1)}, u32[]{:S(2)}, u32[]{:S(2)}) %all-to-all-start) | async-done | bytes 196640 | tf_op jit(solution)/shard_map/all_to_all | solution.py:265
  33.4 0.6 shard_map.86
  34.0 29.1 %all_to_all.25 = bf16[8,192,512]{2,1,0:T(8,128)(2,1)S(1)} all-to-all(bf16[8,192,512]{2,1,0:T(8,128)(2,1)S(1)} %shard_map.86), channel_id=1, replica_groups=mesh['xlo'=2,'core'=2,'y'=4,'z'=16,'xhi'=2] {'xhi','y'}, dimensions={0} | all-to-all | bytes 3145728 | tf_op jit(solution)/shard_map/all_to_all | solution.py:303
  63.1 1.6 %shard_map.87 = f32[2,264,512]{2,1,0:T(8,128)S(1)} custom-call(bf16[2,4,192,512]{3,2,1,0:T(8,128)(2,1)S(1)} %bitcast.17, bf16[512,1536]{1,0:T(8,128)(2,1)S(1)} %get-tuple-element.32.hidden_ref, bf16[512,1536]{1,0:T(8,128)(2,1)S(1)} %copy-done.1, bf16[16,1536]{1,0:T(8,128)(2,1)S(1)} %get-tuple-element.34.gain_ref), custom_call_target="tpu_custom_call" | custom-call | flops 900000000 | bytes 6000000 | tf_op jit(solution)/shard_map/pallas_call | solution.py:307
  64.7 4.6 %all_to_all.26 = f32[2,264,512]{2,1,0:T(8,128)S(1)} all-to-all(f32[2,264,512]{2,1,0:T(8,128)S(1)} %shard_map.87), channel_id=1, replica_groups=mesh['xlo'=2,'core'=2,'y'=4,'z'=16,'xhi'=2] {'core'}, dimensions={0} | all-to-all | bytes 2162688 | tf_op jit(solution)/shard_map/all_to_all | solution.py:316
  69.3 2.5 %collective-permute-start = (f32[264,512]{1,0:T(8,128)S(1)}, f32[264,512]{1,0:T(8,128)S(1)}, u32[]{:S(2)}, u32[]{:S(2)}) collective-permute-start(f32[264,512]{1,0:T(8,128)S(1)} %fusion.12.own_ref), channel_id=1, source_target_pairs={{0,256},{256,0},{1,257},{257,1},{2,258},{258,2},{3,259},{259,3},{4... | collective-permute-start | bytes 1622024 | tf_op jit(solution)/shard_map/ppermute | solution.py:319
  71.8 0.9 shard_map.89
  72.7 12.8 %collective-permute-done.other_ref = f32[264,512]{1,0:T(8,128)S(1)} collective-permute-done((f32[264,512]{1,0:T(8,128)S(1)}, f32[264,512]{1,0:T(8,128)S(1)}, u32[]{:S(2)}, u32[]{:S(2)}) %collective-permute-start) | collective-permute-done | bytes 540704 | tf_op jit(solution)/shard_map/ppermute | solution.py:319
  85.6 2.2 %all_gather.3.both_ref = bf16[512,512]{1,0:T(8,128)(2,1)S(1)} all-gather(bf16[256,512]{1,0:T(8,128)(2,1)S(1)} %get-tuple-element.38), channel_id=1, replica_groups=mesh['xlo'=2,'core'=2,'y'=4,'z'=16,'xhi'=2] {'core'}, dimensions={0}, use_global_device_ids=true | all-gather | bytes 786432 | tf_op jit(solution)/shard_map/all_gather | solution.py:332
  87.8 2.8 %shard_map.90 = (bf16[2,4,192,512]{3,2,1,0:T(8,128)(2,1)S(1)}, bf16[512,384]{1,0:T(8,128)(2,1)S(1)}) custom-call(bf16[512,512]{1,0:T(8,128)(2,1)S(1)} %all_gather.3.both_ref, bf16[512,1536]{1,0:T(8,128)(2,1)S(1)} %get-tuple-element.32.hidden_ref, bf16[512,1536]{1,0:T(8,128)(2,1)S(1)} %copy-done.1), custom_call_target="tpu_custom_call" | custom-call | flops 1300000000 | bytes 6000000 | tf_op jit(solution)/shard_map/pallas_call | solution.py:335
  90.6 25.8 %all_to_all.27.near_ref = bf16[8,192,512]{2,1,0:T(8,128)(2,1)S(1)} all-to-all(bf16[8,192,512]{2,1,0:T(8,128)(2,1)S(1)} %bitcast.19), channel_id=1, replica_groups=mesh['xlo'=2,'core'=2,'y'=4,'z'=16,'xhi'=2] {'xhi','y'}, dimensions={0} | all-to-all | bytes 3145728 | tf_op jit(solution)/shard_map/all_to_all | solution.py:343
  116.4 1.4 shard_map.91
  117.8 8.8 %all-to-all-start.4 = ((bf16[16,48,128]{2,1,0:T(8,128)(2,1)}), bf16[16,48,128]{2,1,0:T(8,128)(2,1)S(1)}, u32[]{:S(2)}, u32[]{:S(2)}) async-start(bf16[16,48,128]{2,1,0:T(8,128)(2,1)} %bitcast.10), calls=%async_computation.4 | async-start | bytes 393216 | tf_op jit(solution)/shard_map/all_to_all | solution.py:353
  126.6 0.3 fusion.10
  126.9 4.5 %fusion.9 = bf16[512,1536]{1,0:T(8,128)(2,1)} fusion(bf16[512,1536]{1,0:T(8,128)(2,1)} %param.5, bf16[512,384]{1,0:T(8,128)(2,1)S(1)} %copy-done.3, bf16[1536,384]{1,0:T(8,128)(2,1)S(1)} %shard_map.89, bf16[512,1536]{1,0:T(8,128)(2,1)} %gout_hbm.1, f32[512]{0:T(512)S(1)} %get-tuple-element.58, f32[512]{0:T(512)S(1)} %get-tuple-element.59, ...), kind=kOutput, calls=%fused_computation.13 | convolution fusion | flops 612630528 | bytes 6305792 | tf_op jit(solution)/shard_map/dot_general | solution.py:365
  131.5 9.7 %all-to-all-done.4.x_ref = bf16[16,48,128]{2,1,0:T(8,128)(2,1)S(1)} async-done(((bf16[16,48,128]{2,1,0:T(8,128)(2,1)}), bf16[16,48,128]{2,1,0:T(8,128)(2,1)S(1)}, u32[]{:S(2)}, u32[]{:S(2)}) %all-to-all-start.4) | async-done | bytes 196640 | tf_op jit(solution)/shard_map/all_to_all | solution.py:353
  141.2 0.9 shard_map.92
  (22 shorter events, 0.3 us)
Async XLA Ops:
  0.6 25.4 %copy-start.5 = (bf16[512,1536]{1,0:T(8,128)(2,1)S(1)}, bf16[512,1536]{1,0:T(8,128)(2,1)}, u32[]{:S(2)}) copy-start(bf16[512,1536]{1,0:T(8,128)(2,1)} %param.5) | copy-start | bytes 4718596
  0.6 25.2 %copy-start.6 = (f32[1536]{0:T(1024)S(1)}, f32[1536]{0:T(1024)}, u32[]{:S(2)}) copy-start(f32[1536]{0:T(1024)} %param.7) | copy-start | bytes 18436
  2.3 31.0 %all-to-all-start = ((bf16[16,48,128]{2,1,0:T(8,128)(2,1)}), bf16[16,48,128]{2,1,0:T(8,128)(2,1)S(1)}, u32[]{:S(2)}, u32[]{:S(2)}) async-start(bf16[16,48,128]{2,1,0:T(8,128)(2,1)} %shard_map.84), calls=%async_computation | async-start | bytes 393216 | tf_op jit(solution)/shard_map/all_to_all | solution.py:265
  29.1 1.1 copy-start
  33.9 29.1 %copy-start.1 = (bf16[512,1536]{1,0:T(8,128)(2,1)S(1)}, bf16[512,1536]{1,0:T(8,128)(2,1)}, u32[]{:S(2)}) copy-start(bf16[512,1536]{1,0:T(8,128)(2,1)} %copy-done) | copy-start | bytes 4718596
  69.3 16.2 %collective-permute-start = (f32[264,512]{1,0:T(8,128)S(1)}, f32[264,512]{1,0:T(8,128)S(1)}, u32[]{:S(2)}, u32[]{:S(2)}) collective-permute-start(f32[264,512]{1,0:T(8,128)S(1)} %fusion.12.own_ref), channel_id=1, source_target_pairs={{0,256},{256,0},{1,257},{257,1},{2,258},{258,2},{3,259},{259,3},{4... | collective-permute-start | bytes 1622024 | tf_op jit(solution)/shard_map/ppermute | solution.py:319
  90.6 25.8 %copy-start.2 = (bf16[512,384]{1,0:T(8,128)(2,1)}, bf16[512,384]{1,0:T(8,128)(2,1)S(1)}, u32[]{:S(2)}) copy-start(bf16[512,384]{1,0:T(8,128)(2,1)S(1)} %get-tuple-element.44) | copy-start | bytes 1179652
  116.4 10.2 %copy-start.3 = (bf16[512,384]{1,0:T(8,128)(2,1)S(1)}, bf16[512,384]{1,0:T(8,128)(2,1)}, u32[]{:S(2)}) copy-start(bf16[512,384]{1,0:T(8,128)(2,1)} %copy-done.2) | copy-start | bytes 1179652
  117.8 23.4 %all-to-all-start.4 = ((bf16[16,48,128]{2,1,0:T(8,128)(2,1)}), bf16[16,48,128]{2,1,0:T(8,128)(2,1)S(1)}, u32[]{:S(2)}, u32[]{:S(2)}) async-start(bf16[16,48,128]{2,1,0:T(8,128)(2,1)} %bitcast.10), calls=%async_computation.4 | async-start | bytes 393216 | tf_op jit(solution)/shard_map/all_to_all | solution.py:353
  126.9 14.3 %copy-start.4 = (bf16[12,384]{1,0:T(8,128)(2,1)S(1)}, bf16[12,384]{1,0:T(8,128)(2,1)}, u32[]{:S(2)}) copy-start(bf16[12,384]{1,0:T(8,128)(2,1)} %qkv_ref.1) | copy-start | bytes 27652

commit v6 on v5

--- a/solution.py
+++ b/solution.py
@@ -15,7 +15,8 @@
 
 SEC = ("xlo", "core")
 FSDP = ("y", "z", "xhi")
-NEAR = ("xhi", "y")
+NEAR = ("core", "y", "xhi")
+FAR = ("core", "z")
 LANES = 128
 VMEM_LIMIT = 28 * 1024 * 1024
 
@@ -37,8 +38,31 @@
     return (column == source_of_row(row)).astype(jnp.float32).astype(jnp.bfloat16)
 
 
-def unpack_block(rows, blocks, column_block):
-    return lambda i: i + by_rows(i, rows) * (rows * (blocks - 1)) + column_block * rows
+def mirrored(index, count):
+    return index + lax.axis_index("core") * (count - 1 - 2 * index)
+
+
+def near_all_to_all(x):
+    ny, nx = lax.axis_size("y"), lax.axis_size("xhi")
+    groups = [
+        [(c * ny + (y if c == 0 else ny - 1 - y)) * nx + h for h in range(nx) for y in range(ny)]
+        for c in range(2)
+    ]
+    return lax.all_to_all(x, NEAR, 0, 0, axis_index_groups=groups)
+
+
+def far_all_to_all(x):
+    nz = lax.axis_size("z")
+    groups = [list(range(nz)), list(range(2 * nz - 1, nz - 1, -1))]
+    return lax.all_to_all(x, FAR, 0, 0, axis_index_groups=groups)
+
+
+def unpack_block(rows, blocks, column_block, nz):
+    def source(i):
+        z = by_rows(i, rows)
+        return mirrored(z, nz) * (rows * blocks) + column_block * rows + i - z * rows
+
+    return source
 
 
 def near_order(rows, nz):
@@ -79,7 +103,7 @@
     blocks = width // LANES
     x = x_ref[...]
     for b in range(blocks):
-        pick = picks((span, x.shape[0]), unpack_block(rows, blocks, b))
+        pick = picks((span, x.shape[0]), unpack_block(rows, blocks, b, span // rows))
         part = dot(pick, x).astype(jnp.bfloat16)
         for k in range(copies):
             o_ref[k, :, b * LANES : (b + 1) * LANES] = part
@@ -113,7 +137,7 @@
     for y in range(ny):
         for x in range(nx):
             at = (y * nx + x) * part
-            w_ref[at : at + part, :] = near_ref[x, y]
+            w_ref[at : at + part, :] = near_ref[x, mirrored(y, ny)]
     sums = dot(gain_ref[...], w_ref[:, :cut])
     proj = dot(hidden_ref[...], w_ref[:, :cut])
     att = dot(gout_ref[...], w_ref[:, cut:])
@@ -130,7 +154,7 @@
     cut = o_ref.shape[1]
     pick = picks((span, span), near_order(rows, nz))
     for y in range(ny):
-        block = jnp.concatenate([near_ref[x, y, :, :cut] for x in range(nx)], axis=0)
+        block = jnp.concatenate([near_ref[x, mirrored(y, ny), :, :cut] for x in range(nx)], axis=0)
         o_ref[y * span : (y + 1) * span, :] = dot(pick, block).astype(jnp.bfloat16)
 
 
@@ -170,8 +194,9 @@
         part_qkv = dot(hidden_ref[:, at], gproj_ref[...], tn_dims).astype(jnp.bfloat16)
         part_out = dot(gout_ref[:, at], att_ref[...], tn_dims).astype(jnp.bfloat16)
         for x in range(nx):
-            near_ref[x, y, :, :cut] = part_qkv[x * part : (x + 1) * part]
-            near_ref[x, y, :, cut:] = part_out[x * part : (x + 1) * part]
+            listed = mirrored(y, ny)
+            near_ref[x, listed, :, :cut] = part_qkv[x * part : (x + 1) * part]
+            near_ref[x, listed, :, cut:] = part_out[x * part : (x + 1) * part]
 
 
 def fold_kernel(rows, near_ref, o_ref):
@@ -185,7 +210,7 @@
     column = lax.broadcasted_iota(jnp.int32, (o_ref.shape[0], span), 1)
     packed = jnp.zeros(o_ref.shape, jnp.float32)
     for b in range(blocks):
-        pick = row == unpack_block(rows, blocks, b)(column)
+        pick = row == unpack_block(rows, blocks, b, span // rows)(column)
         pick = pick.astype(jnp.float32).astype(jnp.bfloat16)
         packed = packed + dot(pick, total[:, b * LANES : (b + 1) * LANES])
     o_ref[...] = packed.astype(jnp.bfloat16)
@@ -262,7 +287,7 @@
             pltpu.SemaphoreType.DMA((2,)),
         ],
     )(keep(qkv_weight), keep(out_weight.T))
-    along_z = lax.all_to_all(packed, "z", 0, 0).reshape(nz * blocks * rows, LANES)
+    along_z = far_all_to_all(packed).reshape(nz * blocks * rows, LANES)
 
     tok_float = tokens.astype(jnp.float32)
     stats = lax.psum(
@@ -300,7 +325,7 @@
         300_000_000,
         2_000_000,
     )(along_z)
-    near = lax.all_to_all(spread, NEAR, 0, 0)
+    near = near_all_to_all(spread)
 
     near = near.reshape(nx, ny, nz * rows, width)
     half_rows = tok_rows // 2
@@ -340,7 +365,7 @@
         scratch_shapes=[pltpu.VMEM((tok_rows, head), jnp.bfloat16)],
     )(both, hidden_p, gout_p)
 
-    received = lax.all_to_all(sent.reshape(nx * ny, nz * rows, width), NEAR, 0, 0)
+    received = near_all_to_all(sent.reshape(nx * ny, nz * rows, width))
     received, grad_proj, weight_sums = lax.optimization_barrier(
         (received, grad_proj, weight_sums)
     )
@@ -350,7 +375,7 @@
         300_000_000,
         2_000_000,
     )(received)
-    folded = lax.all_to_all(folded.reshape(nz, blocks * rows, LANES), "z", 0, 0)
+    folded = far_all_to_all(folded.reshape(nz, blocks * rows, LANES))
     grad_qkv, grad_outw_t, grad_gain = call(
         finish_kernel,
         (

time: 143 us -> 141 us (0.986)
  the two profiles are of different devices: /device:TPU:32 before, /device:TPU:1 now
where the time goes in v6:
time: 141 us
  blocking collectives  66.9 us (47%)
  starting transfers between devices  27.8 us (20%)
  waiting for transfers between devices  24 us (17%)
  Pallas kernels  12.4 us (9%)
  matrix products  4.54 us (3%)
  other arithmetic  2.94 us (2%)
    all_to_all x2, blocking collectives, near_all_to_all(): return lax.all_to_all(x, NEAR, 0, 0, axis_index_groups=groups)  51.3 us
    all_to_all x2, starting transfers between devices, far_all_to_all(): return lax.all_to_all(x, FAR, 0, 0, axis_index_groups=groups)  25.5 us
    ppermute x1, waiting for transfers between devices, on_device(): other = lax.ppermute(half, 'xlo', [(0, 1), (1, 0)])  12.2 us
    all_to_all x2, waiting for transfers between devices, far_all_to_all(): return lax.all_to_all(x, FAR, 0, 0, axis_index_groups=groups)  11.7 us
    all_to_all x1, blocking collectives, on_device(): half = lax.all_to_all(partial, 'core', 0, 0)  6.79 us
    psum x1, blocking collectives, on_device(): lax.psum(jnp.stack([jnp.sum(tok_float, axis=1), jnp.sum(tok_float * tok_f...  5.8 us
    dot_general x1, matrix products, on_device(): lax.dot_general(grad_proj, weights, nt_dims, preferred_element_type=jnp.f...  4.54 us
    all_gather x1, blocking collectives, on_device(): both = lax.all_gather(half, 'core', axis=0, tiled=True)  3.01 us
  transfers between devices with their start and end apart: 3, of which 3 were waited for; matrix products, arithmetic and copies ran while one was open for 5% of the time, Pallas kernels for 2%

profile of v6, /device:TPU:1, one launch (start us, length us, event | category | flops | bytes accessed | tf_op | source)
XLA Modules:
  0.0 140.6 jit_solution(5560625321159377859)
XLA Ops:
  0.7 1.7 %shard_map.84 = bf16[16,48,128]{2,1,0:T(8,128)(2,1)} custom-call(bf16[12,384]{1,0:T(8,128)(2,1)} %qkv_ref.1, bf16[12,128]{1,0:T(8,128)(2,1)} %bitcast.27), custom_call_target="tpu_custom_call" | custom-call | flops 1000000 | bytes 200000 | tf_op jit(solution)/shard_map/pallas_call | solution.py:278
  2.3 16.0 %all-to-all-start = ((bf16[16,48,128]{2,1,0:T(8,128)(2,1)}), bf16[16,48,128]{2,1,0:T(8,128)(2,1)S(1)}, u32[]{:S(2)}, u32[]{:S(2)}) async-start(bf16[16,48,128]{2,1,0:T(8,128)(2,1)} %shard_map.84), calls=%async_computation | async-start | bytes 393216 | tf_op jit(solution)/shard_map/all_to_all | solution.py:57
  18.3 2.0 %convert_reduce_fusion = (f32[512]{0:T(512)S(1)}, f32[512]{0:T(512)S(1)}) fusion(bf16[512,1536]{1,0:T(8,128)(2,1)} %param.5), kind=kLoop, calls=%fused_computation.2 | loop fusion | flops 3144704 | bytes 1576960 | tf_op jit(solution)/shard_map/reduce_sum | solution.py:294
  20.3 5.8 %psum.7 = f32[2,512]{1,0:T(2,128)S(1)} all-reduce(f32[2,512]{1,0:T(2,128)S(1)} %pad_maximum_fusion), channel_id=1, replica_groups=mesh['xlo'=2,'core'=2,'y'=4,'z'=16,'xhi'=2] {'xlo','core'}, use_global_device_ids=true, to_apply=%region_2.0 | all-reduce | flops 1024 | bytes 8192 | tf_op jit(solution)/shard_map/psum | solution.py:293
  26.2 0.5 fusion.8.hidden_ref
  26.8 2.5 %shard_map.85 = (bf16[512,1536]{1,0:T(8,128)(2,1)S(1)}, bf16[512,1536]{1,0:T(8,128)(2,1)S(1)}, bf16[16,1536]{1,0:T(8,128)(2,1)S(1)}) custom-call(bf16[512,1536]{1,0:T(8,128)(2,1)S(1)} %fusion.8.hidden_ref, bf16[512,1536]{1,0:T(8,128)(2,1)} %gout_hbm.1, f32[1,1536]{1,0:T(1,128)S(1)} %broadcast_in_dim.2.gain_ref), custom_call_target="tpu_custom_call" | custom-call | flops 1300000000 | bytes 6000000 | tf_op jit(solution)/shard_map/pallas_call | solution.py:301
  29.3 1.1 copy-done
  30.4 2.4 %all-to-all-done = bf16[16,48,128]{2,1,0:T(8,128)(2,1)S(1)} async-done(((bf16[16,48,128]{2,1,0:T(8,128)(2,1)}), bf16[16,48,128]{2,1,0:T(8,128)(2,1)S(1)}, u32[]{:S(2)}, u32[]{:S(2)}) %all-to-all-start) | async-done | bytes 196640 | tf_op jit(solution)/shard_map/all_to_all | solution.py:57
  32.8 0.6 shard_map.86
  33.4 26.4 %all_to_all.25 = bf16[8,192,512]{2,1,0:T(8,128)(2,1)S(1)} all-to-all(bf16[8,192,512]{2,1,0:T(8,128)(2,1)S(1)} %shard_map.86), channel_id=1, replica_groups={{0,32,64,96,1,33,65,97},{224,192,160,128,225,193,161,129},{2,34,66,98,3..., dimensions={0} | all-to-all | bytes 3145728 | tf_op jit(solution)/shard_map/all_to_all | solution.py:51
  59.8 1.6 %shard_map.87 = f32[2,264,512]{2,1,0:T(8,128)S(1)} custom-call(bf16[2,4,192,512]{3,2,1,0:T(8,128)(2,1)S(1)} %bitcast.17, bf16[512,1536]{1,0:T(8,128)(2,1)S(1)} %get-tuple-element.32.hidden_ref, bf16[512,1536]{1,0:T(8,128)(2,1)S(1)} %copy-done.1, bf16[16,1536]{1,0:T(8,128)(2,1)S(1)} %get-tuple-element.34.gain_ref), custom_call_target="tpu_custom_call" | custom-call | flops 900000000 | bytes 6000000 | tf_op jit(solution)/shard_map/pallas_call | solution.py:332
  61.4 6.8 %all_to_all.26 = f32[2,264,512]{2,1,0:T(8,128)S(1)} all-to-all(f32[2,264,512]{2,1,0:T(8,128)S(1)} %shard_map.87), channel_id=1, replica_groups=mesh['xlo'=2,'core'=2,'y'=4,'z'=16,'xhi'=2] {'core'}, dimensions={0} | all-to-all | bytes 2162688 | tf_op jit(solution)/shard_map/all_to_all | solution.py:341
  68.2 2.2 %collective-permute-start = (f32[264,512]{1,0:T(8,128)S(1)}, f32[264,512]{1,0:T(8,128)S(1)}, u32[]{:S(2)}, u32[]{:S(2)}) collective-permute-start(f32[264,512]{1,0:T(8,128)S(1)} %fusion.12.own_ref), channel_id=1, source_target_pairs={{0,256},{256,0},{1,257},{257,1},{2,258},{258,2},{3,259},{259,3},{4... | collective-permute-start | bytes 1622024 | tf_op jit(solution)/shard_map/ppermute | solution.py:344
  70.5 0.9 shard_map.89
  71.4 12.2 %collective-permute-done.other_ref = f32[264,512]{1,0:T(8,128)S(1)} collective-permute-done((f32[264,512]{1,0:T(8,128)S(1)}, f32[264,512]{1,0:T(8,128)S(1)}, u32[]{:S(2)}, u32[]{:S(2)}) %collective-permute-start) | collective-permute-done | bytes 540704 | tf_op jit(solution)/shard_map/ppermute | solution.py:344
  83.7 3.0 %all_gather.3.both_ref = bf16[512,512]{1,0:T(8,128)(2,1)S(1)} all-gather(bf16[256,512]{1,0:T(8,128)(2,1)S(1)} %get-tuple-element.38), channel_id=1, replica_groups=mesh['xlo'=2,'core'=2,'y'=4,'z'=16,'xhi'=2] {'core'}, dimensions={0}, use_global_device_ids=true | all-gather | bytes 786432 | tf_op jit(solution)/shard_map/all_gather | solution.py:357
  86.7 2.8 %shard_map.90 = (bf16[2,4,192,512]{3,2,1,0:T(8,128)(2,1)S(1)}, bf16[512,384]{1,0:T(8,128)(2,1)S(1)}) custom-call(bf16[512,512]{1,0:T(8,128)(2,1)S(1)} %all_gather.3.both_ref, bf16[512,1536]{1,0:T(8,128)(2,1)S(1)} %get-tuple-element.32.hidden_ref, bf16[512,1536]{1,0:T(8,128)(2,1)S(1)} %copy-done.1), custom_call_target="tpu_custom_call" | custom-call | flops 1300000000 | bytes 6000000 | tf_op jit(solution)/shard_map/pallas_call | solution.py:360
  89.5 25.0 %all_to_all.27.near_ref = bf16[8,192,512]{2,1,0:T(8,128)(2,1)S(1)} all-to-all(bf16[8,192,512]{2,1,0:T(8,128)(2,1)S(1)} %bitcast.19), channel_id=1, replica_groups={{0,32,64,96,1,33,65,97},{224,192,160,128,225,193,161,129},{2,34,66,98,3..., dimensions={0} | all-to-all | bytes 3145728 | tf_op jit(solution)/shard_map/all_to_all | solution.py:51
  114.5 1.4 shard_map.91
  115.9 9.6 %all-to-all-start.4 = ((bf16[16,48,128]{2,1,0:T(8,128)(2,1)}), bf16[16,48,128]{2,1,0:T(8,128)(2,1)S(1)}, u32[]{:S(2)}, u32[]{:S(2)}) async-start(bf16[16,48,128]{2,1,0:T(8,128)(2,1)} %bitcast.10), calls=%async_computation.4 | async-start | bytes 393216 | tf_op jit(solution)/shard_map/all_to_all | solution.py:57
  125.5 0.3 fusion.10
  125.8 4.5 %fusion.9 = bf16[512,1536]{1,0:T(8,128)(2,1)} fusion(bf16[512,1536]{1,0:T(8,128)(2,1)} %param.5, bf16[512,384]{1,0:T(8,128)(2,1)S(1)} %copy-done.3, bf16[1536,384]{1,0:T(8,128)(2,1)S(1)} %shard_map.89, bf16[512,1536]{1,0:T(8,128)(2,1)} %gout_hbm.1, f32[512]{0:T(512)S(1)} %get-tuple-element.58, f32[512]{0:T(512)S(1)} %get-tuple-element.59, ...), kind=kOutput, calls=%fused_computation.13 | convolution fusion | flops 612630528 | bytes 6305792 | tf_op jit(solution)/shard_map/dot_general | solution.py:390
  130.4 9.4 %all-to-all-done.4.x_ref = bf16[16,48,128]{2,1,0:T(8,128)(2,1)S(1)} async-done(((bf16[16,48,128]{2,1,0:T(8,128)(2,1)}), bf16[16,48,128]{2,1,0:T(8,128)(2,1)S(1)}, u32[]{:S(2)}, u32[]{:S(2)}) %all-to-all-start.4) | async-done | bytes 196640 | tf_op jit(solution)/shard_map/all_to_all | solution.py:57
  139.8 0.9 shard_map.92
  (22 shorter events, 0.3 us)
Async XLA Ops:
  0.6 25.6 %copy-start.5 = (bf16[512,1536]{1,0:T(8,128)(2,1)S(1)}, bf16[512,1536]{1,0:T(8,128)(2,1)}, u32[]{:S(2)}) copy-start(bf16[512,1536]{1,0:T(8,128)(2,1)} %param.5) | copy-start | bytes 4718596
  0.6 25.5 %copy-start.6 = (f32[1536]{0:T(1024)S(1)}, f32[1536]{0:T(1024)}, u32[]{:S(2)}) copy-start(f32[1536]{0:T(1024)} %param.7) | copy-start | bytes 18436
  2.3 30.5 %all-to-all-start = ((bf16[16,48,128]{2,1,0:T(8,128)(2,1)}), bf16[16,48,128]{2,1,0:T(8,128)(2,1)S(1)}, u32[]{:S(2)}, u32[]{:S(2)}) async-start(bf16[16,48,128]{2,1,0:T(8,128)(2,1)} %shard_map.84), calls=%async_computation | async-start | bytes 393216 | tf_op jit(solution)/shard_map/all_to_all | solution.py:57
  29.3 1.1 copy-start
  33.4 26.4 %copy-start.1 = (bf16[512,1536]{1,0:T(8,128)(2,1)S(1)}, bf16[512,1536]{1,0:T(8,128)(2,1)}, u32[]{:S(2)}) copy-start(bf16[512,1536]{1,0:T(8,128)(2,1)} %copy-done) | copy-start | bytes 4718596
  68.2 15.4 %collective-permute-start = (f32[264,512]{1,0:T(8,128)S(1)}, f32[264,512]{1,0:T(8,128)S(1)}, u32[]{:S(2)}, u32[]{:S(2)}) collective-permute-start(f32[264,512]{1,0:T(8,128)S(1)} %fusion.12.own_ref), channel_id=1, source_target_pairs={{0,256},{256,0},{1,257},{257,1},{2,258},{258,2},{3,259},{259,3},{4... | collective-permute-start | bytes 1622024 | tf_op jit(solution)/shard_map/ppermute | solution.py:344
  89.5 25.0 %copy-start.2 = (bf16[512,384]{1,0:T(8,128)(2,1)}, bf16[512,384]{1,0:T(8,128)(2,1)S(1)}, u32[]{:S(2)}) copy-start(bf16[512,384]{1,0:T(8,128)(2,1)S(1)} %get-tuple-element.44) | copy-start | bytes 1179652
  114.5 11.0 %copy-start.3 = (bf16[512,384]{1,0:T(8,128)(2,1)S(1)}, bf16[512,384]{1,0:T(8,128)(2,1)}, u32[]{:S(2)}) copy-start(bf16[512,384]{1,0:T(8,128)(2,1)} %copy-done.2) | copy-start | bytes 1179652
  115.9 23.8 %all-to-all-start.4 = ((bf16[16,48,128]{2,1,0:T(8,128)(2,1)}), bf16[16,48,128]{2,1,0:T(8,128)(2,1)S(1)}, u32[]{:S(2)}, u32[]{:S(2)}) async-start(bf16[16,48,128]{2,1,0:T(8,128)(2,1)} %bitcast.10), calls=%async_computation.4 | async-start | bytes 393216 | tf_op jit(solution)/shard_map/all_to_all | solution.py:57
  125.8 13.9 %copy-start.4 = (bf16[12,384]{1,0:T(8,128)(2,1)S(1)}, bf16[12,384]{1,0:T(8,128)(2,1)}, u32[]{:S(2)}) copy-start(bf16[12,384]{1,0:T(8,128)(2,1)} %qkv_ref.1) | copy-start | bytes 27652

commit v7 on v6

--- a/solution.py
+++ b/solution.py
@@ -110,9 +110,9 @@
 
 
 def prepare_kernel(
-    rows, nz, hidden_ref, gout_hbm, gain_ref, hp_ref, gp_ref, gains_ref, gout_ref, sem
+    rows, nz, hidden_ref, gout_hbm, gain_ref, hp_hbm, gp_ref, gains_ref, gout_ref, hp_ref, sem
 ):
-    fetch = pltpu.make_async_copy(gout_hbm, gout_ref, sem)
+    fetch = pltpu.make_async_copy(gout_hbm, gout_ref, sem.at[0])
     fetch.start()
     span = 2 * nz * rows
     pick = picks((span, span), near_order(rows, nz))
@@ -124,10 +124,13 @@
         row = lax.broadcasted_iota(jnp.int32, (16, span), 0)
         both = jnp.where(row == 0, high, jnp.where(row == 1, gain - high, 0.0))
         gains_ref[:, at] = dot(both.astype(jnp.bfloat16), pick).astype(jnp.bfloat16)
+    store = pltpu.make_async_copy(hp_ref, hp_hbm, sem.at[1])
+    store.start()
     fetch.wait()
     for y in range(hidden_ref.shape[1] // span):
         at = slice(y * span, (y + 1) * span)
         gp_ref[:, at] = dot(gout_ref[:, at], pick).astype(jnp.bfloat16)
+    store.wait()
 
 
 def project_kernel(near_ref, hidden_ref, gout_ref, gain_ref, partial_ref, w_ref):
@@ -301,16 +304,18 @@
     hidden_p, gout_p, gains_p = call(
         functools.partial(prepare_kernel, rows, nz),
         (
-            array((tok_rows, local_width)),
+            pltpu.HBM((tok_rows, local_width), jnp.bfloat16),
             array((tok_rows, local_width)),
             array((16, local_width)),
         ),
         1_300_000_000,
         6_000_000,
         in_specs=[in_vmem, in_hbm, in_vmem],
+        out_specs=(in_hbm, in_vmem, in_vmem),
         scratch_shapes=[
             pltpu.VMEM((tok_rows, local_width), jnp.bfloat16),
-            pltpu.SemaphoreType.DMA,
+            pltpu.VMEM((tok_rows, local_width), jnp.bfloat16),
+            pltpu.SemaphoreType.DMA((2,)),
         ],
     )(hidden, keep(grad_out), gain.reshape(1, local_width))
     own = lax.axis_index(FSDP) * rows

time: 141 us -> 142 us (level)
  Pallas kernels: 12.4 us -> 14.2 us
    pallas_call x1, Pallas kernels: 2.54 us -> 4.31 us  [on_device(): call(functools.partial(prepare_kernel, rows, nz), (pltpu.HBM((tok_rows, l...]
  transfers between devices with their start and end apart: 3 -> 3, of which waited for: 3 -> 3; matrix products, arithmetic and copies ran while one was open for 5% -> 5% of each run, Pallas kernels for 2% -> 4%
where the time goes in v7:
time: 142 us; the launch traced here: 141 us
  blocking collectives  67 us (47%)
  starting transfers between devices  28.4 us (20%)
  waiting for transfers between devices  23.4 us (16%)
  Pallas kernels  14.2 us (10%)
  matrix products  4.53 us (3%)
  other arithmetic  2.94 us (2%)
    all_to_all x2, blocking collectives, near_all_to_all(): return lax.all_to_all(x, NEAR, 0, 0, axis_index_groups=groups)  51.4 us
    all_to_all x2, starting transfers between devices, far_all_to_all(): return lax.all_to_all(x, FAR, 0, 0, axis_index_groups=groups)  26.1 us
    ppermute x1, waiting for transfers between devices, on_device(): other = lax.ppermute(half, 'xlo', [(0, 1), (1, 0)])  12.2 us
    all_to_all x2, waiting for transfers between devices, far_all_to_all(): return lax.all_to_all(x, FAR, 0, 0, axis_index_groups=groups)  11.1 us
    all_to_all x1, blocking collectives, on_device(): half = lax.all_to_all(partial, 'core', 0, 0)  6.79 us
    psum x1, blocking collectives, on_device(): lax.psum(jnp.stack([jnp.sum(tok_float, axis=1), jnp.sum(tok_float * tok_f...  5.8 us
    dot_general x1, matrix products, on_device(): lax.dot_general(grad_proj, weights, nt_dims, preferred_element_type=jnp.f...  4.53 us
    pallas_call x1, Pallas kernels, on_device(): call(functools.partial(prepare_kernel, rows, nz), (pltpu.HBM((tok_rows, l...  4.31 us
  transfers between devices with their start and end apart: 3, of which 3 were waited for; matrix products, arithmetic and copies ran while one was open for 5% of the time, Pallas kernels for 4%

profile of v7, /device:TPU:1, one launch (start us, length us, event | category | flops | bytes accessed | tf_op | source)
XLA Modules:
  0.0 141.2 jit_solution(14113424122985291822)
XLA Ops:
  0.7 1.7 %shard_map.84 = bf16[16,48,128]{2,1,0:T(8,128)(2,1)} custom-call(bf16[12,384]{1,0:T(8,128)(2,1)} %qkv_ref.1, bf16[12,128]{1,0:T(8,128)(2,1)} %bitcast.27), custom_call_target="tpu_custom_call" | custom-call | flops 1000000 | bytes 200000 | tf_op jit(solution)/shard_map/pallas_call | solution.py:281
  2.3 16.0 %all-to-all-start = ((bf16[16,48,128]{2,1,0:T(8,128)(2,1)}), bf16[16,48,128]{2,1,0:T(8,128)(2,1)S(1)}, u32[]{:S(2)}, u32[]{:S(2)}) async-start(bf16[16,48,128]{2,1,0:T(8,128)(2,1)} %shard_map.84), calls=%async_computation | async-start | bytes 393216 | tf_op jit(solution)/shard_map/all_to_all | solution.py:57
  18.3 2.0 %convert_reduce_fusion = (f32[512]{0:T(512)S(1)}, f32[512]{0:T(512)S(1)}) fusion(bf16[512,1536]{1,0:T(8,128)(2,1)} %param.5), kind=kLoop, calls=%fused_computation.2 | loop fusion | flops 3144704 | bytes 1576960 | tf_op jit(solution)/shard_map/reduce_sum | solution.py:297
  20.3 5.8 %psum.7 = f32[2,512]{1,0:T(2,128)S(1)} all-reduce(f32[2,512]{1,0:T(2,128)S(1)} %pad_maximum_fusion), channel_id=1, replica_groups=mesh['xlo'=2,'core'=2,'y'=4,'z'=16,'xhi'=2] {'xlo','core'}, use_global_device_ids=true, to_apply=%region_2.0 | all-reduce | flops 1024 | bytes 8192 | tf_op jit(solution)/shard_map/psum | solution.py:296
  26.1 0.1 dynamic-slice_bitcast_fusion.gain_ref
  26.2 0.5 fusion.8.hidden_ref
  26.8 4.3 %shard_map.85 = (bf16[512,1536]{1,0:T(8,128)(2,1)}, bf16[512,1536]{1,0:T(8,128)(2,1)S(1)}, bf16[16,1536]{1,0:T(8,128)(2,1)S(1)}) custom-call(bf16[512,1536]{1,0:T(8,128)(2,1)S(1)} %fusion.8.hidden_ref, bf16[512,1536]{1,0:T(8,128)(2,1)} %gout_hbm.1, f32[1,1536]{1,0:T(1,128)S(1)} %broadcast_in_dim.2.gain_ref), custom_call_target="tpu_custom_call" | custom-call | flops 1300000000 | bytes 6000000 | tf_op jit(solution)/shard_map/pallas_call | solution.py:304
  31.1 1.7 %all-to-all-done = bf16[16,48,128]{2,1,0:T(8,128)(2,1)S(1)} async-done(((bf16[16,48,128]{2,1,0:T(8,128)(2,1)}), bf16[16,48,128]{2,1,0:T(8,128)(2,1)S(1)}, u32[]{:S(2)}, u32[]{:S(2)}) %all-to-all-start) | async-done | bytes 196640 | tf_op jit(solution)/shard_map/all_to_all | solution.py:57
  32.8 0.6 shard_map.86
  33.4 26.3 %all_to_all.25 = bf16[8,192,512]{2,1,0:T(8,128)(2,1)S(1)} all-to-all(bf16[8,192,512]{2,1,0:T(8,128)(2,1)S(1)} %shard_map.86), channel_id=1, replica_groups={{0,32,64,96,1,33,65,97},{224,192,160,128,225,193,161,129},{2,34,66,98,3..., dimensions={0} | all-to-all | bytes 3145728 | tf_op jit(solution)/shard_map/all_to_all | solution.py:51
  59.8 1.6 %shard_map.87 = f32[2,264,512]{2,1,0:T(8,128)S(1)} custom-call(bf16[2,4,192,512]{3,2,1,0:T(8,128)(2,1)S(1)} %bitcast.17, bf16[512,1536]{1,0:T(8,128)(2,1)S(1)} %copy-done, bf16[512,1536]{1,0:T(8,128)(2,1)S(1)} %get-tuple-element.33.gout_ref, bf16[16,1536]{1,0:T(8,128)(2,1)S(1)} %get-tuple-element.34.gain_ref), custom_call_target="tpu_custom_call" | custom-call | flops 900000000 | bytes 6000000 | tf_op jit(solution)/shard_map/pallas_call | solution.py:337
  61.4 6.8 %all_to_all.26 = f32[2,264,512]{2,1,0:T(8,128)S(1)} all-to-all(f32[2,264,512]{2,1,0:T(8,128)S(1)} %shard_map.87), channel_id=1, replica_groups=mesh['xlo'=2,'core'=2,'y'=4,'z'=16,'xhi'=2] {'core'}, dimensions={0} | all-to-all | bytes 2162688 | tf_op jit(solution)/shard_map/all_to_all | solution.py:346
  68.2 2.2 %collective-permute-start = (f32[264,512]{1,0:T(8,128)S(1)}, f32[264,512]{1,0:T(8,128)S(1)}, u32[]{:S(2)}, u32[]{:S(2)}) collective-permute-start(f32[264,512]{1,0:T(8,128)S(1)} %fusion.12.own_ref), channel_id=1, source_target_pairs={{0,256},{256,0},{1,257},{257,1},{2,258},{258,2},{3,259},{259,3},{4... | collective-permute-start | bytes 1622024 | tf_op jit(solution)/shard_map/ppermute | solution.py:349
  70.5 0.9 shard_map.89
  71.4 12.2 %collective-permute-done.other_ref = f32[264,512]{1,0:T(8,128)S(1)} collective-permute-done((f32[264,512]{1,0:T(8,128)S(1)}, f32[264,512]{1,0:T(8,128)S(1)}, u32[]{:S(2)}, u32[]{:S(2)}) %collective-permute-start) | collective-permute-done | bytes 540704 | tf_op jit(solution)/shard_map/ppermute | solution.py:349
  83.7 3.0 %all_gather.3.both_ref = bf16[512,512]{1,0:T(8,128)(2,1)S(1)} all-gather(bf16[256,512]{1,0:T(8,128)(2,1)S(1)} %get-tuple-element.38), channel_id=1, replica_groups=mesh['xlo'=2,'core'=2,'y'=4,'z'=16,'xhi'=2] {'core'}, dimensions={0}, use_global_device_ids=true | all-gather | bytes 786432 | tf_op jit(solution)/shard_map/all_gather | solution.py:362
  86.7 2.8 %shard_map.90 = (bf16[2,4,192,512]{3,2,1,0:T(8,128)(2,1)S(1)}, bf16[512,384]{1,0:T(8,128)(2,1)S(1)}) custom-call(bf16[512,512]{1,0:T(8,128)(2,1)S(1)} %all_gather.3.both_ref, bf16[512,1536]{1,0:T(8,128)(2,1)S(1)} %copy-done, bf16[512,1536]{1,0:T(8,128)(2,1)S(1)} %get-tuple-element.33.gout_ref), custom_call_target="tpu_custom_call" | custom-call | flops 1300000000 | bytes 6000000 | tf_op jit(solution)/shard_map/pallas_call | solution.py:365
  89.5 25.0 %all_to_all.27.near_ref = bf16[8,192,512]{2,1,0:T(8,128)(2,1)S(1)} all-to-all(bf16[8,192,512]{2,1,0:T(8,128)(2,1)S(1)} %bitcast.19), channel_id=1, replica_groups={{0,32,64,96,1,33,65,97},{224,192,160,128,225,193,161,129},{2,34,66,98,3..., dimensions={0} | all-to-all | bytes 3145728 | tf_op jit(solution)/shard_map/all_to_all | solution.py:51
  114.5 1.4 shard_map.91
  115.9 10.2 %all-to-all-start.4 = ((bf16[16,48,128]{2,1,0:T(8,128)(2,1)}), bf16[16,48,128]{2,1,0:T(8,128)(2,1)S(1)}, u32[]{:S(2)}, u32[]{:S(2)}) async-start(bf16[16,48,128]{2,1,0:T(8,128)(2,1)} %bitcast.10), calls=%async_computation.4 | async-start | bytes 393216 | tf_op jit(solution)/shard_map/all_to_all | solution.py:57
  126.1 0.3 fusion.10
  126.4 4.5 %fusion.9 = bf16[512,1536]{1,0:T(8,128)(2,1)} fusion(bf16[512,1536]{1,0:T(8,128)(2,1)} %param.5, bf16[512,384]{1,0:T(8,128)(2,1)S(1)} %copy-done.2, bf16[1536,384]{1,0:T(8,128)(2,1)S(1)} %shard_map.89, bf16[512,1536]{1,0:T(8,128)(2,1)} %gout_hbm.1, f32[512]{0:T(512)S(1)} %get-tuple-element.58, f32[512]{0:T(512)S(1)} %get-tuple-element.59, ...), kind=kOutput, calls=%fused_computation.13 | convolution fusion | flops 612630528 | bytes 6305792 | tf_op jit(solution)/shard_map/dot_general | solution.py:395
  131.0 9.4 %all-to-all-done.4.x_ref = bf16[16,48,128]{2,1,0:T(8,128)(2,1)S(1)} async-done(((bf16[16,48,128]{2,1,0:T(8,128)(2,1)}), bf16[16,48,128]{2,1,0:T(8,128)(2,1)S(1)}, u32[]{:S(2)}, u32[]{:S(2)}) %all-to-all-start.4) | async-done | bytes 196640 | tf_op jit(solution)/shard_map/all_to_all | solution.py:57
  140.4 0.9 shard_map.92
  (20 shorter events, 0.2 us)
Async XLA Ops:
  0.6 25.6 %copy-start.4 = (bf16[512,1536]{1,0:T(8,128)(2,1)S(1)}, bf16[512,1536]{1,0:T(8,128)(2,1)}, u32[]{:S(2)}) copy-start(bf16[512,1536]{1,0:T(8,128)(2,1)} %param.5) | copy-start | bytes 4718596
  0.6 25.5 %copy-start.5 = (f32[1536]{0:T(1024)S(1)}, f32[1536]{0:T(1024)}, u32[]{:S(2)}) copy-start(f32[1536]{0:T(1024)} %param.7) | copy-start | bytes 18436
  2.3 30.5 %all-to-all-start = ((bf16[16,48,128]{2,1,0:T(8,128)(2,1)}), bf16[16,48,128]{2,1,0:T(8,128)(2,1)S(1)}, u32[]{:S(2)}, u32[]{:S(2)}) async-start(bf16[16,48,128]{2,1,0:T(8,128)(2,1)} %shard_map.84), calls=%async_computation | async-start | bytes 393216 | tf_op jit(solution)/shard_map/all_to_all | solution.py:57
  33.4 26.4 %copy-start = (bf16[512,1536]{1,0:T(8,128)(2,1)S(1)}, bf16[512,1536]{1,0:T(8,128)(2,1)}, u32[]{:S(2)}) copy-start(bf16[512,1536]{1,0:T(8,128)(2,1)} %get-tuple-element.32.hidden_ref) | copy-start | bytes 4718596
  68.2 15.4 %collective-permute-start = (f32[264,512]{1,0:T(8,128)S(1)}, f32[264,512]{1,0:T(8,128)S(1)}, u32[]{:S(2)}, u32[]{:S(2)}) collective-permute-start(f32[264,512]{1,0:T(8,128)S(1)} %fusion.12.own_ref), channel_id=1, source_target_pairs={{0,256},{256,0},{1,257},{257,1},{2,258},{258,2},{3,259},{259,3},{4... | collective-permute-start | bytes 1622024 | tf_op jit(solution)/shard_map/ppermute | solution.py:349
  89.5 25.0 %copy-start.1 = (bf16[512,384]{1,0:T(8,128)(2,1)}, bf16[512,384]{1,0:T(8,128)(2,1)S(1)}, u32[]{:S(2)}) copy-start(bf16[512,384]{1,0:T(8,128)(2,1)S(1)} %get-tuple-element.44) | copy-start | bytes 1179652
  114.5 11.6 %copy-start.2 = (bf16[512,384]{1,0:T(8,128)(2,1)S(1)}, bf16[512,384]{1,0:T(8,128)(2,1)}, u32[]{:S(2)}) copy-start(bf16[512,384]{1,0:T(8,128)(2,1)} %copy-done.1) | copy-start | bytes 1179652
  115.9 24.4 %all-to-all-start.4 = ((bf16[16,48,128]{2,1,0:T(8,128)(2,1)}), bf16[16,48,128]{2,1,0:T(8,128)(2,1)S(1)}, u32[]{:S(2)}, u32[]{:S(2)}) async-start(bf16[16,48,128]{2,1,0:T(8,128)(2,1)} %bitcast.10), calls=%async_computation.4 | async-start | bytes 393216 | tf_op jit(solution)/shard_map/all_to_all | solution.py:57
  126.4 13.9 %copy-start.3 = (bf16[12,384]{1,0:T(8,128)(2,1)S(1)}, bf16[12,384]{1,0:T(8,128)(2,1)}, u32[]{:S(2)}) copy-start(bf16[12,384]{1,0:T(8,128)(2,1)} %qkv_ref.1) | copy-start | bytes 27652

commit v8 on v6

--- a/solution.py
+++ b/solution.py
@@ -109,11 +109,7 @@
             o_ref[k, :, b * LANES : (b + 1) * LANES] = part
 
 
-def prepare_kernel(
-    rows, nz, hidden_ref, gout_hbm, gain_ref, hp_ref, gp_ref, gains_ref, gout_ref, sem
-):
-    fetch = pltpu.make_async_copy(gout_hbm, gout_ref, sem)
-    fetch.start()
+def prepare_kernel(rows, nz, hidden_ref, gain_ref, hp_ref, gains_ref):
     span = 2 * nz * rows
     pick = picks((span, span), near_order(rows, nz))
     for y in range(hidden_ref.shape[1] // span):
@@ -124,31 +120,40 @@
         row = lax.broadcasted_iota(jnp.int32, (16, span), 0)
         both = jnp.where(row == 0, high, jnp.where(row == 1, gain - high, 0.0))
         gains_ref[:, at] = dot(both.astype(jnp.bfloat16), pick).astype(jnp.bfloat16)
-    fetch.wait()
-    for y in range(hidden_ref.shape[1] // span):
-        at = slice(y * span, (y + 1) * span)
-        gp_ref[:, at] = dot(gout_ref[:, at], pick).astype(jnp.bfloat16)
-
-
-def project_kernel(near_ref, hidden_ref, gout_ref, gain_ref, partial_ref, w_ref):
+
+
+def project_kernel(
+    rows, nz, near_ref, hidden_ref, gout_hbm, gain_ref, partial_ref, w_ref, gout_ref, sem
+):
+    fetch = pltpu.make_async_copy(gout_hbm, gout_ref, sem)
+    fetch.start()
     nx, ny, part, width = near_ref.shape
+    span = nx * part
     cut = width - LANES
     half = hidden_ref.shape[0] // 2
+    pick = picks((span, span), near_order(rows, nz))
     for y in range(ny):
+        listed = mirrored(y, ny)
         for x in range(nx):
             at = (y * nx + x) * part
-            w_ref[at : at + part, :] = near_ref[x, mirrored(y, ny)]
+            w_ref[at : at + part, :cut] = near_ref[x, listed, :, :cut]
+        block = jnp.concatenate([near_ref[x, listed, :, cut:] for x in range(nx)], axis=0)
+        w_ref[y * span : (y + 1) * span, cut:] = dot(pick, block).astype(jnp.bfloat16)
     sums = dot(gain_ref[...], w_ref[:, :cut])
     proj = dot(hidden_ref[...], w_ref[:, :cut])
-    att = dot(gout_ref[...], w_ref[:, cut:])
     for h in range(2):
         partial_ref[h, half:, :cut] = sums[:8]
         partial_ref[h, half:, cut:] = jnp.zeros((8, LANES), jnp.float32)
         partial_ref[h, :half, :cut] = proj[h * half : (h + 1) * half]
+    fetch.wait()
+    att = dot(gout_ref[...], w_ref[:, cut:])
+    for h in range(2):
         partial_ref[h, :half, cut:] = att[h * half : (h + 1) * half]
 
 
-def natural_kernel(rows, nz, near_ref, o_ref):
+def natural_kernel(rows, nz, near_ref, gout_hbm, o_ref, gp_ref, gout_ref, sem):
+    fetch = pltpu.make_async_copy(gout_hbm, gout_ref, sem)
+    fetch.start()
     nx, ny, part, _ = near_ref.shape
     span = nx * part
     cut = o_ref.shape[1]
@@ -156,6 +161,10 @@
     for y in range(ny):
         block = jnp.concatenate([near_ref[x, mirrored(y, ny), :, :cut] for x in range(nx)], axis=0)
         o_ref[y * span : (y + 1) * span, :] = dot(pick, block).astype(jnp.bfloat16)
+    fetch.wait()
+    for y in range(ny):
+        at = slice(y * span, (y + 1) * span)
+        gp_ref[:, at] = dot(gout_ref[:, at], pick).astype(jnp.bfloat16)
 
 
 def add_kernel(own_ref, other_ref, both_ref, sums_ref):
@@ -298,26 +307,18 @@
     inv_std = lax.rsqrt(stats[1] / model_width - row_mean * row_mean + EPS)
     normed = (tok_float - row_mean[:, None]) * inv_std[:, None]
     hidden = (normed * gain[None, :]).astype(jnp.bfloat16)
-    hidden_p, gout_p, gains_p = call(
+    hidden_p, gains_p = call(
         functools.partial(prepare_kernel, rows, nz),
-        (
-            array((tok_rows, local_width)),
-            array((tok_rows, local_width)),
-            array((16, local_width)),
-        ),
-        1_300_000_000,
-        6_000_000,
-        in_specs=[in_vmem, in_hbm, in_vmem],
-        scratch_shapes=[
-            pltpu.VMEM((tok_rows, local_width), jnp.bfloat16),
-            pltpu.SemaphoreType.DMA,
-        ],
-    )(hidden, keep(grad_out), gain.reshape(1, local_width))
+        (array((tok_rows, local_width)), array((16, local_width))),
+        700_000_000,
+        3_000_000,
+    )(hidden, gain.reshape(1, local_width))
+    fetched = [pltpu.VMEM((tok_rows, local_width), jnp.bfloat16), pltpu.SemaphoreType.DMA]
     own = lax.axis_index(FSDP) * rows
     own_gain = lax.dynamic_slice(gain, (own,), (rows,)).reshape(1, rows)
 
-    along_z, hidden_p, gout_p, gains_p, own_gain = lax.optimization_barrier(
-        (along_z, hidden_p, gout_p, gains_p, own_gain)
+    along_z, hidden_p, gains_p, own_gain = lax.optimization_barrier(
+        (along_z, hidden_p, gains_p, own_gain)
     )
     spread = call(
         functools.partial(spread_kernel, rows),
@@ -330,24 +331,27 @@
     near = near.reshape(nx, ny, nz * rows, width)
     half_rows = tok_rows // 2
     partial = call(
-        project_kernel,
+        functools.partial(project_kernel, rows, nz),
         array((2, half_rows + 8, width), jnp.float32),
         900_000_000,
         6_000_000,
-        scratch_shapes=[pltpu.VMEM((local_width, width), jnp.bfloat16)],
-    )(near, hidden_p, gout_p, gains_p)
+        in_specs=[in_vmem, in_vmem, in_hbm, in_vmem],
+        scratch_shapes=[pltpu.VMEM((local_width, width), jnp.bfloat16)] + fetched,
+    )(near, hidden_p, keep(grad_out), gains_p)
 
     near, partial = lax.optimization_barrier((near, partial))
     half = lax.all_to_all(partial, "core", 0, 0)
     half = half[0] + half[1]
     near, half = lax.optimization_barrier((near, half))
     other = lax.ppermute(half, "xlo", [(0, 1), (1, 0)])
-    weights = call(
+    weights, gout_p = call(
         functools.partial(natural_kernel, rows, nz),
-        array((local_width, cut)),
-        460_000_000,
-        3_000_000,
-    )(near)
+        (array((local_width, cut)), array((tok_rows, local_width))),
+        1_060_000_000,
+        6_000_000,
+        in_specs=[in_vmem, in_hbm],
+        scratch_shapes=fetched,
+    )(near, keep(grad_out))
     half, weight_sums = call(
         add_kernel,
         (array((half_rows, width)), array((1, cut), jnp.float32)),
@@ -356,7 +360,7 @@
     )(half, other)
     both = lax.all_gather(half, "core", axis=0, tiled=True)
 
-    both, weights = lax.optimization_barrier((both, weights))
+    both, weights, gout_p = lax.optimization_barrier((both, weights, gout_p))
     sent, grad_proj = call(
         attend_kernel,
         (array((nx, ny, nz * rows, width)), array((tok_rows, cut))),

time: 141 us -> 140 us (level)
  the two profiles are of different devices: /device:TPU:1 before, /device:TPU:32 now
where the time goes in v8:
time: 140 us; the launch traced here: 139 us
  blocking collectives  62.8 us (45%)
  starting transfers between devices  28.7 us (20%)
  waiting for transfers between devices  24.3 us (17%)
  Pallas kernels  14.2 us (10%)
  matrix products  4.54 us (3%)
  other arithmetic  2.95 us (2%)
    all_to_all x2, blocking collectives, near_all_to_all(): return lax.all_to_all(x, NEAR, 0, 0, axis_index_groups=groups)  49.7 us
    all_to_all x2, starting transfers between devices, far_all_to_all(): return lax.all_to_all(x, FAR, 0, 0, axis_index_groups=groups)  26.1 us
    all_to_all x2, waiting for transfers between devices, far_all_to_all(): return lax.all_to_all(x, FAR, 0, 0, axis_index_groups=groups)  14.2 us
    ppermute x1, waiting for transfers between devices, on_device(): other = lax.ppermute(half, 'xlo', [(0, 1), (1, 0)])  10.1 us
    psum x1, blocking collectives, on_device(): lax.psum(jnp.stack([jnp.sum(tok_float, axis=1), jnp.sum(tok_float * tok_f...  6.33 us
    all_to_all x1, blocking collectives, on_device(): half = lax.all_to_all(partial, 'core', 0, 0)  4.58 us
    dot_general x1, matrix products, on_device(): lax.dot_general(grad_proj, weights, nt_dims, preferred_element_type=jnp.f...  4.54 us
    pallas_call x1, Pallas kernels, on_device(): call(functools.partial(project_kernel, rows, nz), array((2, half_rows + 8...  2.89 us
  transfers between devices with their start and end apart: 3, of which 3 were waited for; matrix products, arithmetic and copies ran while one was open for 5% of the time, Pallas kernels for 3%

profile of v8, /device:TPU:32, one launch (start us, length us, event | category | flops | bytes accessed | tf_op | source)
XLA Modules:
  0.0 139.4 jit_solution(5050857153714866706)
XLA Ops:
  0.7 1.7 %shard_map.84 = bf16[16,48,128]{2,1,0:T(8,128)(2,1)} custom-call(bf16[12,384]{1,0:T(8,128)(2,1)} %qkv_ref.1, bf16[12,128]{1,0:T(8,128)(2,1)} %bitcast.27), custom_call_target="tpu_custom_call" | custom-call | flops 1000000 | bytes 200000 | tf_op jit(solution)/shard_map/pallas_call | solution.py:287
  2.3 15.2 %all-to-all-start = ((bf16[16,48,128]{2,1,0:T(8,128)(2,1)}), bf16[16,48,128]{2,1,0:T(8,128)(2,1)S(1)}, u32[]{:S(2)}, u32[]{:S(2)}) async-start(bf16[16,48,128]{2,1,0:T(8,128)(2,1)} %shard_map.84), calls=%async_computation | async-start | bytes 393216 | tf_op jit(solution)/shard_map/all_to_all | solution.py:57
  17.6 2.0 %convert_reduce_fusion = (f32[512]{0:T(512)S(1)}, f32[512]{0:T(512)S(1)}) fusion(bf16[512,1536]{1,0:T(8,128)(2,1)} %param.5), kind=kLoop, calls=%fused_computation.2 | loop fusion | flops 3144704 | bytes 1576960 | tf_op jit(solution)/shard_map/reduce_sum | solution.py:303
  19.6 6.3 %psum.7 = f32[2,512]{1,0:T(2,128)S(1)} all-reduce(f32[2,512]{1,0:T(2,128)S(1)} %pad_maximum_fusion), channel_id=1, replica_groups=mesh['xlo'=2,'core'=2,'y'=4,'z'=16,'xhi'=2] {'xlo','core'}, use_global_device_ids=true, to_apply=%region_2.0 | all-reduce | flops 1024 | bytes 8192 | tf_op jit(solution)/shard_map/psum | solution.py:302
  26.0 0.5 fusion.8.hidden_ref
  26.5 1.4 shard_map.85
  27.9 4.5 %all-to-all-done = bf16[16,48,128]{2,1,0:T(8,128)(2,1)S(1)} async-done(((bf16[16,48,128]{2,1,0:T(8,128)(2,1)}), bf16[16,48,128]{2,1,0:T(8,128)(2,1)S(1)}, u32[]{:S(2)}, u32[]{:S(2)}) %all-to-all-start) | async-done | bytes 196640 | tf_op jit(solution)/shard_map/all_to_all | solution.py:57
  32.5 0.6 shard_map.86
  33.1 24.1 %all_to_all.25 = bf16[8,192,512]{2,1,0:T(8,128)(2,1)S(1)} all-to-all(bf16[8,192,512]{2,1,0:T(8,128)(2,1)S(1)} %shard_map.86), channel_id=1, replica_groups={{0,32,64,96,1,33,65,97},{224,192,160,128,225,193,161,129},{2,34,66,98,3..., dimensions={0} | all-to-all | bytes 3145728 | tf_op jit(solution)/shard_map/all_to_all | solution.py:51
  57.2 2.9 %shard_map.87 = f32[2,264,512]{2,1,0:T(8,128)S(1)} custom-call(bf16[2,4,192,512]{3,2,1,0:T(8,128)(2,1)S(1)} %bitcast.17, bf16[512,1536]{1,0:T(8,128)(2,1)S(1)} %get-tuple-element.32.hidden_ref, bf16[512,1536]{1,0:T(8,128)(2,1)} %gout_hbm.3, bf16[16,1536]{1,0:T(8,128)(2,1)S(1)} %get-tuple-element.33.gain_ref), custom_call_target="tpu_custom_call" | custom-call | flops 900000000 | bytes 6000000 | tf_op jit(solution)/shard_map/pallas_call | solution.py:333
  60.1 4.6 %all_to_all.26 = f32[2,264,512]{2,1,0:T(8,128)S(1)} all-to-all(f32[2,264,512]{2,1,0:T(8,128)S(1)} %shard_map.87), channel_id=1, replica_groups=mesh['xlo'=2,'core'=2,'y'=4,'z'=16,'xhi'=2] {'core'}, dimensions={0} | all-to-all | bytes 2162688 | tf_op jit(solution)/shard_map/all_to_all | solution.py:343
  64.7 2.5 %collective-permute-start = (f32[264,512]{1,0:T(8,128)S(1)}, f32[264,512]{1,0:T(8,128)S(1)}, u32[]{:S(2)}, u32[]{:S(2)}) collective-permute-start(f32[264,512]{1,0:T(8,128)S(1)} %fusion.12.own_ref), channel_id=1, source_target_pairs={{0,256},{256,0},{1,257},{257,1},{2,258},{258,2},{3,259},{259,3},{4... | collective-permute-start | bytes 1622024 | tf_op jit(solution)/shard_map/ppermute | solution.py:346
  67.3 2.5 %shard_map.89 = (bf16[1536,384]{1,0:T(8,128)(2,1)S(1)}, bf16[512,1536]{1,0:T(8,128)(2,1)S(1)}) custom-call(bf16[2,4,192,512]{3,2,1,0:T(8,128)(2,1)S(1)} %bitcast.18, bf16[512,1536]{1,0:T(8,128)(2,1)} %gout_hbm.3), custom_call_target="tpu_custom_call" | custom-call | flops 1060000000 | bytes 6000000 | tf_op jit(solution)/shard_map/pallas_call | solution.py:347
  69.9 1.0 copy-done.1
  70.9 10.1 %collective-permute-done.other_ref = f32[264,512]{1,0:T(8,128)S(1)} collective-permute-done((f32[264,512]{1,0:T(8,128)S(1)}, f32[264,512]{1,0:T(8,128)S(1)}, u32[]{:S(2)}, u32[]{:S(2)}) %collective-permute-start) | collective-permute-done | bytes 540704 | tf_op jit(solution)/shard_map/ppermute | solution.py:346
  81.0 2.2 %all_gather.3.both_ref = bf16[512,512]{1,0:T(8,128)(2,1)S(1)} all-gather(bf16[256,512]{1,0:T(8,128)(2,1)S(1)} %get-tuple-element.37), channel_id=1, replica_groups=mesh['xlo'=2,'core'=2,'y'=4,'z'=16,'xhi'=2] {'core'}, dimensions={0}, use_global_device_ids=true | all-gather | bytes 786432 | tf_op jit(solution)/shard_map/all_gather | solution.py:361
  83.2 2.8 %shard_map.90 = (bf16[2,4,192,512]{3,2,1,0:T(8,128)(2,1)S(1)}, bf16[512,384]{1,0:T(8,128)(2,1)S(1)}) custom-call(bf16[512,512]{1,0:T(8,128)(2,1)S(1)} %all_gather.3.both_ref, bf16[512,1536]{1,0:T(8,128)(2,1)S(1)} %get-tuple-element.32.hidden_ref, bf16[512,1536]{1,0:T(8,128)(2,1)S(1)} %get-tuple-element.42.gout_ref), custom_call_target="tpu_custom_call" | custom-call | flops 1300000000 | bytes 6000000 | tf_op jit(solution)/shard_map/pallas_call | solution.py:364
  86.0 25.7 %all_to_all.27.near_ref = bf16[8,192,512]{2,1,0:T(8,128)(2,1)S(1)} all-to-all(bf16[8,192,512]{2,1,0:T(8,128)(2,1)S(1)} %bitcast.19), channel_id=1, replica_groups={{0,32,64,96,1,33,65,97},{224,192,160,128,225,193,161,129},{2,34,66,98,3..., dimensions={0} | all-to-all | bytes 3145728 | tf_op jit(solution)/shard_map/all_to_all | solution.py:51
  111.7 1.4 shard_map.91
  113.1 10.9 %all-to-all-start.4 = ((bf16[16,48,128]{2,1,0:T(8,128)(2,1)}), bf16[16,48,128]{2,1,0:T(8,128)(2,1)S(1)}, u32[]{:S(2)}, u32[]{:S(2)}) async-start(bf16[16,48,128]{2,1,0:T(8,128)(2,1)} %bitcast.10), calls=%async_computation.4 | async-start | bytes 393216 | tf_op jit(solution)/shard_map/all_to_all | solution.py:57
  124.0 0.3 fusion.10
  124.3 4.5 %fusion.9 = bf16[512,1536]{1,0:T(8,128)(2,1)} fusion(bf16[512,1536]{1,0:T(8,128)(2,1)} %param.5, bf16[512,384]{1,0:T(8,128)(2,1)S(1)} %get-tuple-element.46, bf16[1536,384]{1,0:T(8,128)(2,1)S(1)} %copy-done.2, bf16[512,1536]{1,0:T(8,128)(2,1)} %gout_hbm.3, f32[512]{0:T(512)S(1)} %get-tuple-element.60, f32[512]{0:T(512)S(1)} %get-tuple-element.61, ...), kind=kOutput, calls=%fused_computation.13 | convolution fusion | flops 612630528 | bytes 6305792 | tf_op jit(solution)/shard_map/dot_general | solution.py:394
  128.9 9.7 %all-to-all-done.4.x_ref = bf16[16,48,128]{2,1,0:T(8,128)(2,1)S(1)} async-done(((bf16[16,48,128]{2,1,0:T(8,128)(2,1)}), bf16[16,48,128]{2,1,0:T(8,128)(2,1)S(1)}, u32[]{:S(2)}, u32[]{:S(2)}) %all-to-all-start.4) | async-done | bytes 196640 | tf_op jit(solution)/shard_map/all_to_all | solution.py:57
  138.6 0.9 shard_map.92
  (18 shorter events, 0.3 us)
Async XLA Ops:
  0.6 25.3 %copy-start.3 = (bf16[512,1536]{1,0:T(8,128)(2,1)S(1)}, bf16[512,1536]{1,0:T(8,128)(2,1)}, u32[]{:S(2)}) copy-start(bf16[512,1536]{1,0:T(8,128)(2,1)} %param.5) | copy-start | bytes 4718596
  0.6 25.3 %copy-start.4 = (f32[1536]{0:T(1024)S(1)}, f32[1536]{0:T(1024)}, u32[]{:S(2)}) copy-start(f32[1536]{0:T(1024)} %param.7) | copy-start | bytes 18436
  2.3 30.2 %all-to-all-start = ((bf16[16,48,128]{2,1,0:T(8,128)(2,1)}), bf16[16,48,128]{2,1,0:T(8,128)(2,1)S(1)}, u32[]{:S(2)}, u32[]{:S(2)}) async-start(bf16[16,48,128]{2,1,0:T(8,128)(2,1)} %shard_map.84), calls=%async_computation | async-start | bytes 393216 | tf_op jit(solution)/shard_map/all_to_all | solution.py:57
  64.7 16.2 %collective-permute-start = (f32[264,512]{1,0:T(8,128)S(1)}, f32[264,512]{1,0:T(8,128)S(1)}, u32[]{:S(2)}, u32[]{:S(2)}) collective-permute-start(f32[264,512]{1,0:T(8,128)S(1)} %fusion.12.own_ref), channel_id=1, source_target_pairs={{0,256},{256,0},{1,257},{257,1},{2,258},{258,2},{3,259},{259,3},{4... | collective-permute-start | bytes 1622024 | tf_op jit(solution)/shard_map/ppermute | solution.py:346
  69.8 1.0 copy-start.1
  111.7 12.6 %copy-start.2 = (bf16[1536,384]{1,0:T(8,128)(2,1)S(1)}, bf16[1536,384]{1,0:T(8,128)(2,1)}, u32[]{:S(2)}) copy-start(bf16[1536,384]{1,0:T(8,128)(2,1)} %copy-done.1) | copy-start | bytes 3538948
  113.1 25.5 %all-to-all-start.4 = ((bf16[16,48,128]{2,1,0:T(8,128)(2,1)}), bf16[16,48,128]{2,1,0:T(8,128)(2,1)S(1)}, u32[]{:S(2)}, u32[]{:S(2)}) async-start(bf16[16,48,128]{2,1,0:T(8,128)(2,1)} %bitcast.10), calls=%async_computation.4 | async-start | bytes 393216 | tf_op jit(solution)/shard_map/all_to_all | solution.py:57
  124.3 14.2 %copy-start = (bf16[12,384]{1,0:T(8,128)(2,1)S(1)}, bf16[12,384]{1,0:T(8,128)(2,1)}, u32[]{:S(2)}) copy-start(bf16[12,384]{1,0:T(8,128)(2,1)} %qkv_ref.1) | copy-start | bytes 27652
